TPU v7x, 512 devices: a whole 4x8x8 slice. The times are simulated.
512 devices in a mesh: section: 4 (over x), row: 16 (over z, core), dp: 8 (over y).
Axes of the slice: x: 4, y: 8, z: 8, core: 2. Of those that a mesh axis runs over, the one named last changes fastest.
Arguments:
- inputs: bfloat16 [4, 8, 64, 48, 352], P(None, 'dp', 'row'), may hold values from -8 to 8
- depth_kernel: bfloat16 [4, 7, 7, 352], P('section'), may hold values from -0.875 to 0.875
- depth_bias: bfloat16 [4, 352], P('section'), may hold values from -3 to 3
- norm_gain: bfloat16 [4, 352], P('section'), may hold values from 0.099609375 to 1.8984375
- norm_bias: bfloat16 [4, 352], P('section'), may hold values from -3 to 3
- proj_in: bfloat16 [4, 352, 1408], P('section', None, 'dp'), may hold values from -0.3125 to 0.3125
- bias_in: bfloat16 [4, 1408], P('section'), may hold values from -3 to 3
- grn_gamma: bfloat16 [4, 1408], P('section'), may hold values from -3 to 3
- grn_beta: bfloat16 [4, 1408], P('section'), may hold values from -2 to 2
- proj_out: bfloat16 [4, 1408, 352], P('section', 'dp'), may hold values from -0.15625 to 0.15625
- bias_out: bfloat16 [4, 352], P('section'), may hold values from -3 to 3
Outputs:
- saved: bfloat16 [4, 4, 8, 64, 48, 352], P('section', None, 'dp', 'row')
All inputs are finite; a program needn't handle non-finite values.
Results may differ from a plain program's by a relative error of at most 0.015.
Values may be sent and summed in bfloat16 or wider, within the bound.
A program may use at most 64 MiB of HBM per device.

v0:
```python
import functools
import math

import jax
import jax.numpy as jnp
from jax import lax
from jax.experimental import pallas as pl
from jax.experimental.pallas import tpu as pltpu
from jax.sharding import PartitionSpec as P

MESH = pl.DeviceIdType.MESH

EPS_NORM = 1e-06
EPS_GRN = 1e-06


def extended(cells, sides, width):
    for axis, dim in sides:
        count = lax.axis_size(axis)
        ends = count - 1
        head = lax.slice_in_dim(cells, 0, width, axis=dim)
        tail = lax.slice_in_dim(cells, cells.shape[dim] - width, cells.shape[dim], axis=dim)
        cells = jnp.concatenate(
            [
                lax.ppermute(tail, axis, [(i, (i + 1) % count) for i in range(ends)]),
                cells,
                lax.ppermute(head, axis, [((i + 1) % count, i) for i in range(ends)]),
            ],
            axis=dim,
        )
    return cells


def _pointwise_kernel(
    n,
    sections,
    hand_on,
    fresh_index,
    padded_ref,
    fresh_ref,
    held_ref,
    other_ref,
    bias_in_ref,
    gamma_ref,
    beta_ref,
    bias_out_ref,
    taps_ref,
    depth_bias_ref,
    gain_ref,
    shift_ref,
    out_ref,
    *rest,
):
    if hand_on:
        next_ref, wide_ref, normed_ref, act_ref, slots, send_sem, recv_sem = rest[:7]
        hand_send, hand_recv, fresh_sem = rest[7:]
    else:
        wide_ref, normed_ref, act_ref, slots, send_sem, recv_sem = rest
    me = lax.axis_index("row")
    section = lax.axis_index("section")
    barrier = pltpu.get_barrier_semaphore()
    for k in range(1, n):
        pl.semaphore_signal(
            barrier, inc=1, device_id={"row": lax.rem(me + k, n)}, device_id_type=MESH
        )
    waits = n - 1
    if hand_on:
        cells = out_ref.shape[0]
        edge = 3 * cells // 4
        has_above = me > 0
        has_below = me < n - 1
        has_prev = section > 0
        has_next = section < sections - 1
        @pl.when(has_prev)
        def _():
            pl.semaphore_signal(
                barrier, inc=1, device_id={"section": section - 1}, device_id_type=MESH
            )

        waits = waits + has_next.astype(jnp.int32)
    padded_rows, margin_cols, channels = wide_ref.shape
    cols = padded_ref.shape[0] // padded_rows
    out_rows = padded_rows - 6
    zeros = jnp.zeros((8, channels), jnp.float32)
    for r in range(padded_rows):
        wide_ref[r, pl.ds(0, 8), :] = zeros
        wide_ref[r, pl.ds(8, cols), :] = padded_ref[pl.ds(r * cols, cols), :].astype(jnp.float32)
        wide_ref[r, pl.ds(8 + cols, margin_cols - 8 - cols), :] = zeros[: margin_cols - 8 - cols]

    def conv_row(h, carry):
        acc = jnp.broadcast_to(depth_bias_ref[...].astype(jnp.float32), (cols, channels))
        for i in range(7):
            for j in range(7):
                tap = taps_ref[pl.ds(i * 7 + j, 1), :].astype(jnp.float32)
                acc = acc + wide_ref[h + i, pl.ds(j + 5, cols), :] * tap
        mean = jnp.mean(acc, axis=-1, keepdims=True)
        center = acc - mean
        spread = jnp.mean(center * center, axis=-1, keepdims=True)
        normed = (
            center * lax.rsqrt(spread + EPS_NORM) * gain_ref[...].astype(jnp.float32)
            + shift_ref[...].astype(jnp.float32)
        )
        normed_ref[pl.ds(pl.multiple_of(h * cols, 16), cols), :] = normed.astype(normed_ref.dtype)
        return carry

    lax.fori_loop(0, out_rows, conv_row, 0)
    first_core = lax.rem(me, 2) == 0

    def raise_with(proj_in_ref):
        raised = jnp.dot(
            normed_ref[...], proj_in_ref[...], preferred_element_type=jnp.float32
        ) + bias_in_ref[...].astype(jnp.float32)
        act_ref[...] = (0.5 * raised * (1.0 + lax.erf(raised * (1.0 / math.sqrt(2.0))))).astype(
            jnp.bfloat16
        )

    pl.when(first_core)(lambda: raise_with(held_ref))
    pl.when(jnp.logical_not(first_core))(lambda: raise_with(other_ref))
    grouped = act_ref[...].astype(jnp.float32)
    slots[me] = jnp.sum(grouped * grouped, axis=0, keepdims=True)
    pl.semaphore_wait(barrier, waits)
    sends = []
    for k in range(1, n):
        copy = pltpu.make_async_remote_copy(
            src_ref=slots.at[me],
            dst_ref=slots.at[me],
            send_sem=send_sem.at[k],
            recv_sem=recv_sem.at[me],
            device_id={"row": lax.rem(me + k, n)},
            device_id_type=MESH,
        )
        copy.start()
        sends.append(copy)
    if hand_on:
        @pl.when(section == 0)
        def _():
            fresh_copy = pltpu.make_async_copy(fresh_ref.at[fresh_index], next_ref, fresh_sem)
            fresh_copy.start()
            fresh_copy.wait()

        @pl.when(jnp.logical_and(has_prev, jnp.logical_not(has_above)))
        def _():
            next_ref[pl.ds(0, edge), :] = jnp.zeros((edge, next_ref.shape[1]), next_ref.dtype)

        @pl.when(jnp.logical_and(has_prev, jnp.logical_not(has_below)))
        def _():
            next_ref[pl.ds(edge + cells, edge), :] = jnp.zeros(
                (edge, next_ref.shape[1]), next_ref.dtype
            )

    for k in range(1, n):
        src = lax.rem(me + k, n)
        pltpu.make_async_remote_copy(
            src_ref=slots.at[src],
            dst_ref=slots.at[src],
            send_sem=send_sem.at[k],
            recv_sem=recv_sem.at[src],
            device_id={"row": src},
            device_id_type=MESH,
        ).wait_recv()
    for copy in sends:
        copy.wait_send()
    total_sq = slots[0]
    for j in range(1, n):
        total_sq = total_sq + slots[j]
    magnitude = jnp.sqrt(total_sq)
    grn_ratio = magnitude / (jnp.mean(magnitude, axis=-1, keepdims=True) + EPS_GRN)
    grouped = act_ref[...].astype(jnp.float32)
    hidden = (
        gamma_ref[...].astype(jnp.float32) * grouped * grn_ratio
        + beta_ref[...].astype(jnp.float32)
        + grouped
    ).astype(jnp.bfloat16)
    cells = out_ref.shape[0]
    edge = 3 * cells // 4

    def lower_with(proj_out_t_ref):
        update = lax.dot_general(
            hidden,
            proj_out_t_ref[...],
            (((1,), (1,)), ((), ())),
            preferred_element_type=jnp.float32,
        ) + bias_out_ref[...].astype(jnp.float32)
        current = padded_ref[pl.ds(edge, cells), :].astype(jnp.float32)
        out_ref[...] = (current + update).astype(out_ref.dtype)

    pl.when(first_core)(lambda: lower_with(other_ref))
    pl.when(jnp.logical_not(first_core))(lambda: lower_with(held_ref))
    if not hand_on:
        return
    own_rows = pl.ds(edge, cells)
    handed = pltpu.make_async_remote_copy(
        src_ref=out_ref,
        dst_ref=next_ref.at[own_rows],
        send_sem=hand_send.at[1],
        recv_sem=hand_recv.at[1],
        device_id={"section": section + 1},
        device_id_type=MESH,
    )

    @pl.when(has_next)
    def _():
        handed.start()

    halos = (
        (2, pl.ds(edge, edge), pl.ds(edge + cells, edge), -1, has_above),
        (0, pl.ds(cells, edge), pl.ds(0, edge), 1, has_below),
    )

    def halo_copy(slot, src, dst, peer_row):
        return pltpu.make_async_remote_copy(
            src_ref=next_ref.at[src],
            dst_ref=next_ref.at[dst],
            send_sem=hand_send.at[slot],
            recv_sem=hand_recv.at[slot],
            device_id={"row": peer_row},
            device_id_type=MESH,
        )

    @pl.when(has_prev)
    def _():
        handed.wait_recv()
        for slot, src, dst, shift, cond in halos:
            @pl.when(cond)
            def _():
                halo_copy(slot, src, dst, me + shift).start()

        for slot, src, dst, shift, cond in halos:
            @pl.when(halos[slot // 2][4])
            def _():
                halo_copy(slot, src, dst, me).wait_recv()

        for slot, src, dst, shift, cond in halos:
            @pl.when(cond)
            def _():
                halo_copy(slot, src, dst, me + shift).wait_send()

    @pl.when(has_next)
    def _():
        handed.wait_send()


def pointwise(
    padded,
    fresh,
    fresh_index,
    held,
    other,
    bias_in,
    grn_gamma,
    grn_beta,
    bias_out,
    depth_kernel,
    depth_bias,
    norm_gain,
    norm_bias,
    cols,
    hand_on,
):
    n = lax.axis_size("row")
    sections = lax.axis_size("section")
    channels = padded.shape[1]
    padded_rows = padded.shape[0] // cols
    cells = (padded_rows - 6) * cols
    hidden_units = held.shape[1]
    vmem = pl.BlockSpec(memory_space=pltpu.VMEM)
    out_shape = [jax.ShapeDtypeStruct((cells, channels), padded.dtype)]
    scratch = [
        pltpu.VMEM((padded_rows, -(-(cols + 11) // 8) * 8, channels), jnp.float32),
        pltpu.VMEM((cells, channels), jnp.bfloat16),
        pltpu.VMEM((cells, hidden_units), jnp.bfloat16),
        pltpu.VMEM((n, 1, hidden_units), jnp.float32),
        pltpu.SemaphoreType.DMA((n,)),
        pltpu.SemaphoreType.DMA((n,)),
    ]
    if hand_on:
        out_shape.append(jax.ShapeDtypeStruct(fresh.shape[1:], fresh.dtype))
        scratch += [
            pltpu.SemaphoreType.DMA((3,)),
            pltpu.SemaphoreType.DMA((3,)),
            pltpu.SemaphoreType.DMA(()),
        ]
    return pl.pallas_call(
        functools.partial(_pointwise_kernel, n, sections, hand_on, fresh_index),
        out_shape=out_shape,
        in_specs=[vmem, pl.BlockSpec(memory_space=pl.ANY)] + [vmem] * 10,
        out_specs=[vmem] * len(out_shape),
        scratch_shapes=scratch,
        compiler_params=pltpu.CompilerParams(
            collective_id=1 + fresh_index if hand_on else 0, has_side_effects=True
        ),
        cost_estimate=pl.CostEstimate(
            flops=4 * cells * channels * hidden_units,
            transcendentals=cells * hidden_units,
            bytes_accessed=4 * channels * hidden_units + 8 * cells * channels,
        ),
    )(
        padded,
        fresh,
        held,
        other,
        bias_in.reshape(1, -1),
        grn_gamma.reshape(1, -1),
        grn_beta.reshape(1, -1),
        bias_out.reshape(1, -1),
        depth_kernel.reshape(-1, channels),
        depth_bias.reshape(1, -1),
        norm_gain.reshape(1, -1),
        norm_bias.reshape(1, -1),
    )


def passed_along(x, axis, by):
    count = lax.axis_size(axis)
    pairs = [(i, i + by) for i in range(count) if 0 <= i + by < count]
    return lax.ppermute(x, axis, pairs)


def depthwise(padded, kernel, bias_term):
    channels = padded.shape[-1]
    conv_out = lax.conv_general_dilated(
        padded.astype(jnp.float32),
        kernel.astype(jnp.float32)[:, :, None, :],
        (1, 1),
        "VALID",
        dimension_numbers=("NHWC", "HWIO", "NHWC"),
        feature_group_count=channels,
        precision=lax.Precision.HIGHEST,
    )
    return conv_out + bias_term.astype(jnp.float32)


def conv_block(padded, fresh, fresh_index, params, hand_on):
    (
        depth_kernel,
        depth_bias,
        norm_gain,
        norm_bias,
        proj_in,
        bias_in,
        grn_gamma,
        grn_beta,
        proj_out,
        bias_out,
    ) = params
    num_items, padded_rows, num_cols, channels = padded.shape
    results = pointwise(
        padded.reshape(-1, channels),
        fresh.reshape(fresh.shape[0], -1, channels),
        fresh_index,
        proj_in,
        proj_out,
        bias_in,
        grn_gamma,
        grn_beta,
        bias_out,
        depth_kernel,
        depth_bias,
        norm_gain,
        norm_bias,
        num_cols,
        hand_on,
    )
    produced = results[0].reshape(num_items, padded_rows - 6, num_cols, channels)
    arriving = results[1].reshape(padded.shape) if hand_on else None
    return produced, arriving


def gathered_weights(proj_in, proj_out):
    rows = lax.axis_size("row")
    first_core = lax.rem(lax.axis_index("row"), 2) == 0
    mine = jnp.where(first_core, proj_in, proj_out.T)
    held = lax.all_gather(mine, "dp", axis=1, tiled=True)
    other = lax.ppermute(held, "row", [(r, r ^ 1) for r in range(rows)])
    return held, other


def on_device(
    inputs,
    depth_kernel,
    depth_bias,
    norm_gain,
    norm_bias,
    proj_in,
    bias_in,
    grn_gamma,
    grn_beta,
    proj_out,
    bias_out,
):
    fresh = extended(inputs[:, 0], (("row", 1),), 3)
    proj_in, proj_out = gathered_weights(proj_in[0], proj_out[0])
    sections = lax.axis_size("section")
    section_index = lax.axis_index("section")
    num_micro = inputs.shape[0]
    own_params = (
        depth_kernel[0],
        depth_bias[0],
        norm_gain[0],
        norm_bias[0],
        proj_in,
        bias_in[0],
        grn_gamma[0],
        grn_beta[0],
        proj_out,
        bias_out[0],
    )
    num_ticks = num_micro + sections - 1
    current = fresh[:1]
    outputs = []
    for tick_index in range(num_ticks):
        hand_on = tick_index + 1 < num_ticks
        produced, current = conv_block(
            current, fresh, min(tick_index + 1, num_micro - 1), own_params, hand_on
        )
        outputs.append(produced)
    stacked = jnp.stack(outputs)
    saved = lax.dynamic_slice_in_dim(stacked, section_index, num_micro, axis=0)
    return saved[None]


def solution(mesh):
    return jax.shard_map(
        on_device,
        mesh=mesh,
        in_specs=(
            P(None, "dp", "row", None, None),
            P("section", None, None, None),
            P("section", None),
            P("section", None),
            P("section", None),
            P("section", None, "dp"),
            P("section", None),
            P("section", None),
            P("section", None),
            P("section", "dp", None),
            P("section", None),
        ),
        out_specs=P("section", None, "dp", "row", None, None),
        check_vma=False,
    )
```

profile of v0, /device:TPU:7, one launch (start us, length us, event | category | flops | bytes accessed | tf_op | source)
XLA Modules:
  0.0 199.2 jit_solution(6582515434222915073)
XLA Ops:
  0.0 1.0 bitcast_select_fusion
  1.0 23.6 %all_gather.3 = bf16[352,1408]{0,1:T(8,128)(2,1)S(1)} all-gather(bf16[352,176]{0,1:T(8,128)(2,1)S(1)} %bitcast_select_fusion), channel_id=1, replica_groups=mesh['section'=4,'row'=16,'dp'=8] {'dp'}, dimensions={1}, use_global_device_ids=true | all-gather | bytes 1115136 | tf_op jit(solution)/shard_map/all_gather | solution.py:373
  24.6 1.2 copy.15.held_ref
  25.8 7.5 %collective-permute-start.2 = (bf16[352,1408]{1,0:T(8,128)(2,1)S(1)}, bf16[352,1408]{1,0:T(8,128)(2,1)S(1)}, u32[]{:S(2)}, u32[]{:S(2)}) collective-permute-start(bf16[352,1408]{1,0:T(8,128)(2,1)S(1)} %copy.15.held_ref), channel_id=1, source_target_pairs={{0,8},{8,0},{16,24},{24,16},{32,40},{40,32},{48,56},{56,48},{64,72... | collective-permute-start | bytes 2973704 | tf_op jit(solution)/shard_map/ppermute | solution.py:374
  33.3 1.2 fusion
  34.5 3.9 %collective-permute-start = (bf16[4,3,48,352]{3,2,1,0:T(8,128)(2,1)S(1)}, bf16[4,3,48,352]{3,2,1,0:T(8,128)(2,1)S(1)}, u32[]{:S(2)}, u32[]{:S(2)}) collective-permute-start(bf16[4,3,48,352]{3,2,1,0:T(8,128)(2,1)S(1)} %get-tuple-element.29), channel_id=1, source_target_pairs={{0,8},{8,16},{16,24},{24,32},{32,40},{40,48},{48,56},{56,64},{64,7... | collective-permute-start | bytes 1216520 | tf_op jit(solution)/shard_map/ppermute | solution.py:25
  38.4 1.9 collective-permute-start.1
  40.4 0.0 copy-done.4
  40.4 0.6 reshape_squeeze.2.taps_ref
  41.0 2.6 %collective-permute-done = bf16[4,3,48,352]{3,2,1,0:T(8,128)(2,1)S(1)} collective-permute-done((bf16[4,3,48,352]{3,2,1,0:T(8,128)(2,1)S(1)}, bf16[4,3,48,352]{3,2,1,0:T(8,128)(2,1)S(1)}, u32[]{:S(2)}, u32[]{:S(2)}) %collective-permute-start) | collective-permute-done | bytes 405536 | tf_op jit(solution)/shard_map/ppermute | solution.py:25
  43.7 0.8 copy-done.3
  44.4 3.7 %collective-permute-done.1 = bf16[4,3,48,352]{3,2,1,0:T(8,128)(2,1)} collective-permute-done((bf16[4,3,48,352]{3,2,1,0:T(8,128)(2,1)S(1)}, bf16[4,3,48,352]{3,2,1,0:T(8,128)(2,1)}, u32[]{:S(2)}, u32[]{:S(2)}) %collective-permute-start.1) | collective-permute-done | bytes 405536 | tf_op jit(solution)/shard_map/ppermute | solution.py:27
  48.2 1.6 pad_maximum_fusion
  49.8 0.8 slice.14
  50.7 0.0 collective-permute-done.2.other_ref
  50.7 0.4 copy-done
  51.1 0.6 copy-done.2
  51.6 27.2 %shard_map.109 = (bf16[192,352]{1,0:T(8,128)(2,1)}, bf16[480,352]{1,0:T(8,128)(2,1)}) custom-call(bf16[480,352]{1,0:T(8,128)(2,1)} %bitcast.27, bf16[4,480,352]{2,1,0:T(8,128)(2,1)} %bitcast.18, bf16[352,1408]{1,0:T(8,128)(2,1)} %copy-done.1, bf16[352,1408]{1,0:T(8,128)(2,1)} %copy-done.2, bf16[1,1408]{1,0:T(2,128)(2,1)} %bias_in_ref.13, ...), custom_call_target="tpu_custom_call" | custom-call | flops 380633088 | bytes 2523136 | tf_op jit(solution)/shard_map/pallas_call | solution.py:283
  78.9 0.9 constant_dynamic-update-slice_fusion.6
  79.8 21.4 %shard_map.110 = (bf16[192,352]{1,0:T(8,128)(2,1)}, bf16[480,352]{1,0:T(8,128)(2,1)}) custom-call(bf16[480,352]{1,0:T(8,128)(2,1)} %get-tuple-element.18.padded_ref, bf16[4,480,352]{2,1,0:T(8,128)(2,1)} %bitcast.19, bf16[352,1408]{1,0:T(8,128)(2,1)} %copy-done.1, bf16[352,1408]{1,0:T(8,128)(2,1)} %copy-done.2, bf16[1,1408]{1,0:T(2,128)(2,1)} %bias_in_ref.13, ...), custom_call_target="tpu_custom_call" | custom-call | flops 380633088 | bytes 2523136 | tf_op jit(solution)/shard_map/pallas_call | solution.py:283
  101.2 0.9 constant_dynamic-update-slice_fusion.5
  102.2 21.8 %shard_map.111 = (bf16[192,352]{1,0:T(8,128)(2,1)}, bf16[480,352]{1,0:T(8,128)(2,1)}) custom-call(bf16[480,352]{1,0:T(8,128)(2,1)} %get-tuple-element.20.padded_ref, bf16[4,480,352]{2,1,0:T(8,128)(2,1)} %bitcast.20, bf16[352,1408]{1,0:T(8,128)(2,1)} %copy-done.1, bf16[352,1408]{1,0:T(8,128)(2,1)} %copy-done.2, bf16[1,1408]{1,0:T(2,128)(2,1)} %bias_in_ref.13, ...), custom_call_target="tpu_custom_call" | custom-call | flops 380633088 | bytes 2523136 | tf_op jit(solution)/shard_map/pallas_call | solution.py:283
  124.0 0.9 constant_dynamic-update-slice_fusion.4
  124.9 18.8 %shard_map.112 = (bf16[192,352]{1,0:T(8,128)(2,1)}, bf16[480,352]{1,0:T(8,128)(2,1)}) custom-call(bf16[480,352]{1,0:T(8,128)(2,1)} %get-tuple-element.22.padded_ref, bf16[4,480,352]{2,1,0:T(8,128)(2,1)} %bitcast.21, bf16[352,1408]{1,0:T(8,128)(2,1)} %copy-done.1, bf16[352,1408]{1,0:T(8,128)(2,1)} %copy-done.2, bf16[1,1408]{1,0:T(2,128)(2,1)} %bias_in_ref.13, ...), custom_call_target="tpu_custom_call" | custom-call | flops 380633088 | bytes 2523136 | tf_op jit(solution)/shard_map/pallas_call | solution.py:283
  143.7 0.9 constant_dynamic-update-slice_fusion.3
  144.6 18.7 %shard_map.113 = (bf16[192,352]{1,0:T(8,128)(2,1)}, bf16[480,352]{1,0:T(8,128)(2,1)}) custom-call(bf16[480,352]{1,0:T(8,128)(2,1)} %get-tuple-element.24.padded_ref, bf16[4,480,352]{2,1,0:T(8,128)(2,1)} %bitcast.22, bf16[352,1408]{1,0:T(8,128)(2,1)} %copy-done.1, bf16[352,1408]{1,0:T(8,128)(2,1)} %copy-done.2, bf16[1,1408]{1,0:T(2,128)(2,1)} %bias_in_ref.13, ...), custom_call_target="tpu_custom_call" | custom-call | flops 380633088 | bytes 2523136 | tf_op jit(solution)/shard_map/pallas_call | solution.py:283
  163.4 0.9 constant_dynamic-update-slice_fusion.2
  164.3 18.8 %shard_map.114 = (bf16[192,352]{1,0:T(8,128)(2,1)}, bf16[480,352]{1,0:T(8,128)(2,1)}) custom-call(bf16[480,352]{1,0:T(8,128)(2,1)} %get-tuple-element.26.padded_ref, bf16[4,480,352]{2,1,0:T(8,128)(2,1)} %bitcast.23, bf16[352,1408]{1,0:T(8,128)(2,1)} %copy-done.1, bf16[352,1408]{1,0:T(8,128)(2,1)} %copy-done.2, bf16[1,1408]{1,0:T(2,128)(2,1)} %bias_in_ref.13, ...), custom_call_target="tpu_custom_call" | custom-call | flops 380633088 | bytes 2523136 | tf_op jit(solution)/shard_map/pallas_call | solution.py:283
  183.2 0.9 constant_dynamic-update-slice_fusion.1
  184.1 13.2 %shard_map.115 = bf16[192,352]{1,0:T(8,128)(2,1)} custom-call(bf16[480,352]{1,0:T(8,128)(2,1)} %get-tuple-element.28.padded_ref, bf16[4,480,352]{2,1,0:T(8,128)(2,1)} %bitcast.24, bf16[352,1408]{1,0:T(8,128)(2,1)} %copy-done.1, bf16[352,1408]{1,0:T(8,128)(2,1)} %copy-done.2, bf16[1,1408]{1,0:T(2,128)(2,1)} %bias_in_ref.13, bf16[1,1408]{1,0:T(2,128)(2,1)} %gamma_ref.13, ...), custom_call_target="tpu_custom_call" | custom-call | flops 380633088 | bytes 2523136 | tf_op jit(solution)/shard_map/pallas_call | solution.py:283
  197.4 0.9 constant_dynamic-update-slice_fusion
  198.3 0.9 dynamic-slice_bitcast_fusion
  (6 shorter events, 0.0 us)
Async XLA Ops:
  24.6 15.8 %copy-start.4 = (bf16[1,7,7,352]{3,2,1,0:T(8,128)(2,1)S(1)}, bf16[1,7,7,352]{3,2,1,0:T(8,128)(2,1)}, u32[]{:S(2)}) copy-start(bf16[1,7,7,352]{3,2,1,0:T(8,128)(2,1)} %param.12) | copy-start | bytes 103492
  25.8 24.0 %copy-start.1 = (bf16[352,1408]{1,0:T(8,128)(2,1)}, bf16[352,1408]{1,0:T(8,128)(2,1)S(1)}, u32[]{:S(2)}) copy-start(bf16[352,1408]{1,0:T(8,128)(2,1)S(1)} %copy.15.held_ref) | copy-start | bytes 2973700
  25.8 24.8 %collective-permute-start.2 = (bf16[352,1408]{1,0:T(8,128)(2,1)S(1)}, bf16[352,1408]{1,0:T(8,128)(2,1)S(1)}, u32[]{:S(2)}, u32[]{:S(2)}) collective-permute-start(bf16[352,1408]{1,0:T(8,128)(2,1)S(1)} %copy.15.held_ref), channel_id=1, source_target_pairs={{0,8},{8,0},{16,24},{24,16},{32,40},{40,32},{48,56},{56,48},{64,72... | collective-permute-start | bytes 2973704 | tf_op jit(solution)/shard_map/ppermute | solution.py:374
  34.5 9.1 %collective-permute-start = (bf16[4,3,48,352]{3,2,1,0:T(8,128)(2,1)S(1)}, bf16[4,3,48,352]{3,2,1,0:T(8,128)(2,1)S(1)}, u32[]{:S(2)}, u32[]{:S(2)}) collective-permute-start(bf16[4,3,48,352]{3,2,1,0:T(8,128)(2,1)S(1)} %get-tuple-element.29), channel_id=1, source_target_pairs={{0,8},{8,16},{16,24},{24,32},{32,40},{40,48},{48,56},{56,64},{64,7... | collective-permute-start | bytes 1216520 | tf_op jit(solution)/shard_map/ppermute | solution.py:25
  38.4 9.7 %collective-permute-start.1 = (bf16[4,3,48,352]{3,2,1,0:T(8,128)(2,1)S(1)}, bf16[4,3,48,352]{3,2,1,0:T(8,128)(2,1)}, u32[]{:S(2)}, u32[]{:S(2)}) collective-permute-start(bf16[4,3,48,352]{3,2,1,0:T(8,128)(2,1)S(1)} %get-tuple-element.30), channel_id=1, source_target_pairs={{8,0},{16,8},{24,16},{32,24},{40,32},{48,40},{56,48},{64,56},{72,6... | collective-permute-start | bytes 1216520 | tf_op jit(solution)/shard_map/ppermute | solution.py:27
  43.7 0.8 copy-start.3
  49.8 1.3 copy-start
  50.7 1.0 copy-start.2
where the time goes:
time: 200 us; the launch traced here: 199 us
  Pallas kernels  140 us (70%)
  blocking collectives  23.6 us (12%)
  starting transfers between devices  13.3 us (7%)
  local copies, waits for them, and re-layouts  13.1 us (7%)
  waiting for transfers between devices  6.39 us (3%)
  other arithmetic  2.6 us (1%)
    pallas_call x7, Pallas kernels, pointwise(): pl.pallas_call(functools.partial(_pointwise_kernel, n, sections, hand_on,...  140 us
    all_gather x1, blocking collectives, gathered_weights(): held = lax.all_gather(mine, 'dp', axis=1, tiled=True)  23.6 us
    ppermute x1, starting transfers between devices, gathered_weights(): other = lax.ppermute(held, 'row', [(r, r ^ 1) for r in range(rows)])  7.45 us
    unnamed x16, local copies, waits for them, and re-layouts  7.35 us
  transfers between devices with their start and end apart: 3, of which 2 were waited for; matrix products, arithmetic and copies ran while one was open for 2% of the time, Pallas kernels for 0%

commit v1 on v0

--- a/solution.py
+++ b/solution.py
@@ -106,9 +106,12 @@
     lax.fori_loop(0, out_rows, conv_row, 0)
     first_core = lax.rem(me, 2) == 0
 
-    def raise_with(proj_in_ref):
-        raised = jnp.dot(
-            normed_ref[...], proj_in_ref[...], preferred_element_type=jnp.float32
+    def raise_with(proj_in_t_ref):
+        raised = lax.dot_general(
+            normed_ref[...],
+            proj_in_t_ref[...],
+            (((1,), (1,)), ((), ())),
+            preferred_element_type=jnp.float32,
         ) + bias_in_ref[...].astype(jnp.float32)
         act_ref[...] = (0.5 * raised * (1.0 + lax.erf(raised * (1.0 / math.sqrt(2.0))))).astype(
             jnp.bfloat16
@@ -174,12 +177,9 @@
     cells = out_ref.shape[0]
     edge = 3 * cells // 4
 
-    def lower_with(proj_out_t_ref):
-        update = lax.dot_general(
-            hidden,
-            proj_out_t_ref[...],
-            (((1,), (1,)), ((), ())),
-            preferred_element_type=jnp.float32,
+    def lower_with(proj_out_ref):
+        update = jnp.dot(
+            hidden, proj_out_ref[...], preferred_element_type=jnp.float32
         ) + bias_out_ref[...].astype(jnp.float32)
         current = padded_ref[pl.ds(edge, cells), :].astype(jnp.float32)
         out_ref[...] = (current + update).astype(out_ref.dtype)
@@ -262,7 +262,7 @@
     channels = padded.shape[1]
     padded_rows = padded.shape[0] // cols
     cells = (padded_rows - 6) * cols
-    hidden_units = held.shape[1]
+    hidden_units = held.shape[0]
     vmem = pl.BlockSpec(memory_space=pltpu.VMEM)
     out_shape = [jax.ShapeDtypeStruct((cells, channels), padded.dtype)]
     scratch = [
@@ -366,13 +366,93 @@
     return produced, arriving
 
 
+def _gather_kernel(n, mine_ref, held_ref, other_ref, send_sem, recv_sem, pass_send, pass_recv):
+    me = lax.axis_index("dp")
+    row = lax.axis_index("row")
+    partner = {"row": row + 1 - 2 * lax.rem(row, 2)}
+    right = {"dp": lax.rem(me + 1, n)}
+    left = {"dp": lax.rem(me + n - 1, n)}
+    barrier = pltpu.get_barrier_semaphore()
+    for peer in (right, left, partner):
+        pl.semaphore_signal(barrier, inc=1, device_id=peer, device_id_type=MESH)
+    pl.semaphore_wait(barrier, 3)
+    sends = []
+
+    def send(src, dst, send_sems, recv_sems, slot, peer):
+        copy = pltpu.make_async_remote_copy(
+            src_ref=src,
+            dst_ref=dst.at[slot],
+            send_sem=send_sems.at[len(sends)],
+            recv_sem=recv_sems.at[slot],
+            device_id=peer,
+            device_id_type=MESH,
+        )
+        copy.start()
+        sends.append(copy)
+
+    def arrived(slot):
+        pltpu.make_async_remote_copy(
+            src_ref=mine_ref,
+            dst_ref=held_ref.at[slot],
+            send_sem=send_sem.at[0],
+            recv_sem=recv_sem.at[slot],
+            device_id=right,
+            device_id_type=MESH,
+        ).wait_recv()
+
+    to_right = n // 2
+    to_left = n - 1 - to_right
+    send(mine_ref, held_ref, send_sem, recv_sem, me, right)
+    send(mine_ref, held_ref, send_sem, recv_sem, me, left)
+    send(mine_ref, other_ref, pass_send, pass_recv, me, partner)
+    held_ref[me] = mine_ref[...]
+    for k in range(1, max(to_right, to_left) + 1):
+        if k <= to_right:
+            origin = lax.rem(me + n - k, n)
+            arrived(origin)
+            if k < to_right:
+                send(held_ref.at[origin], held_ref, send_sem, recv_sem, origin, right)
+            send(held_ref.at[origin], other_ref, pass_send, pass_recv, origin, partner)
+        if k <= to_left:
+            origin = lax.rem(me + k, n)
+            arrived(origin)
+            if k < to_left:
+                send(held_ref.at[origin], held_ref, send_sem, recv_sem, origin, left)
+            send(held_ref.at[origin], other_ref, pass_send, pass_recv, origin, partner)
+    for slot in range(n):
+        pltpu.make_async_remote_copy(
+            src_ref=mine_ref,
+            dst_ref=other_ref.at[slot],
+            send_sem=pass_send.at[0],
+            recv_sem=pass_recv.at[slot],
+            device_id=partner,
+            device_id_type=MESH,
+        ).wait_recv()
+    for copy in sends:
+        copy.wait_send()
+
+
 def gathered_weights(proj_in, proj_out):
-    rows = lax.axis_size("row")
+    n = lax.axis_size("dp")
     first_core = lax.rem(lax.axis_index("row"), 2) == 0
-    mine = jnp.where(first_core, proj_in, proj_out.T)
-    held = lax.all_gather(mine, "dp", axis=1, tiled=True)
-    other = lax.ppermute(held, "row", [(r, r ^ 1) for r in range(rows)])
-    return held, other
+    mine = jnp.where(first_core, proj_in.T, proj_out)
+    part, channels = mine.shape
+    vmem = pl.BlockSpec(memory_space=pltpu.VMEM)
+    gathered = jax.ShapeDtypeStruct((n, part, channels), mine.dtype)
+    held, other = pl.pallas_call(
+        functools.partial(_gather_kernel, n),
+        out_shape=[gathered, gathered],
+        in_specs=[vmem],
+        out_specs=[vmem, vmem],
+        scratch_shapes=[
+            pltpu.SemaphoreType.DMA((2 * n,)),
+            pltpu.SemaphoreType.DMA((n,)),
+            pltpu.SemaphoreType.DMA((2 * n,)),
+            pltpu.SemaphoreType.DMA((n,)),
+        ],
+        compiler_params=pltpu.CompilerParams(collective_id=7, has_side_effects=True),
+    )(mine)
+    return held.reshape(n * part, channels), other.reshape(n * part, channels)
 
 
 def on_device(

time: 200 us -> 182 us (0.910)
  Pallas kernels: 140 us -> 168 us
  blocking collectives: 23.6 us -> 0 us
  local copies, waits for them, and re-layouts: 13.1 us -> 5.03 us
  starting transfers between devices: 13.3 us -> 6.48 us
  waiting for transfers between devices: 6.39 us -> 0.01 us
    pallas_call x0 -> x1, Pallas kernels: none -> 25.9 us  [gathered_weights(): pl.pallas_call(functools.partial(_gather_kernel, n), out_shape=[gathered,...]
    all_gather x1 -> x0, blocking collectives: 23.6 us -> none  [gathered_weights(): held = lax.all_gather(mine, 'dp', axis=1, tiled=True)]
    ppermute x1 -> x0, starting transfers between devices: 7.45 us -> none  [gathered_weights(): other = lax.ppermute(held, 'row', [(r, r ^ 1) for r in range(rows)])]
    unnamed x16 -> x30, local copies, waits for them, and re-layouts: 7.35 us -> 1.32 us
    ppermute x1, waiting for transfers between devices: 3.74 us -> 0.01 us  [extended(): lax.ppermute(head, axis, [((i + 1) % count, i) for i in range(ends)])]
    ppermute x1, waiting for transfers between devices: 2.65 us -> 0.01 us  [extended(): lax.ppermute(tail, axis, [(i, (i + 1) % count) for i in range(ends)])]
    pallas_call x7, Pallas kernels: 140 us -> 142 us  [pointwise(): pl.pallas_call(functools.partial(_pointwise_kernel, n, sections, hand_on,...]
  transfers between devices with their start and end apart: 3 -> 2, of which waited for: 2 -> 0; matrix products, arithmetic and copies ran while one was open for 2% -> 1% of each run, Pallas kernels for 0% -> 14%
where the time goes in v1:
time: 182 us; the launch traced here: 181 us
  Pallas kernels  168 us (92%)
  starting transfers between devices  6.48 us (4%)
  local copies, waits for them, and re-layouts  5.03 us (3%)
    pallas_call x7, Pallas kernels, pointwise(): pl.pallas_call(functools.partial(_pointwise_kernel, n, sections, hand_on,...  142 us
    pallas_call x1, Pallas kernels, gathered_weights(): pl.pallas_call(functools.partial(_gather_kernel, n), out_shape=[gathered,...  25.9 us
    ppermute x1, starting transfers between devices, extended(): lax.ppermute(tail, axis, [(i, (i + 1) % count) for i in range(ends)])  4.56 us
  transfers between devices with their start and end apart: 2, of which 0 were waited for; matrix products, arithmetic and copies ran while one was open for 1% of the time, Pallas kernels for 14%

profile of v1, /device:TPU:7, one launch (start us, length us, event | category | flops | bytes accessed | tf_op | source)
XLA Modules:
  0.0 181.1 jit_solution(10710439454159893590)
XLA Ops:
  0.0 0.0 copy-start.9
  0.0 1.3 fusion
  1.3 4.6 %collective-permute-start = (bf16[4,3,48,352]{3,2,1,0:T(8,128)(2,1)S(1)}, bf16[4,3,48,352]{3,2,1,0:T(8,128)(2,1)S(1)}, u32[]{:S(2)}, u32[]{:S(2)}) collective-permute-start(bf16[4,3,48,352]{3,2,1,0:T(8,128)(2,1)S(1)} %get-tuple-element.33), channel_id=1, source_target_pairs={{0,8},{8,16},{16,24},{24,32},{32,40},{40,48},{48,56},{56,64},{64,7... | collective-permute-start | bytes 1216520 | tf_op jit(solution)/shard_map/ppermute | solution.py:25
  5.9 1.9 %collective-permute-start.1 = (bf16[4,3,48,352]{3,2,1,0:T(8,128)(2,1)S(1)}, bf16[4,3,48,352]{3,2,1,0:T(8,128)(2,1)S(1)}, u32[]{:S(2)}, u32[]{:S(2)}) collective-permute-start(bf16[4,3,48,352]{3,2,1,0:T(8,128)(2,1)S(1)} %get-tuple-element.34), channel_id=1, source_target_pairs={{8,0},{16,8},{24,16},{32,24},{40,32},{48,40},{56,48},{64,56},{72,6... | collective-permute-start | bytes 1216520 | tf_op jit(solution)/shard_map/ppermute | solution.py:27
  7.8 0.0 copy-done.11
  7.9 0.6 reshape_squeeze.2.taps_ref
  8.5 0.0 copy-done.10
  8.5 0.0 copy-done.9
  8.5 0.7 bitcast_select_fusion.mine_ref
  9.2 25.9 %shard_map.109 = (bf16[8,176,352]{2,1,0:T(8,128)(2,1)}, bf16[8,176,352]{2,1,0:T(8,128)(2,1)}) custom-call(bf16[176,352]{1,0:T(8,128)(2,1)} %bitcast_select_fusion.mine_ref), custom_call_target="tpu_custom_call" | custom-call | tf_op jit(solution)/shard_map/pallas_call | solution.py:442
  35.1 0.0 collective-permute-done
  35.1 0.0 collective-permute-done.1
  35.2 0.0 copy-done.1
  35.2 0.3 pad_maximum_fusion
  35.5 0.0 copy-start
  35.5 0.8 slice.14
  36.3 0.4 copy-done
  36.7 28.9 %shard_map.110 = (bf16[192,352]{1,0:T(8,128)(2,1)}, bf16[480,352]{1,0:T(8,128)(2,1)}) custom-call(bf16[480,352]{1,0:T(8,128)(2,1)} %bitcast.43, bf16[4,480,352]{2,1,0:T(8,128)(2,1)} %bitcast.20, bf16[1408,352]{1,0:T(8,128)(2,1)} %bitcast.27, bf16[1408,352]{1,0:T(8,128)(2,1)} %bitcast.34, bf16[1,1408]{1,0:T(2,128)(2,1)} %bias_in_ref.13, ...), custom_call_target="tpu_custom_call" | custom-call | flops 380633088 | bytes 2523136 | tf_op jit(solution)/shard_map/pallas_call | solution.py:283
  65.7 21.6 %shard_map.111 = (bf16[192,352]{1,0:T(8,128)(2,1)}, bf16[480,352]{1,0:T(8,128)(2,1)}) custom-call(bf16[480,352]{1,0:T(8,128)(2,1)} %get-tuple-element.22.padded_ref, bf16[4,480,352]{2,1,0:T(8,128)(2,1)} %bitcast.21, bf16[1408,352]{1,0:T(8,128)(2,1)} %bitcast.28, bf16[1408,352]{1,0:T(8,128)(2,1)} %bitcast.35, bf16[1,1408]{1,0:T(2,128)(2,1)} %bias_in_ref.13, ...), custom_call_target="tpu_custom_call" | custom-call | flops 380633088 | bytes 2523136 | tf_op jit(solution)/shard_map/pallas_call | solution.py:283
  87.2 21.7 %shard_map.112 = (bf16[192,352]{1,0:T(8,128)(2,1)}, bf16[480,352]{1,0:T(8,128)(2,1)}) custom-call(bf16[480,352]{1,0:T(8,128)(2,1)} %get-tuple-element.24.padded_ref, bf16[4,480,352]{2,1,0:T(8,128)(2,1)} %bitcast.22, bf16[1408,352]{1,0:T(8,128)(2,1)} %bitcast.29, bf16[1408,352]{1,0:T(8,128)(2,1)} %bitcast.36, bf16[1,1408]{1,0:T(2,128)(2,1)} %bias_in_ref.13, ...), custom_call_target="tpu_custom_call" | custom-call | flops 380633088 | bytes 2523136 | tf_op jit(solution)/shard_map/pallas_call | solution.py:283
  108.9 19.1 %shard_map.113 = (bf16[192,352]{1,0:T(8,128)(2,1)}, bf16[480,352]{1,0:T(8,128)(2,1)}) custom-call(bf16[480,352]{1,0:T(8,128)(2,1)} %get-tuple-element.26.padded_ref, bf16[4,480,352]{2,1,0:T(8,128)(2,1)} %bitcast.23, bf16[1408,352]{1,0:T(8,128)(2,1)} %bitcast.30, bf16[1408,352]{1,0:T(8,128)(2,1)} %bitcast.37, bf16[1,1408]{1,0:T(2,128)(2,1)} %bias_in_ref.13, ...), custom_call_target="tpu_custom_call" | custom-call | flops 380633088 | bytes 2523136 | tf_op jit(solution)/shard_map/pallas_call | solution.py:283
  128.0 18.9 %shard_map.114 = (bf16[192,352]{1,0:T(8,128)(2,1)}, bf16[480,352]{1,0:T(8,128)(2,1)}) custom-call(bf16[480,352]{1,0:T(8,128)(2,1)} %get-tuple-element.28.padded_ref, bf16[4,480,352]{2,1,0:T(8,128)(2,1)} %bitcast.24, bf16[1408,352]{1,0:T(8,128)(2,1)} %bitcast.31, bf16[1408,352]{1,0:T(8,128)(2,1)} %bitcast.38, bf16[1,1408]{1,0:T(2,128)(2,1)} %bias_in_ref.13, ...), custom_call_target="tpu_custom_call" | custom-call | flops 380633088 | bytes 2523136 | tf_op jit(solution)/shard_map/pallas_call | solution.py:283
  146.9 18.7 %shard_map.115 = (bf16[192,352]{1,0:T(8,128)(2,1)}, bf16[480,352]{1,0:T(8,128)(2,1)}) custom-call(bf16[480,352]{1,0:T(8,128)(2,1)} %get-tuple-element.30.padded_ref, bf16[4,480,352]{2,1,0:T(8,128)(2,1)} %bitcast.25, bf16[1408,352]{1,0:T(8,128)(2,1)} %bitcast.32, bf16[1408,352]{1,0:T(8,128)(2,1)} %bitcast.39, bf16[1,1408]{1,0:T(2,128)(2,1)} %bias_in_ref.13, ...), custom_call_target="tpu_custom_call" | custom-call | flops 380633088 | bytes 2523136 | tf_op jit(solution)/shard_map/pallas_call | solution.py:283
  165.7 13.5 %shard_map.116 = bf16[192,352]{1,0:T(8,128)(2,1)} custom-call(bf16[480,352]{1,0:T(8,128)(2,1)} %get-tuple-element.32.padded_ref, bf16[4,480,352]{2,1,0:T(8,128)(2,1)} %bitcast.26, bf16[1408,352]{1,0:T(8,128)(2,1)} %bitcast.33, bf16[1408,352]{1,0:T(8,128)(2,1)} %bitcast.40, bf16[1,1408]{1,0:T(2,128)(2,1)} %bias_in_ref.13, bf16[1,1408]{1,0:T(2,128)(2,1)} %gamma_ref.13, ...), custom_call_target="tpu_custom_call" | custom-call | flops 380633088 | bytes 2523136 | tf_op jit(solution)/shard_map/pallas_call | solution.py:283
  179.2 0.0 copy-start.8
  179.2 0.0 copy-start.2
  179.2 0.0 copy-done.3
  179.2 0.0 copy-done.4
  179.3 0.0 copy-done.5
  179.4 0.7 copy-done.8
  180.1 0.0 copy-done.2
  180.2 0.9 dynamic-slice_bitcast_fusion
  (17 shorter events, 0.2 us)
Async XLA Ops:
  0.0 35.2 %copy-start.1 = (bf16[4,1,4,48,352]{4,3,2,1,0:T(8,128)(2,1)S(1)}, bf16[4,1,4,48,352]{4,3,2,1,0:T(8,128)(2,1)}, u32[]{:S(2)}) copy-start(bf16[4,1,4,48,352]{4,3,2,1,0:T(8,128)(2,1)} %param.11) | copy-start | bytes 1622020
  0.0 7.8 %copy-start.11 = (bf16[1,7,7,352]{3,2,1,0:T(8,128)(2,1)S(1)}, bf16[1,7,7,352]{3,2,1,0:T(8,128)(2,1)}, u32[]{:S(2)}) copy-start(bf16[1,7,7,352]{3,2,1,0:T(8,128)(2,1)} %param.12) | copy-start | bytes 103492
  0.0 8.5 %copy-start.10 = (bf16[1,176,352]{2,1,0:T(8,128)(2,1)S(1)}, bf16[1,176,352]{2,1,0:T(8,128)(2,1)}, u32[]{:S(2)}) copy-start(bf16[1,176,352]{2,1,0:T(8,128)(2,1)} %param.20) | copy-start | bytes 371716
  0.0 8.5 %copy-start.9 = (bf16[1,352,176]{1,2,0:T(8,128)(2,1)S(1)}, bf16[1,352,176]{1,2,0:T(8,128)(2,1)}, u32[]{:S(2)}) copy-start(bf16[1,352,176]{1,2,0:T(8,128)(2,1)} %param.16) | copy-start | bytes 371716
  1.3 33.8 %collective-permute-start = (bf16[4,3,48,352]{3,2,1,0:T(8,128)(2,1)S(1)}, bf16[4,3,48,352]{3,2,1,0:T(8,128)(2,1)S(1)}, u32[]{:S(2)}, u32[]{:S(2)}) collective-permute-start(bf16[4,3,48,352]{3,2,1,0:T(8,128)(2,1)S(1)} %get-tuple-element.33), channel_id=1, source_target_pairs={{0,8},{8,16},{16,24},{24,32},{32,40},{40,48},{48,56},{56,64},{64,7... | collective-permute-start | bytes 1216520 | tf_op jit(solution)/shard_map/ppermute | solution.py:25
  5.9 29.2 %collective-permute-start.1 = (bf16[4,3,48,352]{3,2,1,0:T(8,128)(2,1)S(1)}, bf16[4,3,48,352]{3,2,1,0:T(8,128)(2,1)S(1)}, u32[]{:S(2)}, u32[]{:S(2)}) collective-permute-start(bf16[4,3,48,352]{3,2,1,0:T(8,128)(2,1)S(1)} %get-tuple-element.34), channel_id=1, source_target_pairs={{8,0},{16,8},{24,16},{32,24},{40,32},{48,40},{56,48},{64,56},{72,6... | collective-permute-start | bytes 1216520 | tf_op jit(solution)/shard_map/ppermute | solution.py:27
  35.5 1.3 copy-start
  165.7 13.5 %copy-start.3 = (bf16[192,352]{1,0:T(8,128)(2,1)S(1)}, bf16[192,352]{1,0:T(8,128)(2,1)}, u32[]{:S(2)}) copy-start(bf16[192,352]{1,0:T(8,128)(2,1)} %get-tuple-element.21) | copy-start | bytes 405508
  165.7 13.6 %copy-start.4 = (bf16[192,352]{1,0:T(8,128)(2,1)S(1)}, bf16[192,352]{1,0:T(8,128)(2,1)}, u32[]{:S(2)}) copy-start(bf16[192,352]{1,0:T(8,128)(2,1)} %get-tuple-element.23) | copy-start | bytes 405508
  165.7 13.6 %copy-start.5 = (bf16[192,352]{1,0:T(8,128)(2,1)S(1)}, bf16[192,352]{1,0:T(8,128)(2,1)}, u32[]{:S(2)}) copy-start(bf16[192,352]{1,0:T(8,128)(2,1)} %get-tuple-element.25) | copy-start | bytes 405508
  165.7 13.6 %copy-start.6 = (bf16[192,352]{1,0:T(8,128)(2,1)S(1)}, bf16[192,352]{1,0:T(8,128)(2,1)}, u32[]{:S(2)}) copy-start(bf16[192,352]{1,0:T(8,128)(2,1)} %get-tuple-element.27) | copy-start | bytes 405508
  165.7 13.7 %copy-start.7 = (bf16[192,352]{1,0:T(8,128)(2,1)S(1)}, bf16[192,352]{1,0:T(8,128)(2,1)}, u32[]{:S(2)}) copy-start(bf16[192,352]{1,0:T(8,128)(2,1)} %get-tuple-element.29) | copy-start | bytes 405508
  179.2 0.9 copy-start.8
  179.2 1.0 copy-start.2

commit v2 on v1

--- a/solution.py
+++ b/solution.py
@@ -404,21 +404,24 @@
     to_left = n - 1 - to_right
     send(mine_ref, held_ref, send_sem, recv_sem, me, right)
     send(mine_ref, held_ref, send_sem, recv_sem, me, left)
-    send(mine_ref, other_ref, pass_send, pass_recv, me, partner)
     held_ref[me] = mine_ref[...]
+    landed = []
     for k in range(1, max(to_right, to_left) + 1):
         if k <= to_right:
             origin = lax.rem(me + n - k, n)
             arrived(origin)
             if k < to_right:
                 send(held_ref.at[origin], held_ref, send_sem, recv_sem, origin, right)
-            send(held_ref.at[origin], other_ref, pass_send, pass_recv, origin, partner)
+            landed.append(origin)
         if k <= to_left:
             origin = lax.rem(me + k, n)
             arrived(origin)
             if k < to_left:
                 send(held_ref.at[origin], held_ref, send_sem, recv_sem, origin, left)
-            send(held_ref.at[origin], other_ref, pass_send, pass_recv, origin, partner)
+            landed.append(origin)
+    send(mine_ref, other_ref, pass_send, pass_recv, me, partner)
+    for origin in landed:
+        send(held_ref.at[origin], other_ref, pass_send, pass_recv, origin, partner)
     for slot in range(n):
         pltpu.make_async_remote_copy(
             src_ref=mine_ref,

time: 182 us -> 184 us (1.011)
  Pallas kernels: 168 us -> 170 us
  transfers between devices with their start and end apart: 2 -> 2, of which waited for: 0 -> 0; matrix products, arithmetic and copies ran while one was open for 1% -> 1% of each run, Pallas kernels for 14% -> 15%
where the time goes in v2:
time: 184 us; the launch traced here: 183 us
  Pallas kernels  170 us (92%)
  starting transfers between devices  6.48 us (4%)
  local copies, waits for them, and re-layouts  5.03 us (3%)
    pallas_call x7, Pallas kernels, pointwise(): pl.pallas_call(functools.partial(_pointwise_kernel, n, sections, hand_on,...  142 us
    pallas_call x1, Pallas kernels, gathered_weights(): pl.pallas_call(functools.partial(_gather_kernel, n), out_shape=[gathered,...  27.3 us
    ppermute x1, starting transfers between devices, extended(): lax.ppermute(tail, axis, [(i, (i + 1) % count) for i in range(ends)])  4.56 us
  transfers between devices with their start and end apart: 2, of which 0 were waited for; matrix products, arithmetic and copies ran while one was open for 1% of the time, Pallas kernels for 15%

profile of v2, /device:TPU:7, one launch (start us, length us, event | category | flops | bytes accessed | tf_op | source)
XLA Modules:
  0.0 182.5 jit_solution(17805017037292826734)
XLA Ops:
  0.0 0.0 copy-start.9
  0.0 1.3 fusion
  1.3 4.6 %collective-permute-start = (bf16[4,3,48,352]{3,2,1,0:T(8,128)(2,1)S(1)}, bf16[4,3,48,352]{3,2,1,0:T(8,128)(2,1)S(1)}, u32[]{:S(2)}, u32[]{:S(2)}) collective-permute-start(bf16[4,3,48,352]{3,2,1,0:T(8,128)(2,1)S(1)} %get-tuple-element.33), channel_id=1, source_target_pairs={{0,8},{8,16},{16,24},{24,32},{32,40},{40,48},{48,56},{56,64},{64,7... | collective-permute-start | bytes 1216520 | tf_op jit(solution)/shard_map/ppermute | solution.py:25
  5.9 1.9 %collective-permute-start.1 = (bf16[4,3,48,352]{3,2,1,0:T(8,128)(2,1)S(1)}, bf16[4,3,48,352]{3,2,1,0:T(8,128)(2,1)S(1)}, u32[]{:S(2)}, u32[]{:S(2)}) collective-permute-start(bf16[4,3,48,352]{3,2,1,0:T(8,128)(2,1)S(1)} %get-tuple-element.34), channel_id=1, source_target_pairs={{8,0},{16,8},{24,16},{32,24},{40,32},{48,40},{56,48},{64,56},{72,6... | collective-permute-start | bytes 1216520 | tf_op jit(solution)/shard_map/ppermute | solution.py:27
  7.8 0.0 copy-done.11
  7.9 0.6 reshape_squeeze.2.taps_ref
  8.5 0.0 copy-done.10
  8.5 0.0 copy-done.9
  8.5 0.7 bitcast_select_fusion.mine_ref
  9.2 27.3 %shard_map.109 = (bf16[8,176,352]{2,1,0:T(8,128)(2,1)}, bf16[8,176,352]{2,1,0:T(8,128)(2,1)}) custom-call(bf16[176,352]{1,0:T(8,128)(2,1)} %bitcast_select_fusion.mine_ref), custom_call_target="tpu_custom_call" | custom-call | tf_op jit(solution)/shard_map/pallas_call | solution.py:445
  36.5 0.0 collective-permute-done
  36.5 0.0 collective-permute-done.1
  36.5 0.0 copy-done.1
  36.5 0.3 pad_maximum_fusion
  36.8 0.0 copy-start
  36.8 0.8 slice.14
  37.7 0.4 copy-done
  38.1 28.9 %shard_map.110 = (bf16[192,352]{1,0:T(8,128)(2,1)}, bf16[480,352]{1,0:T(8,128)(2,1)}) custom-call(bf16[480,352]{1,0:T(8,128)(2,1)} %bitcast.43, bf16[4,480,352]{2,1,0:T(8,128)(2,1)} %bitcast.20, bf16[1408,352]{1,0:T(8,128)(2,1)} %bitcast.27, bf16[1408,352]{1,0:T(8,128)(2,1)} %bitcast.34, bf16[1,1408]{1,0:T(2,128)(2,1)} %bias_in_ref.13, ...), custom_call_target="tpu_custom_call" | custom-call | flops 380633088 | bytes 2523136 | tf_op jit(solution)/shard_map/pallas_call | solution.py:283
  67.0 21.6 %shard_map.111 = (bf16[192,352]{1,0:T(8,128)(2,1)}, bf16[480,352]{1,0:T(8,128)(2,1)}) custom-call(bf16[480,352]{1,0:T(8,128)(2,1)} %get-tuple-element.22.padded_ref, bf16[4,480,352]{2,1,0:T(8,128)(2,1)} %bitcast.21, bf16[1408,352]{1,0:T(8,128)(2,1)} %bitcast.28, bf16[1408,352]{1,0:T(8,128)(2,1)} %bitcast.35, bf16[1,1408]{1,0:T(2,128)(2,1)} %bias_in_ref.13, ...), custom_call_target="tpu_custom_call" | custom-call | flops 380633088 | bytes 2523136 | tf_op jit(solution)/shard_map/pallas_call | solution.py:283
  88.7 21.6 %shard_map.112 = (bf16[192,352]{1,0:T(8,128)(2,1)}, bf16[480,352]{1,0:T(8,128)(2,1)}) custom-call(bf16[480,352]{1,0:T(8,128)(2,1)} %get-tuple-element.24.padded_ref, bf16[4,480,352]{2,1,0:T(8,128)(2,1)} %bitcast.22, bf16[1408,352]{1,0:T(8,128)(2,1)} %bitcast.29, bf16[1408,352]{1,0:T(8,128)(2,1)} %bitcast.36, bf16[1,1408]{1,0:T(2,128)(2,1)} %bias_in_ref.13, ...), custom_call_target="tpu_custom_call" | custom-call | flops 380633088 | bytes 2523136 | tf_op jit(solution)/shard_map/pallas_call | solution.py:283
  110.3 19.2 %shard_map.113 = (bf16[192,352]{1,0:T(8,128)(2,1)}, bf16[480,352]{1,0:T(8,128)(2,1)}) custom-call(bf16[480,352]{1,0:T(8,128)(2,1)} %get-tuple-element.26.padded_ref, bf16[4,480,352]{2,1,0:T(8,128)(2,1)} %bitcast.23, bf16[1408,352]{1,0:T(8,128)(2,1)} %bitcast.30, bf16[1408,352]{1,0:T(8,128)(2,1)} %bitcast.37, bf16[1,1408]{1,0:T(2,128)(2,1)} %bias_in_ref.13, ...), custom_call_target="tpu_custom_call" | custom-call | flops 380633088 | bytes 2523136 | tf_op jit(solution)/shard_map/pallas_call | solution.py:283
  129.5 18.8 %shard_map.114 = (bf16[192,352]{1,0:T(8,128)(2,1)}, bf16[480,352]{1,0:T(8,128)(2,1)}) custom-call(bf16[480,352]{1,0:T(8,128)(2,1)} %get-tuple-element.28.padded_ref, bf16[4,480,352]{2,1,0:T(8,128)(2,1)} %bitcast.24, bf16[1408,352]{1,0:T(8,128)(2,1)} %bitcast.31, bf16[1408,352]{1,0:T(8,128)(2,1)} %bitcast.38, bf16[1,1408]{1,0:T(2,128)(2,1)} %bias_in_ref.13, ...), custom_call_target="tpu_custom_call" | custom-call | flops 380633088 | bytes 2523136 | tf_op jit(solution)/shard_map/pallas_call | solution.py:283
  148.3 18.7 %shard_map.115 = (bf16[192,352]{1,0:T(8,128)(2,1)}, bf16[480,352]{1,0:T(8,128)(2,1)}) custom-call(bf16[480,352]{1,0:T(8,128)(2,1)} %get-tuple-element.30.padded_ref, bf16[4,480,352]{2,1,0:T(8,128)(2,1)} %bitcast.25, bf16[1408,352]{1,0:T(8,128)(2,1)} %bitcast.32, bf16[1408,352]{1,0:T(8,128)(2,1)} %bitcast.39, bf16[1,1408]{1,0:T(2,128)(2,1)} %bias_in_ref.13, ...), custom_call_target="tpu_custom_call" | custom-call | flops 380633088 | bytes 2523136 | tf_op jit(solution)/shard_map/pallas_call | solution.py:283
  167.0 0.0 copy-start.3
  167.0 0.0 copy-start.4
  167.0 0.0 copy-start.5
  167.1 13.6 %shard_map.116 = bf16[192,352]{1,0:T(8,128)(2,1)} custom-call(bf16[480,352]{1,0:T(8,128)(2,1)} %get-tuple-element.32.padded_ref, bf16[4,480,352]{2,1,0:T(8,128)(2,1)} %bitcast.26, bf16[1408,352]{1,0:T(8,128)(2,1)} %bitcast.33, bf16[1408,352]{1,0:T(8,128)(2,1)} %bitcast.40, bf16[1,1408]{1,0:T(2,128)(2,1)} %bias_in_ref.13, bf16[1,1408]{1,0:T(2,128)(2,1)} %gamma_ref.13, ...), custom_call_target="tpu_custom_call" | custom-call | flops 380633088 | bytes 2523136 | tf_op jit(solution)/shard_map/pallas_call | solution.py:283
  180.8 0.0 copy-done.6
  180.8 0.0 copy-done.7
  180.9 0.7 copy-done.8
  181.6 0.0 copy-done.2
  181.7 0.9 dynamic-slice_bitcast_fusion
  (17 shorter events, 0.2 us)
Async XLA Ops:
  0.0 36.5 %copy-start.1 = (bf16[4,1,4,48,352]{4,3,2,1,0:T(8,128)(2,1)S(1)}, bf16[4,1,4,48,352]{4,3,2,1,0:T(8,128)(2,1)}, u32[]{:S(2)}) copy-start(bf16[4,1,4,48,352]{4,3,2,1,0:T(8,128)(2,1)} %param.11) | copy-start | bytes 1622020
  0.0 7.8 %copy-start.11 = (bf16[1,7,7,352]{3,2,1,0:T(8,128)(2,1)S(1)}, bf16[1,7,7,352]{3,2,1,0:T(8,128)(2,1)}, u32[]{:S(2)}) copy-start(bf16[1,7,7,352]{3,2,1,0:T(8,128)(2,1)} %param.12) | copy-start | bytes 103492
  0.0 8.5 %copy-start.10 = (bf16[1,176,352]{2,1,0:T(8,128)(2,1)S(1)}, bf16[1,176,352]{2,1,0:T(8,128)(2,1)}, u32[]{:S(2)}) copy-start(bf16[1,176,352]{2,1,0:T(8,128)(2,1)} %param.20) | copy-start | bytes 371716
  0.0 8.5 %copy-start.9 = (bf16[1,352,176]{1,2,0:T(8,128)(2,1)S(1)}, bf16[1,352,176]{1,2,0:T(8,128)(2,1)}, u32[]{:S(2)}) copy-start(bf16[1,352,176]{1,2,0:T(8,128)(2,1)} %param.16) | copy-start | bytes 371716
  1.3 35.1 %collective-permute-start = (bf16[4,3,48,352]{3,2,1,0:T(8,128)(2,1)S(1)}, bf16[4,3,48,352]{3,2,1,0:T(8,128)(2,1)S(1)}, u32[]{:S(2)}, u32[]{:S(2)}) collective-permute-start(bf16[4,3,48,352]{3,2,1,0:T(8,128)(2,1)S(1)} %get-tuple-element.33), channel_id=1, source_target_pairs={{0,8},{8,16},{16,24},{24,32},{32,40},{40,48},{48,56},{56,64},{64,7... | collective-permute-start | bytes 1216520 | tf_op jit(solution)/shard_map/ppermute | solution.py:25
  5.9 30.6 %collective-permute-start.1 = (bf16[4,3,48,352]{3,2,1,0:T(8,128)(2,1)S(1)}, bf16[4,3,48,352]{3,2,1,0:T(8,128)(2,1)S(1)}, u32[]{:S(2)}, u32[]{:S(2)}) collective-permute-start(bf16[4,3,48,352]{3,2,1,0:T(8,128)(2,1)S(1)} %get-tuple-element.34), channel_id=1, source_target_pairs={{8,0},{16,8},{24,16},{32,24},{40,32},{48,40},{56,48},{64,56},{72,6... | collective-permute-start | bytes 1216520 | tf_op jit(solution)/shard_map/ppermute | solution.py:27
  36.8 1.3 copy-start
  167.0 13.7 %copy-start.3 = (bf16[192,352]{1,0:T(8,128)(2,1)S(1)}, bf16[192,352]{1,0:T(8,128)(2,1)}, u32[]{:S(2)}) copy-start(bf16[192,352]{1,0:T(8,128)(2,1)} %get-tuple-element.21) | copy-start | bytes 405508
  167.0 13.7 %copy-start.4 = (bf16[192,352]{1,0:T(8,128)(2,1)S(1)}, bf16[192,352]{1,0:T(8,128)(2,1)}, u32[]{:S(2)}) copy-start(bf16[192,352]{1,0:T(8,128)(2,1)} %get-tuple-element.23) | copy-start | bytes 405508
  167.0 13.7 %copy-start.5 = (bf16[192,352]{1,0:T(8,128)(2,1)S(1)}, bf16[192,352]{1,0:T(8,128)(2,1)}, u32[]{:S(2)}) copy-start(bf16[192,352]{1,0:T(8,128)(2,1)} %get-tuple-element.25) | copy-start | bytes 405508
  167.0 13.7 %copy-start.6 = (bf16[192,352]{1,0:T(8,128)(2,1)S(1)}, bf16[192,352]{1,0:T(8,128)(2,1)}, u32[]{:S(2)}) copy-start(bf16[192,352]{1,0:T(8,128)(2,1)} %get-tuple-element.27) | copy-start | bytes 405508
  167.1 13.8 %copy-start.7 = (bf16[192,352]{1,0:T(8,128)(2,1)S(1)}, bf16[192,352]{1,0:T(8,128)(2,1)}, u32[]{:S(2)}) copy-start(bf16[192,352]{1,0:T(8,128)(2,1)} %get-tuple-element.29) | copy-start | bytes 405508
  180.7 0.9 copy-start.8
  180.7 1.0 copy-start.2

commit v3 on v1

--- a/solution.py
+++ b/solution.py
@@ -366,7 +366,7 @@
     return produced, arriving
 
 
-def _gather_kernel(n, mine_ref, held_ref, other_ref, send_sem, recv_sem, pass_send, pass_recv):
+def _gather_kernel(n, chunks, mine_ref, held_ref, other_ref, send_sem, recv_sem, pass_send, pass_recv):
     me = lax.axis_index("dp")
     row = lax.axis_index("row")
     partner = {"row": row + 1 - 2 * lax.rem(row, 2)}
@@ -377,57 +377,51 @@
         pl.semaphore_signal(barrier, inc=1, device_id=peer, device_id_type=MESH)
     pl.semaphore_wait(barrier, 3)
     sends = []
-
-    def send(src, dst, send_sems, recv_sems, slot, peer):
+    parts = len(chunks)
+
+    def send(src, dst, send_sems, recv_sems, slot, c, peer):
         copy = pltpu.make_async_remote_copy(
-            src_ref=src,
-            dst_ref=dst.at[slot],
+            src_ref=src.at[chunks[c]],
+            dst_ref=dst.at[slot, chunks[c]],
             send_sem=send_sems.at[len(sends)],
-            recv_sem=recv_sems.at[slot],
+            recv_sem=recv_sems.at[slot * parts + c],
             device_id=peer,
             device_id_type=MESH,
         )
         copy.start()
         sends.append(copy)
 
-    def arrived(slot):
+    def arrived(dst, recv_sems, slot, c):
         pltpu.make_async_remote_copy(
-            src_ref=mine_ref,
-            dst_ref=held_ref.at[slot],
+            src_ref=mine_ref.at[chunks[c]],
+            dst_ref=dst.at[slot, chunks[c]],
             send_sem=send_sem.at[0],
-            recv_sem=recv_sem.at[slot],
+            recv_sem=recv_sems.at[slot * parts + c],
             device_id=right,
             device_id_type=MESH,
         ).wait_recv()
 
     to_right = n // 2
     to_left = n - 1 - to_right
-    send(mine_ref, held_ref, send_sem, recv_sem, me, right)
-    send(mine_ref, held_ref, send_sem, recv_sem, me, left)
-    send(mine_ref, other_ref, pass_send, pass_recv, me, partner)
+    for c in range(parts):
+        send(mine_ref, held_ref, send_sem, recv_sem, me, c, right)
+        send(mine_ref, held_ref, send_sem, recv_sem, me, c, left)
+    for c in range(parts):
+        send(mine_ref, other_ref, pass_send, pass_recv, me, c, partner)
     held_ref[me] = mine_ref[...]
     for k in range(1, max(to_right, to_left) + 1):
-        if k <= to_right:
-            origin = lax.rem(me + n - k, n)
-            arrived(origin)
-            if k < to_right:
-                send(held_ref.at[origin], held_ref, send_sem, recv_sem, origin, right)
-            send(held_ref.at[origin], other_ref, pass_send, pass_recv, origin, partner)
-        if k <= to_left:
-            origin = lax.rem(me + k, n)
-            arrived(origin)
-            if k < to_left:
-                send(held_ref.at[origin], held_ref, send_sem, recv_sem, origin, left)
-            send(held_ref.at[origin], other_ref, pass_send, pass_recv, origin, partner)
+        for c in range(parts):
+            for steps, way, peer in ((to_right, -1, right), (to_left, 1, left)):
+                if k > steps:
+                    continue
+                origin = lax.rem(me + n + way * k, n)
+                arrived(held_ref, recv_sem, origin, c)
+                if k < steps:
+                    send(held_ref.at[origin], held_ref, send_sem, recv_sem, origin, c, peer)
+                send(held_ref.at[origin], other_ref, pass_send, pass_recv, origin, c, partner)
     for slot in range(n):
-        pltpu.make_async_remote_copy(
-            src_ref=mine_ref,
-            dst_ref=other_ref.at[slot],
-            send_sem=pass_send.at[0],
-            recv_sem=pass_recv.at[slot],
-            device_id=partner,
-            device_id_type=MESH,
-        ).wait_recv()
+        for c in range(parts):
+            arrived(other_ref, pass_recv, slot, c)
     for copy in sends:
         copy.wait_send()
 
@@ -440,15 +434,15 @@
     vmem = pl.BlockSpec(memory_space=pltpu.VMEM)
     gathered = jax.ShapeDtypeStruct((n, part, channels), mine.dtype)
     held, other = pl.pallas_call(
-        functools.partial(_gather_kernel, n),
+        functools.partial(_gather_kernel, n, (pl.ds(0, 96), pl.ds(96, part - 96))),
         out_shape=[gathered, gathered],
         in_specs=[vmem],
         out_specs=[vmem, vmem],
         scratch_shapes=[
+            pltpu.SemaphoreType.DMA((4 * n,)),
             pltpu.SemaphoreType.DMA((2 * n,)),
-            pltpu.SemaphoreType.DMA((n,)),
+            pltpu.SemaphoreType.DMA((4 * n,)),
             pltpu.SemaphoreType.DMA((2 * n,)),
-            pltpu.SemaphoreType.DMA((n,)),
         ],
         compiler_params=pltpu.CompilerParams(collective_id=7, has_side_effects=True),
     )(mine)

time: 182 us -> 180 us (0.989)
  Pallas kernels: 168 us -> 166 us
  transfers between devices with their start and end apart: 2 -> 2, of which waited for: 0 -> 0; matrix products, arithmetic and copies ran while one was open for 1% -> 1% of each run, Pallas kernels for 14% -> 13%
where the time goes in v3:
time: 180 us; the launch traced here: 179 us
  Pallas kernels  166 us (92%)
  starting transfers between devices  6.48 us (4%)
  local copies, waits for them, and re-layouts  5.03 us (3%)
    pallas_call x7, Pallas kernels, pointwise(): pl.pallas_call(functools.partial(_pointwise_kernel, n, sections, hand_on,...  142 us
    pallas_call x1, Pallas kernels, gathered_weights(): pl.pallas_call(functools.partial(_gather_kernel, n, (pl.ds(0, 96), pl.ds(...  24.2 us
    ppermute x1, starting transfers between devices, extended(): lax.ppermute(tail, axis, [(i, (i + 1) % count) for i in range(ends)])  4.56 us
  transfers between devices with their start and end apart: 2, of which 0 were waited for; matrix products, arithmetic and copies ran while one was open for 1% of the time, Pallas kernels for 13%

profile of v3, /device:TPU:7, one launch (start us, length us, event | category | flops | bytes accessed | tf_op | source)
XLA Modules:
  0.0 179.2 jit_solution(14004887436329169054)
XLA Ops:
  0.0 0.0 copy-start.9
  0.0 1.3 fusion
  1.3 4.6 %collective-permute-start = (bf16[4,3,48,352]{3,2,1,0:T(8,128)(2,1)S(1)}, bf16[4,3,48,352]{3,2,1,0:T(8,128)(2,1)S(1)}, u32[]{:S(2)}, u32[]{:S(2)}) collective-permute-start(bf16[4,3,48,352]{3,2,1,0:T(8,128)(2,1)S(1)} %get-tuple-element.33), channel_id=1, source_target_pairs={{0,8},{8,16},{16,24},{24,32},{32,40},{40,48},{48,56},{56,64},{64,7... | collective-permute-start | bytes 1216520 | tf_op jit(solution)/shard_map/ppermute | solution.py:25
  5.9 1.9 %collective-permute-start.1 = (bf16[4,3,48,352]{3,2,1,0:T(8,128)(2,1)S(1)}, bf16[4,3,48,352]{3,2,1,0:T(8,128)(2,1)S(1)}, u32[]{:S(2)}, u32[]{:S(2)}) collective-permute-start(bf16[4,3,48,352]{3,2,1,0:T(8,128)(2,1)S(1)} %get-tuple-element.34), channel_id=1, source_target_pairs={{8,0},{16,8},{24,16},{32,24},{40,32},{48,40},{56,48},{64,56},{72,6... | collective-permute-start | bytes 1216520 | tf_op jit(solution)/shard_map/ppermute | solution.py:27
  7.8 0.0 copy-done.11
  7.9 0.6 reshape_squeeze.2.taps_ref
  8.5 0.0 copy-done.10
  8.5 0.0 copy-done.9
  8.5 0.7 bitcast_select_fusion.mine_ref
  9.2 24.2 %shard_map.109 = (bf16[8,176,352]{2,1,0:T(8,128)(2,1)}, bf16[8,176,352]{2,1,0:T(8,128)(2,1)}) custom-call(bf16[176,352]{1,0:T(8,128)(2,1)} %bitcast_select_fusion.mine_ref), custom_call_target="tpu_custom_call" | custom-call | tf_op jit(solution)/shard_map/pallas_call | solution.py:436
  33.4 0.0 collective-permute-done
  33.4 0.0 collective-permute-done.1
  33.4 0.0 copy-done.1
  33.4 0.3 pad_maximum_fusion
  33.7 0.0 copy-start
  33.7 0.8 slice.14
  34.6 0.4 copy-done
  35.0 28.6 %shard_map.110 = (bf16[192,352]{1,0:T(8,128)(2,1)}, bf16[480,352]{1,0:T(8,128)(2,1)}) custom-call(bf16[480,352]{1,0:T(8,128)(2,1)} %bitcast.43, bf16[4,480,352]{2,1,0:T(8,128)(2,1)} %bitcast.20, bf16[1408,352]{1,0:T(8,128)(2,1)} %bitcast.27, bf16[1408,352]{1,0:T(8,128)(2,1)} %bitcast.34, bf16[1,1408]{1,0:T(2,128)(2,1)} %bias_in_ref.13, ...), custom_call_target="tpu_custom_call" | custom-call | flops 380633088 | bytes 2523136 | tf_op jit(solution)/shard_map/pallas_call | solution.py:283
  63.6 21.3 %shard_map.111 = (bf16[192,352]{1,0:T(8,128)(2,1)}, bf16[480,352]{1,0:T(8,128)(2,1)}) custom-call(bf16[480,352]{1,0:T(8,128)(2,1)} %get-tuple-element.22.padded_ref, bf16[4,480,352]{2,1,0:T(8,128)(2,1)} %bitcast.21, bf16[1408,352]{1,0:T(8,128)(2,1)} %bitcast.28, bf16[1408,352]{1,0:T(8,128)(2,1)} %bitcast.35, bf16[1,1408]{1,0:T(2,128)(2,1)} %bias_in_ref.13, ...), custom_call_target="tpu_custom_call" | custom-call | flops 380633088 | bytes 2523136 | tf_op jit(solution)/shard_map/pallas_call | solution.py:283
  84.9 21.7 %shard_map.112 = (bf16[192,352]{1,0:T(8,128)(2,1)}, bf16[480,352]{1,0:T(8,128)(2,1)}) custom-call(bf16[480,352]{1,0:T(8,128)(2,1)} %get-tuple-element.24.padded_ref, bf16[4,480,352]{2,1,0:T(8,128)(2,1)} %bitcast.22, bf16[1408,352]{1,0:T(8,128)(2,1)} %bitcast.29, bf16[1408,352]{1,0:T(8,128)(2,1)} %bitcast.36, bf16[1,1408]{1,0:T(2,128)(2,1)} %bias_in_ref.13, ...), custom_call_target="tpu_custom_call" | custom-call | flops 380633088 | bytes 2523136 | tf_op jit(solution)/shard_map/pallas_call | solution.py:283
  106.7 18.9 %shard_map.113 = (bf16[192,352]{1,0:T(8,128)(2,1)}, bf16[480,352]{1,0:T(8,128)(2,1)}) custom-call(bf16[480,352]{1,0:T(8,128)(2,1)} %get-tuple-element.26.padded_ref, bf16[4,480,352]{2,1,0:T(8,128)(2,1)} %bitcast.23, bf16[1408,352]{1,0:T(8,128)(2,1)} %bitcast.30, bf16[1408,352]{1,0:T(8,128)(2,1)} %bitcast.37, bf16[1,1408]{1,0:T(2,128)(2,1)} %bias_in_ref.13, ...), custom_call_target="tpu_custom_call" | custom-call | flops 380633088 | bytes 2523136 | tf_op jit(solution)/shard_map/pallas_call | solution.py:283
  125.5 19.3 %shard_map.114 = (bf16[192,352]{1,0:T(8,128)(2,1)}, bf16[480,352]{1,0:T(8,128)(2,1)}) custom-call(bf16[480,352]{1,0:T(8,128)(2,1)} %get-tuple-element.28.padded_ref, bf16[4,480,352]{2,1,0:T(8,128)(2,1)} %bitcast.24, bf16[1408,352]{1,0:T(8,128)(2,1)} %bitcast.31, bf16[1408,352]{1,0:T(8,128)(2,1)} %bitcast.38, bf16[1,1408]{1,0:T(2,128)(2,1)} %bias_in_ref.13, ...), custom_call_target="tpu_custom_call" | custom-call | flops 380633088 | bytes 2523136 | tf_op jit(solution)/shard_map/pallas_call | solution.py:283
  144.9 19.0 %shard_map.115 = (bf16[192,352]{1,0:T(8,128)(2,1)}, bf16[480,352]{1,0:T(8,128)(2,1)}) custom-call(bf16[480,352]{1,0:T(8,128)(2,1)} %get-tuple-element.30.padded_ref, bf16[4,480,352]{2,1,0:T(8,128)(2,1)} %bitcast.25, bf16[1408,352]{1,0:T(8,128)(2,1)} %bitcast.32, bf16[1408,352]{1,0:T(8,128)(2,1)} %bitcast.39, bf16[1,1408]{1,0:T(2,128)(2,1)} %bias_in_ref.13, ...), custom_call_target="tpu_custom_call" | custom-call | flops 380633088 | bytes 2523136 | tf_op jit(solution)/shard_map/pallas_call | solution.py:283
  163.9 13.4 %shard_map.116 = bf16[192,352]{1,0:T(8,128)(2,1)} custom-call(bf16[480,352]{1,0:T(8,128)(2,1)} %get-tuple-element.32.padded_ref, bf16[4,480,352]{2,1,0:T(8,128)(2,1)} %bitcast.26, bf16[1408,352]{1,0:T(8,128)(2,1)} %bitcast.33, bf16[1408,352]{1,0:T(8,128)(2,1)} %bitcast.40, bf16[1,1408]{1,0:T(2,128)(2,1)} %bias_in_ref.13, bf16[1,1408]{1,0:T(2,128)(2,1)} %gamma_ref.13, ...), custom_call_target="tpu_custom_call" | custom-call | flops 380633088 | bytes 2523136 | tf_op jit(solution)/shard_map/pallas_call | solution.py:283
  177.3 0.0 copy-start.8
  177.4 0.0 copy-start.2
  177.4 0.0 copy-done.3
  177.4 0.0 copy-done.4
  177.4 0.0 copy-done.5
  177.6 0.7 copy-done.8
  178.3 0.0 copy-done.2
  178.4 0.9 dynamic-slice_bitcast_fusion
  (17 shorter events, 0.2 us)
Async XLA Ops:
  0.0 33.4 %copy-start.1 = (bf16[4,1,4,48,352]{4,3,2,1,0:T(8,128)(2,1)S(1)}, bf16[4,1,4,48,352]{4,3,2,1,0:T(8,128)(2,1)}, u32[]{:S(2)}) copy-start(bf16[4,1,4,48,352]{4,3,2,1,0:T(8,128)(2,1)} %param.11) | copy-start | bytes 1622020
  0.0 7.8 %copy-start.11 = (bf16[1,7,7,352]{3,2,1,0:T(8,128)(2,1)S(1)}, bf16[1,7,7,352]{3,2,1,0:T(8,128)(2,1)}, u32[]{:S(2)}) copy-start(bf16[1,7,7,352]{3,2,1,0:T(8,128)(2,1)} %param.12) | copy-start | bytes 103492
  0.0 8.5 %copy-start.10 = (bf16[1,176,352]{2,1,0:T(8,128)(2,1)S(1)}, bf16[1,176,352]{2,1,0:T(8,128)(2,1)}, u32[]{:S(2)}) copy-start(bf16[1,176,352]{2,1,0:T(8,128)(2,1)} %param.20) | copy-start | bytes 371716
  0.0 8.5 %copy-start.9 = (bf16[1,352,176]{1,2,0:T(8,128)(2,1)S(1)}, bf16[1,352,176]{1,2,0:T(8,128)(2,1)}, u32[]{:S(2)}) copy-start(bf16[1,352,176]{1,2,0:T(8,128)(2,1)} %param.16) | copy-start | bytes 371716
  1.3 32.0 %collective-permute-start = (bf16[4,3,48,352]{3,2,1,0:T(8,128)(2,1)S(1)}, bf16[4,3,48,352]{3,2,1,0:T(8,128)(2,1)S(1)}, u32[]{:S(2)}, u32[]{:S(2)}) collective-permute-start(bf16[4,3,48,352]{3,2,1,0:T(8,128)(2,1)S(1)} %get-tuple-element.33), channel_id=1, source_target_pairs={{0,8},{8,16},{16,24},{24,32},{32,40},{40,48},{48,56},{56,64},{64,7... | collective-permute-start | bytes 1216520 | tf_op jit(solution)/shard_map/ppermute | solution.py:25
  5.9 27.5 %collective-permute-start.1 = (bf16[4,3,48,352]{3,2,1,0:T(8,128)(2,1)S(1)}, bf16[4,3,48,352]{3,2,1,0:T(8,128)(2,1)S(1)}, u32[]{:S(2)}, u32[]{:S(2)}) collective-permute-start(bf16[4,3,48,352]{3,2,1,0:T(8,128)(2,1)S(1)} %get-tuple-element.34), channel_id=1, source_target_pairs={{8,0},{16,8},{24,16},{32,24},{40,32},{48,40},{56,48},{64,56},{72,6... | collective-permute-start | bytes 1216520 | tf_op jit(solution)/shard_map/ppermute | solution.py:27
  33.7 1.3 copy-start
  163.8 13.5 %copy-start.3 = (bf16[192,352]{1,0:T(8,128)(2,1)S(1)}, bf16[192,352]{1,0:T(8,128)(2,1)}, u32[]{:S(2)}) copy-start(bf16[192,352]{1,0:T(8,128)(2,1)} %get-tuple-element.21) | copy-start | bytes 405508
  163.9 13.5 %copy-start.4 = (bf16[192,352]{1,0:T(8,128)(2,1)S(1)}, bf16[192,352]{1,0:T(8,128)(2,1)}, u32[]{:S(2)}) copy-start(bf16[192,352]{1,0:T(8,128)(2,1)} %get-tuple-element.23) | copy-start | bytes 405508
  163.9 13.6 %copy-start.5 = (bf16[192,352]{1,0:T(8,128)(2,1)S(1)}, bf16[192,352]{1,0:T(8,128)(2,1)}, u32[]{:S(2)}) copy-start(bf16[192,352]{1,0:T(8,128)(2,1)} %get-tuple-element.25) | copy-start | bytes 405508
  163.9 13.6 %copy-start.6 = (bf16[192,352]{1,0:T(8,128)(2,1)S(1)}, bf16[192,352]{1,0:T(8,128)(2,1)}, u32[]{:S(2)}) copy-start(bf16[192,352]{1,0:T(8,128)(2,1)} %get-tuple-element.27) | copy-start | bytes 405508
  163.9 13.6 %copy-start.7 = (bf16[192,352]{1,0:T(8,128)(2,1)S(1)}, bf16[192,352]{1,0:T(8,128)(2,1)}, u32[]{:S(2)}) copy-start(bf16[192,352]{1,0:T(8,128)(2,1)} %get-tuple-element.29) | copy-start | bytes 405508
  177.3 0.9 copy-start.8
  177.4 1.0 copy-start.2

commit v4 on v3

--- a/solution.py
+++ b/solution.py
@@ -52,10 +52,10 @@
     *rest,
 ):
     if hand_on:
-        next_ref, wide_ref, normed_ref, act_ref, slots, send_sem, recv_sem = rest[:7]
-        hand_send, hand_recv, fresh_sem = rest[7:]
+        next_ref, wide_ref, conv_ref, normed_ref, act_ref, slots, send_sem, recv_sem = rest[:8]
+        hand_send, hand_recv, fresh_sem = rest[8:]
     else:
-        wide_ref, normed_ref, act_ref, slots, send_sem, recv_sem = rest
+        wide_ref, conv_ref, normed_ref, act_ref, slots, send_sem, recv_sem = rest
     me = lax.axis_index("row")
     section = lax.axis_index("section")
     barrier = pltpu.get_barrier_semaphore()
@@ -87,12 +87,27 @@
         wide_ref[r, pl.ds(8, cols), :] = padded_ref[pl.ds(r * cols, cols), :].astype(jnp.float32)
         wide_ref[r, pl.ds(8 + cols, margin_cols - 8 - cols), :] = zeros[: margin_cols - 8 - cols]
 
-    def conv_row(h, carry):
-        acc = jnp.broadcast_to(depth_bias_ref[...].astype(jnp.float32), (cols, channels))
-        for i in range(7):
+    for start in range(0, channels, 128):
+        lanes = pl.ds(start, min(128, channels - start))
+        acc = [
+            jnp.broadcast_to(
+                depth_bias_ref[:, lanes].astype(jnp.float32), (cols, min(128, channels - start))
+            )
+            for h in range(out_rows)
+        ]
+        for r in range(padded_rows):
             for j in range(7):
-                tap = taps_ref[pl.ds(i * 7 + j, 1), :].astype(jnp.float32)
-                acc = acc + wide_ref[h + i, pl.ds(j + 5, cols), :] * tap
+                slab = wide_ref[r, pl.ds(j + 5, cols), lanes]
+                for h in range(out_rows):
+                    i = r - h
+                    if 0 <= i < 7:
+                        tap = taps_ref[pl.ds(i * 7 + j, 1), lanes].astype(jnp.float32)
+                        acc[h] = acc[h] + slab * tap
+        for h in range(out_rows):
+            conv_ref[h, :, lanes] = acc[h]
+
+    def norm_row(h, carry):
+        acc = conv_ref[h]
         mean = jnp.mean(acc, axis=-1, keepdims=True)
         center = acc - mean
         spread = jnp.mean(center * center, axis=-1, keepdims=True)
@@ -103,7 +118,7 @@
         normed_ref[pl.ds(pl.multiple_of(h * cols, 16), cols), :] = normed.astype(normed_ref.dtype)
         return carry
 
-    lax.fori_loop(0, out_rows, conv_row, 0)
+    lax.fori_loop(0, out_rows, norm_row, 0)
     first_core = lax.rem(me, 2) == 0
 
     def raise_with(proj_in_t_ref):
@@ -267,6 +282,7 @@
     out_shape = [jax.ShapeDtypeStruct((cells, channels), padded.dtype)]
     scratch = [
         pltpu.VMEM((padded_rows, -(-(cols + 11) // 8) * 8, channels), jnp.float32),
+        pltpu.VMEM((padded_rows - 6, cols, channels), jnp.float32),
         pltpu.VMEM((cells, channels), jnp.bfloat16),
         pltpu.VMEM((cells, hidden_units), jnp.bfloat16),
         pltpu.VMEM((n, 1, hidden_units), jnp.float32),

time: 180 us -> 178 us (0.989)
    pallas_call x7, Pallas kernels: 142 us -> 140 us  [pointwise(): pl.pallas_call(functools.partial(_pointwise_kernel, n, sections, hand_on,...]
  transfers between devices with their start and end apart: 2 -> 2, of which waited for: 0 -> 0; matrix products, arithmetic and copies ran while one was open for 1% -> 1% of each run, Pallas kernels for 13% -> 14%
where the time goes in v4:
time: 178 us; the launch traced here: 177 us
  Pallas kernels  165 us (93%)
  starting transfers between devices  6.48 us (4%)
  local copies, waits for them, and re-layouts  5.05 us (3%)
    pallas_call x7, Pallas kernels, pointwise(): pl.pallas_call(functools.partial(_pointwise_kernel, n, sections, hand_on,...  140 us
    pallas_call x1, Pallas kernels, gathered_weights(): pl.pallas_call(functools.partial(_gather_kernel, n, (pl.ds(0, 96), pl.ds(...  24.2 us
    ppermute x1, starting transfers between devices, extended(): lax.ppermute(tail, axis, [(i, (i + 1) % count) for i in range(ends)])  4.56 us
  transfers between devices with their start and end apart: 2, of which 0 were waited for; matrix products, arithmetic and copies ran while one was open for 1% of the time, Pallas kernels for 14%

profile of v4, /device:TPU:7, one launch (start us, length us, event | category | flops | bytes accessed | tf_op | source)
XLA Modules:
  0.0 177.4 jit_solution(10468680792757391067)
XLA Ops:
  0.0 0.0 copy-start.9
  0.0 1.3 fusion
  1.3 4.6 %collective-permute-start = (bf16[4,3,48,352]{3,2,1,0:T(8,128)(2,1)S(1)}, bf16[4,3,48,352]{3,2,1,0:T(8,128)(2,1)S(1)}, u32[]{:S(2)}, u32[]{:S(2)}) collective-permute-start(bf16[4,3,48,352]{3,2,1,0:T(8,128)(2,1)S(1)} %get-tuple-element.33), channel_id=1, source_target_pairs={{0,8},{8,16},{16,24},{24,32},{32,40},{40,48},{48,56},{56,64},{64,7... | collective-permute-start | bytes 1216520 | tf_op jit(solution)/shard_map/ppermute | solution.py:25
  5.9 1.9 %collective-permute-start.1 = (bf16[4,3,48,352]{3,2,1,0:T(8,128)(2,1)S(1)}, bf16[4,3,48,352]{3,2,1,0:T(8,128)(2,1)S(1)}, u32[]{:S(2)}, u32[]{:S(2)}) collective-permute-start(bf16[4,3,48,352]{3,2,1,0:T(8,128)(2,1)S(1)} %get-tuple-element.34), channel_id=1, source_target_pairs={{8,0},{16,8},{24,16},{32,24},{40,32},{48,40},{56,48},{64,56},{72,6... | collective-permute-start | bytes 1216520 | tf_op jit(solution)/shard_map/ppermute | solution.py:27
  7.9 0.6 reshape_squeeze.2.taps_ref
  8.5 0.0 copy-done.9
  8.5 0.7 bitcast_select_fusion.mine_ref
  9.2 24.2 %shard_map.109 = (bf16[8,176,352]{2,1,0:T(8,128)(2,1)}, bf16[8,176,352]{2,1,0:T(8,128)(2,1)}) custom-call(bf16[176,352]{1,0:T(8,128)(2,1)} %bitcast_select_fusion.mine_ref), custom_call_target="tpu_custom_call" | custom-call | tf_op jit(solution)/shard_map/pallas_call | solution.py:452
  33.4 0.0 collective-permute-done
  33.4 0.0 collective-permute-done.1
  33.4 0.3 pad_maximum_fusion
  33.7 0.8 slice.14
  34.5 0.4 copy-done
  35.0 28.1 %shard_map.110 = (bf16[192,352]{1,0:T(8,128)(2,1)}, bf16[480,352]{1,0:T(8,128)(2,1)}) custom-call(bf16[480,352]{1,0:T(8,128)(2,1)} %bitcast.43, bf16[4,480,352]{2,1,0:T(8,128)(2,1)} %bitcast.20, bf16[1408,352]{1,0:T(8,128)(2,1)} %bitcast.27, bf16[1408,352]{1,0:T(8,128)(2,1)} %bitcast.34, bf16[1,1408]{1,0:T(2,128)(2,1)} %bias_in_ref.13, ...), custom_call_target="tpu_custom_call" | custom-call | flops 380633088 | bytes 2523136 | tf_op jit(solution)/shard_map/pallas_call | solution.py:299
  63.0 20.9 %shard_map.111 = (bf16[192,352]{1,0:T(8,128)(2,1)}, bf16[480,352]{1,0:T(8,128)(2,1)}) custom-call(bf16[480,352]{1,0:T(8,128)(2,1)} %get-tuple-element.22.padded_ref, bf16[4,480,352]{2,1,0:T(8,128)(2,1)} %bitcast.21, bf16[1408,352]{1,0:T(8,128)(2,1)} %bitcast.28, bf16[1408,352]{1,0:T(8,128)(2,1)} %bitcast.35, bf16[1,1408]{1,0:T(2,128)(2,1)} %bias_in_ref.13, ...), custom_call_target="tpu_custom_call" | custom-call | flops 380633088 | bytes 2523136 | tf_op jit(solution)/shard_map/pallas_call | solution.py:299
  84.0 21.1 %shard_map.112 = (bf16[192,352]{1,0:T(8,128)(2,1)}, bf16[480,352]{1,0:T(8,128)(2,1)}) custom-call(bf16[480,352]{1,0:T(8,128)(2,1)} %get-tuple-element.24.padded_ref, bf16[4,480,352]{2,1,0:T(8,128)(2,1)} %bitcast.22, bf16[1408,352]{1,0:T(8,128)(2,1)} %bitcast.29, bf16[1408,352]{1,0:T(8,128)(2,1)} %bitcast.36, bf16[1,1408]{1,0:T(2,128)(2,1)} %bias_in_ref.13, ...), custom_call_target="tpu_custom_call" | custom-call | flops 380633088 | bytes 2523136 | tf_op jit(solution)/shard_map/pallas_call | solution.py:299
  105.1 18.6 %shard_map.113 = (bf16[192,352]{1,0:T(8,128)(2,1)}, bf16[480,352]{1,0:T(8,128)(2,1)}) custom-call(bf16[480,352]{1,0:T(8,128)(2,1)} %get-tuple-element.26.padded_ref, bf16[4,480,352]{2,1,0:T(8,128)(2,1)} %bitcast.23, bf16[1408,352]{1,0:T(8,128)(2,1)} %bitcast.30, bf16[1408,352]{1,0:T(8,128)(2,1)} %bitcast.37, bf16[1,1408]{1,0:T(2,128)(2,1)} %bias_in_ref.13, ...), custom_call_target="tpu_custom_call" | custom-call | flops 380633088 | bytes 2523136 | tf_op jit(solution)/shard_map/pallas_call | solution.py:299
  123.7 20.0 %shard_map.114 = (bf16[192,352]{1,0:T(8,128)(2,1)}, bf16[480,352]{1,0:T(8,128)(2,1)}) custom-call(bf16[480,352]{1,0:T(8,128)(2,1)} %get-tuple-element.28.padded_ref, bf16[4,480,352]{2,1,0:T(8,128)(2,1)} %bitcast.24, bf16[1408,352]{1,0:T(8,128)(2,1)} %bitcast.31, bf16[1408,352]{1,0:T(8,128)(2,1)} %bitcast.38, bf16[1,1408]{1,0:T(2,128)(2,1)} %bias_in_ref.13, ...), custom_call_target="tpu_custom_call" | custom-call | flops 380633088 | bytes 2523136 | tf_op jit(solution)/shard_map/pallas_call | solution.py:299
  143.7 18.8 %shard_map.115 = (bf16[192,352]{1,0:T(8,128)(2,1)}, bf16[480,352]{1,0:T(8,128)(2,1)}) custom-call(bf16[480,352]{1,0:T(8,128)(2,1)} %get-tuple-element.30.padded_ref, bf16[4,480,352]{2,1,0:T(8,128)(2,1)} %bitcast.25, bf16[1408,352]{1,0:T(8,128)(2,1)} %bitcast.32, bf16[1408,352]{1,0:T(8,128)(2,1)} %bitcast.39, bf16[1,1408]{1,0:T(2,128)(2,1)} %bias_in_ref.13, ...), custom_call_target="tpu_custom_call" | custom-call | flops 380633088 | bytes 2523136 | tf_op jit(solution)/shard_map/pallas_call | solution.py:299
  162.5 0.0 copy-start.3
  162.5 0.0 copy-start.4
  162.5 0.0 copy-start.5
  162.5 0.0 copy-start.6
  162.5 0.0 copy-start.7
  162.6 12.9 %shard_map.116 = bf16[192,352]{1,0:T(8,128)(2,1)} custom-call(bf16[480,352]{1,0:T(8,128)(2,1)} %get-tuple-element.32.padded_ref, bf16[4,480,352]{2,1,0:T(8,128)(2,1)} %bitcast.26, bf16[1408,352]{1,0:T(8,128)(2,1)} %bitcast.33, bf16[1408,352]{1,0:T(8,128)(2,1)} %bitcast.40, bf16[1,1408]{1,0:T(2,128)(2,1)} %bias_in_ref.13, bf16[1,1408]{1,0:T(2,128)(2,1)} %gamma_ref.13, ...), custom_call_target="tpu_custom_call" | custom-call | flops 380633088 | bytes 2523136 | tf_op jit(solution)/shard_map/pallas_call | solution.py:299
  175.5 0.0 copy-start.8
  175.5 0.0 copy-start.2
  175.5 0.0 copy-done.3
  175.5 0.0 copy-done.4
  175.7 0.7 copy-done.8
  176.4 0.0 copy-done.2
  176.5 0.9 dynamic-slice_bitcast_fusion
  (17 shorter events, 0.2 us)
Async XLA Ops:
  0.0 33.4 %copy-start.1 = (bf16[4,1,4,48,352]{4,3,2,1,0:T(8,128)(2,1)S(1)}, bf16[4,1,4,48,352]{4,3,2,1,0:T(8,128)(2,1)}, u32[]{:S(2)}) copy-start(bf16[4,1,4,48,352]{4,3,2,1,0:T(8,128)(2,1)} %param.11) | copy-start | bytes 1622020
  0.0 7.8 %copy-start.11 = (bf16[1,7,7,352]{3,2,1,0:T(8,128)(2,1)S(1)}, bf16[1,7,7,352]{3,2,1,0:T(8,128)(2,1)}, u32[]{:S(2)}) copy-start(bf16[1,7,7,352]{3,2,1,0:T(8,128)(2,1)} %param.12) | copy-start | bytes 103492
  0.0 8.5 %copy-start.10 = (bf16[1,176,352]{2,1,0:T(8,128)(2,1)S(1)}, bf16[1,176,352]{2,1,0:T(8,128)(2,1)}, u32[]{:S(2)}) copy-start(bf16[1,176,352]{2,1,0:T(8,128)(2,1)} %param.20) | copy-start | bytes 371716
  0.0 8.5 %copy-start.9 = (bf16[1,352,176]{1,2,0:T(8,128)(2,1)S(1)}, bf16[1,352,176]{1,2,0:T(8,128)(2,1)}, u32[]{:S(2)}) copy-start(bf16[1,352,176]{1,2,0:T(8,128)(2,1)} %param.16) | copy-start | bytes 371716
  1.3 32.0 %collective-permute-start = (bf16[4,3,48,352]{3,2,1,0:T(8,128)(2,1)S(1)}, bf16[4,3,48,352]{3,2,1,0:T(8,128)(2,1)S(1)}, u32[]{:S(2)}, u32[]{:S(2)}) collective-permute-start(bf16[4,3,48,352]{3,2,1,0:T(8,128)(2,1)S(1)} %get-tuple-element.33), channel_id=1, source_target_pairs={{0,8},{8,16},{16,24},{24,32},{32,40},{40,48},{48,56},{56,64},{64,7... | collective-permute-start | bytes 1216520 | tf_op jit(solution)/shard_map/ppermute | solution.py:25
  5.9 27.5 %collective-permute-start.1 = (bf16[4,3,48,352]{3,2,1,0:T(8,128)(2,1)S(1)}, bf16[4,3,48,352]{3,2,1,0:T(8,128)(2,1)S(1)}, u32[]{:S(2)}, u32[]{:S(2)}) collective-permute-start(bf16[4,3,48,352]{3,2,1,0:T(8,128)(2,1)S(1)} %get-tuple-element.34), channel_id=1, source_target_pairs={{8,0},{16,8},{24,16},{32,24},{40,32},{48,40},{56,48},{64,56},{72,6... | collective-permute-start | bytes 1216520 | tf_op jit(solution)/shard_map/ppermute | solution.py:27
  33.7 1.3 copy-start
  162.5 13.0 %copy-start.3 = (bf16[192,352]{1,0:T(8,128)(2,1)S(1)}, bf16[192,352]{1,0:T(8,128)(2,1)}, u32[]{:S(2)}) copy-start(bf16[192,352]{1,0:T(8,128)(2,1)} %get-tuple-element.21) | copy-start | bytes 405508
  162.5 13.0 %copy-start.4 = (bf16[192,352]{1,0:T(8,128)(2,1)S(1)}, bf16[192,352]{1,0:T(8,128)(2,1)}, u32[]{:S(2)}) copy-start(bf16[192,352]{1,0:T(8,128)(2,1)} %get-tuple-element.23) | copy-start | bytes 405508
  162.5 13.0 %copy-start.5 = (bf16[192,352]{1,0:T(8,128)(2,1)S(1)}, bf16[192,352]{1,0:T(8,128)(2,1)}, u32[]{:S(2)}) copy-start(bf16[192,352]{1,0:T(8,128)(2,1)} %get-tuple-element.25) | copy-start | bytes 405508
  162.5 13.1 %copy-start.6 = (bf16[192,352]{1,0:T(8,128)(2,1)S(1)}, bf16[192,352]{1,0:T(8,128)(2,1)}, u32[]{:S(2)}) copy-start(bf16[192,352]{1,0:T(8,128)(2,1)} %get-tuple-element.27) | copy-start | bytes 405508
  162.5 13.1 %copy-start.7 = (bf16[192,352]{1,0:T(8,128)(2,1)S(1)}, bf16[192,352]{1,0:T(8,128)(2,1)}, u32[]{:S(2)}) copy-start(bf16[192,352]{1,0:T(8,128)(2,1)} %get-tuple-element.29) | copy-start | bytes 405508
  175.5 0.9 copy-start.8
  175.5 1.0 copy-start.2

commit v5 on v4

--- a/solution.py
+++ b/solution.py
@@ -138,7 +138,7 @@
     slots[me] = jnp.sum(grouped * grouped, axis=0, keepdims=True)
     pl.semaphore_wait(barrier, waits)
     sends = []
-    for k in range(1, n):
+    for k in sorted(range(1, n), key=lambda k: -min(k, n - k)):
         copy = pltpu.make_async_remote_copy(
             src_ref=slots.at[me],
             dst_ref=slots.at[me],
@@ -176,8 +176,6 @@
             device_id={"row": src},
             device_id_type=MESH,
         ).wait_recv()
-    for copy in sends:
-        copy.wait_send()
     total_sq = slots[0]
     for j in range(1, n):
         total_sq = total_sq + slots[j]
@@ -202,6 +200,8 @@
     pl.when(first_core)(lambda: lower_with(other_ref))
     pl.when(jnp.logical_not(first_core))(lambda: lower_with(held_ref))
     if not hand_on:
+        for copy in sends:
+            copy.wait_send()
         return
     own_rows = pl.ds(edge, cells)
     handed = pltpu.make_async_remote_copy(
@@ -253,6 +253,9 @@
     @pl.when(has_next)
     def _():
         handed.wait_send()
+
+    for copy in sends:
+        copy.wait_send()
 
 
 def pointwise(

time: 178 us -> 176 us (0.989)
  Pallas kernels: 165 us -> 162 us
    pallas_call x7, Pallas kernels: 140 us -> 138 us  [pointwise(): pl.pallas_call(functools.partial(_pointwise_kernel, n, sections, hand_on,...]
where the time goes in v5:
time: 176 us; the launch traced here: 175 us
  Pallas kernels  162 us (92%)
  starting transfers between devices  6.48 us (4%)
  local copies, waits for them, and re-layouts  5.05 us (3%)
    pallas_call x7, Pallas kernels, pointwise(): pl.pallas_call(functools.partial(_pointwise_kernel, n, sections, hand_on,...  138 us
    pallas_call x1, Pallas kernels, gathered_weights(): pl.pallas_call(functools.partial(_gather_kernel, n, (pl.ds(0, 96), pl.ds(...  24.2 us
    ppermute x1, starting transfers between devices, extended(): lax.ppermute(tail, axis, [(i, (i + 1) % count) for i in range(ends)])  4.56 us
  transfers between devices with their start and end apart: 2, of which 0 were waited for; matrix products, arithmetic and copies ran while one was open for 1% of the time, Pallas kernels for 14%

profile of v5, /device:TPU:7, one launch (start us, length us, event | category | flops | bytes accessed | tf_op | source)
XLA Modules:
  0.0 175.1 jit_solution(5096090829207070813)
XLA Ops:
  0.0 0.0 copy-start.9
  0.0 1.3 fusion
  1.3 4.6 %collective-permute-start = (bf16[4,3,48,352]{3,2,1,0:T(8,128)(2,1)S(1)}, bf16[4,3,48,352]{3,2,1,0:T(8,128)(2,1)S(1)}, u32[]{:S(2)}, u32[]{:S(2)}) collective-permute-start(bf16[4,3,48,352]{3,2,1,0:T(8,128)(2,1)S(1)} %get-tuple-element.33), channel_id=1, source_target_pairs={{0,8},{8,16},{16,24},{24,32},{32,40},{40,48},{48,56},{56,64},{64,7... | collective-permute-start | bytes 1216520 | tf_op jit(solution)/shard_map/ppermute | solution.py:25
  5.9 1.9 %collective-permute-start.1 = (bf16[4,3,48,352]{3,2,1,0:T(8,128)(2,1)S(1)}, bf16[4,3,48,352]{3,2,1,0:T(8,128)(2,1)S(1)}, u32[]{:S(2)}, u32[]{:S(2)}) collective-permute-start(bf16[4,3,48,352]{3,2,1,0:T(8,128)(2,1)S(1)} %get-tuple-element.34), channel_id=1, source_target_pairs={{8,0},{16,8},{24,16},{32,24},{40,32},{48,40},{56,48},{64,56},{72,6... | collective-permute-start | bytes 1216520 | tf_op jit(solution)/shard_map/ppermute | solution.py:27
  7.8 0.0 copy-done.11
  7.9 0.6 reshape_squeeze.2.taps_ref
  8.5 0.0 copy-done.10
  8.5 0.0 copy-done.9
  8.5 0.7 bitcast_select_fusion.mine_ref
  9.2 24.2 %shard_map.109 = (bf16[8,176,352]{2,1,0:T(8,128)(2,1)}, bf16[8,176,352]{2,1,0:T(8,128)(2,1)}) custom-call(bf16[176,352]{1,0:T(8,128)(2,1)} %bitcast_select_fusion.mine_ref), custom_call_target="tpu_custom_call" | custom-call | tf_op jit(solution)/shard_map/pallas_call | solution.py:455
  33.4 0.0 collective-permute-done
  33.4 0.0 collective-permute-done.1
  33.4 0.0 copy-done.1
  33.4 0.3 pad_maximum_fusion
  33.7 0.0 copy-start
  33.7 0.8 slice.14
  34.5 0.4 copy-done
  35.0 27.7 %shard_map.110 = (bf16[192,352]{1,0:T(8,128)(2,1)}, bf16[480,352]{1,0:T(8,128)(2,1)}) custom-call(bf16[480,352]{1,0:T(8,128)(2,1)} %bitcast.43, bf16[4,480,352]{2,1,0:T(8,128)(2,1)} %bitcast.20, bf16[1408,352]{1,0:T(8,128)(2,1)} %bitcast.27, bf16[1408,352]{1,0:T(8,128)(2,1)} %bitcast.34, bf16[1,1408]{1,0:T(2,128)(2,1)} %bias_in_ref.13, ...), custom_call_target="tpu_custom_call" | custom-call | flops 380633088 | bytes 2523136 | tf_op jit(solution)/shard_map/pallas_call | solution.py:302
  62.7 21.4 %shard_map.111 = (bf16[192,352]{1,0:T(8,128)(2,1)}, bf16[480,352]{1,0:T(8,128)(2,1)}) custom-call(bf16[480,352]{1,0:T(8,128)(2,1)} %get-tuple-element.22.padded_ref, bf16[4,480,352]{2,1,0:T(8,128)(2,1)} %bitcast.21, bf16[1408,352]{1,0:T(8,128)(2,1)} %bitcast.28, bf16[1408,352]{1,0:T(8,128)(2,1)} %bitcast.35, bf16[1,1408]{1,0:T(2,128)(2,1)} %bias_in_ref.13, ...), custom_call_target="tpu_custom_call" | custom-call | flops 380633088 | bytes 2523136 | tf_op jit(solution)/shard_map/pallas_call | solution.py:302
  84.2 20.6 %shard_map.112 = (bf16[192,352]{1,0:T(8,128)(2,1)}, bf16[480,352]{1,0:T(8,128)(2,1)}) custom-call(bf16[480,352]{1,0:T(8,128)(2,1)} %get-tuple-element.24.padded_ref, bf16[4,480,352]{2,1,0:T(8,128)(2,1)} %bitcast.22, bf16[1408,352]{1,0:T(8,128)(2,1)} %bitcast.29, bf16[1408,352]{1,0:T(8,128)(2,1)} %bitcast.36, bf16[1,1408]{1,0:T(2,128)(2,1)} %bias_in_ref.13, ...), custom_call_target="tpu_custom_call" | custom-call | flops 380633088 | bytes 2523136 | tf_op jit(solution)/shard_map/pallas_call | solution.py:302
  104.8 18.9 %shard_map.113 = (bf16[192,352]{1,0:T(8,128)(2,1)}, bf16[480,352]{1,0:T(8,128)(2,1)}) custom-call(bf16[480,352]{1,0:T(8,128)(2,1)} %get-tuple-element.26.padded_ref, bf16[4,480,352]{2,1,0:T(8,128)(2,1)} %bitcast.23, bf16[1408,352]{1,0:T(8,128)(2,1)} %bitcast.30, bf16[1408,352]{1,0:T(8,128)(2,1)} %bitcast.37, bf16[1,1408]{1,0:T(2,128)(2,1)} %bias_in_ref.13, ...), custom_call_target="tpu_custom_call" | custom-call | flops 380633088 | bytes 2523136 | tf_op jit(solution)/shard_map/pallas_call | solution.py:302
  123.7 18.7 %shard_map.114 = (bf16[192,352]{1,0:T(8,128)(2,1)}, bf16[480,352]{1,0:T(8,128)(2,1)}) custom-call(bf16[480,352]{1,0:T(8,128)(2,1)} %get-tuple-element.28.padded_ref, bf16[4,480,352]{2,1,0:T(8,128)(2,1)} %bitcast.24, bf16[1408,352]{1,0:T(8,128)(2,1)} %bitcast.31, bf16[1408,352]{1,0:T(8,128)(2,1)} %bitcast.38, bf16[1,1408]{1,0:T(2,128)(2,1)} %bias_in_ref.13, ...), custom_call_target="tpu_custom_call" | custom-call | flops 380633088 | bytes 2523136 | tf_op jit(solution)/shard_map/pallas_call | solution.py:302
  142.4 18.5 %shard_map.115 = (bf16[192,352]{1,0:T(8,128)(2,1)}, bf16[480,352]{1,0:T(8,128)(2,1)}) custom-call(bf16[480,352]{1,0:T(8,128)(2,1)} %get-tuple-element.30.padded_ref, bf16[4,480,352]{2,1,0:T(8,128)(2,1)} %bitcast.25, bf16[1408,352]{1,0:T(8,128)(2,1)} %bitcast.32, bf16[1408,352]{1,0:T(8,128)(2,1)} %bitcast.39, bf16[1,1408]{1,0:T(2,128)(2,1)} %bias_in_ref.13, ...), custom_call_target="tpu_custom_call" | custom-call | flops 380633088 | bytes 2523136 | tf_op jit(solution)/shard_map/pallas_call | solution.py:302
  160.9 0.0 copy-start.3
  161.0 12.2 %shard_map.116 = bf16[192,352]{1,0:T(8,128)(2,1)} custom-call(bf16[480,352]{1,0:T(8,128)(2,1)} %get-tuple-element.32.padded_ref, bf16[4,480,352]{2,1,0:T(8,128)(2,1)} %bitcast.26, bf16[1408,352]{1,0:T(8,128)(2,1)} %bitcast.33, bf16[1408,352]{1,0:T(8,128)(2,1)} %bitcast.40, bf16[1,1408]{1,0:T(2,128)(2,1)} %bias_in_ref.13, bf16[1,1408]{1,0:T(2,128)(2,1)} %gamma_ref.13, ...), custom_call_target="tpu_custom_call" | custom-call | flops 380633088 | bytes 2523136 | tf_op jit(solution)/shard_map/pallas_call | solution.py:302
  173.2 0.0 copy-start.8
  173.2 0.0 copy-start.2
  173.2 0.0 copy-done.3
  173.3 0.0 copy-done.5
  173.4 0.7 copy-done.8
  174.1 0.0 copy-done.2
  174.2 0.9 dynamic-slice_bitcast_fusion
  (17 shorter events, 0.2 us)
Async XLA Ops:
  0.0 33.4 %copy-start.1 = (bf16[4,1,4,48,352]{4,3,2,1,0:T(8,128)(2,1)S(1)}, bf16[4,1,4,48,352]{4,3,2,1,0:T(8,128)(2,1)}, u32[]{:S(2)}) copy-start(bf16[4,1,4,48,352]{4,3,2,1,0:T(8,128)(2,1)} %param.11) | copy-start | bytes 1622020
  0.0 7.8 %copy-start.11 = (bf16[1,7,7,352]{3,2,1,0:T(8,128)(2,1)S(1)}, bf16[1,7,7,352]{3,2,1,0:T(8,128)(2,1)}, u32[]{:S(2)}) copy-start(bf16[1,7,7,352]{3,2,1,0:T(8,128)(2,1)} %param.12) | copy-start | bytes 103492
  0.0 8.5 %copy-start.10 = (bf16[1,176,352]{2,1,0:T(8,128)(2,1)S(1)}, bf16[1,176,352]{2,1,0:T(8,128)(2,1)}, u32[]{:S(2)}) copy-start(bf16[1,176,352]{2,1,0:T(8,128)(2,1)} %param.20) | copy-start | bytes 371716
  0.0 8.5 %copy-start.9 = (bf16[1,352,176]{1,2,0:T(8,128)(2,1)S(1)}, bf16[1,352,176]{1,2,0:T(8,128)(2,1)}, u32[]{:S(2)}) copy-start(bf16[1,352,176]{1,2,0:T(8,128)(2,1)} %param.16) | copy-start | bytes 371716
  1.3 32.0 %collective-permute-start = (bf16[4,3,48,352]{3,2,1,0:T(8,128)(2,1)S(1)}, bf16[4,3,48,352]{3,2,1,0:T(8,128)(2,1)S(1)}, u32[]{:S(2)}, u32[]{:S(2)}) collective-permute-start(bf16[4,3,48,352]{3,2,1,0:T(8,128)(2,1)S(1)} %get-tuple-element.33), channel_id=1, source_target_pairs={{0,8},{8,16},{16,24},{24,32},{32,40},{40,48},{48,56},{56,64},{64,7... | collective-permute-start | bytes 1216520 | tf_op jit(solution)/shard_map/ppermute | solution.py:25
  5.9 27.5 %collective-permute-start.1 = (bf16[4,3,48,352]{3,2,1,0:T(8,128)(2,1)S(1)}, bf16[4,3,48,352]{3,2,1,0:T(8,128)(2,1)S(1)}, u32[]{:S(2)}, u32[]{:S(2)}) collective-permute-start(bf16[4,3,48,352]{3,2,1,0:T(8,128)(2,1)S(1)} %get-tuple-element.34), channel_id=1, source_target_pairs={{8,0},{16,8},{24,16},{32,24},{40,32},{48,40},{56,48},{64,56},{72,6... | collective-permute-start | bytes 1216520 | tf_op jit(solution)/shard_map/ppermute | solution.py:27
  33.7 1.3 copy-start
  160.9 12.3 %copy-start.3 = (bf16[192,352]{1,0:T(8,128)(2,1)S(1)}, bf16[192,352]{1,0:T(8,128)(2,1)}, u32[]{:S(2)}) copy-start(bf16[192,352]{1,0:T(8,128)(2,1)} %get-tuple-element.21) | copy-start | bytes 405508
  160.9 12.3 %copy-start.4 = (bf16[192,352]{1,0:T(8,128)(2,1)S(1)}, bf16[192,352]{1,0:T(8,128)(2,1)}, u32[]{:S(2)}) copy-start(bf16[192,352]{1,0:T(8,128)(2,1)} %get-tuple-element.23) | copy-start | bytes 405508
  160.9 12.3 %copy-start.5 = (bf16[192,352]{1,0:T(8,128)(2,1)S(1)}, bf16[192,352]{1,0:T(8,128)(2,1)}, u32[]{:S(2)}) copy-start(bf16[192,352]{1,0:T(8,128)(2,1)} %get-tuple-element.25) | copy-start | bytes 405508
  161.0 12.4 %copy-start.6 = (bf16[192,352]{1,0:T(8,128)(2,1)S(1)}, bf16[192,352]{1,0:T(8,128)(2,1)}, u32[]{:S(2)}) copy-start(bf16[192,352]{1,0:T(8,128)(2,1)} %get-tuple-element.27) | copy-start | bytes 405508
  161.0 12.4 %copy-start.7 = (bf16[192,352]{1,0:T(8,128)(2,1)S(1)}, bf16[192,352]{1,0:T(8,128)(2,1)}, u32[]{:S(2)}) copy-start(bf16[192,352]{1,0:T(8,128)(2,1)} %get-tuple-element.29) | copy-start | bytes 405508
  173.2 0.9 copy-start.8
  173.2 1.0 copy-start.2

commit v6 on v5

--- a/solution.py
+++ b/solution.py
@@ -150,17 +150,16 @@
         copy.start()
         sends.append(copy)
     if hand_on:
-        @pl.when(section == 0)
-        def _():
-            fresh_copy = pltpu.make_async_copy(fresh_ref.at[fresh_index], next_ref, fresh_sem)
-            fresh_copy.start()
-            fresh_copy.wait()
-
-        @pl.when(jnp.logical_and(has_prev, jnp.logical_not(has_above)))
+        fresh_copy = pltpu.make_async_copy(
+            fresh_ref.at[fresh_index], next_ref.at[pl.ds(edge, cells)], fresh_sem
+        )
+        pl.when(section == 0)(fresh_copy.start)
+
+        @pl.when(jnp.logical_not(has_above))
         def _():
             next_ref[pl.ds(0, edge), :] = jnp.zeros((edge, next_ref.shape[1]), next_ref.dtype)
 
-        @pl.when(jnp.logical_and(has_prev, jnp.logical_not(has_below)))
+        @pl.when(jnp.logical_not(has_below))
         def _():
             next_ref[pl.ds(edge + cells, edge), :] = jnp.zeros(
                 (edge, next_ref.shape[1]), next_ref.dtype
@@ -232,23 +231,22 @@
             device_id_type=MESH,
         )
 
-    @pl.when(has_prev)
-    def _():
-        handed.wait_recv()
-        for slot, src, dst, shift, cond in halos:
-            @pl.when(cond)
-            def _():
-                halo_copy(slot, src, dst, me + shift).start()
-
-        for slot, src, dst, shift, cond in halos:
-            @pl.when(halos[slot // 2][4])
-            def _():
-                halo_copy(slot, src, dst, me).wait_recv()
-
-        for slot, src, dst, shift, cond in halos:
-            @pl.when(cond)
-            def _():
-                halo_copy(slot, src, dst, me + shift).wait_send()
+    pl.when(has_prev)(handed.wait_recv)
+    pl.when(section == 0)(fresh_copy.wait)
+    for slot, src, dst, shift, cond in halos:
+        @pl.when(cond)
+        def _():
+            halo_copy(slot, src, dst, me + shift).start()
+
+    for slot, src, dst, shift, cond in halos:
+        @pl.when(halos[slot // 2][4])
+        def _():
+            halo_copy(slot, src, dst, me).wait_recv()
+
+    for slot, src, dst, shift, cond in halos:
+        @pl.when(cond)
+        def _():
+            halo_copy(slot, src, dst, me + shift).wait_send()
 
     @pl.when(has_next)
     def _():
@@ -293,7 +291,7 @@
         pltpu.SemaphoreType.DMA((n,)),
     ]
     if hand_on:
-        out_shape.append(jax.ShapeDtypeStruct(fresh.shape[1:], fresh.dtype))
+        out_shape.append(jax.ShapeDtypeStruct(padded.shape, padded.dtype))
         scratch += [
             pltpu.SemaphoreType.DMA((3,)),
             pltpu.SemaphoreType.DMA((3,)),
@@ -481,7 +479,7 @@
     proj_out,
     bias_out,
 ):
-    fresh = extended(inputs[:, 0], (("row", 1),), 3)
+    fresh = inputs[:, 0]
     proj_in, proj_out = gathered_weights(proj_in[0], proj_out[0])
     sections = lax.axis_size("section")
     section_index = lax.axis_index("section")
@@ -499,7 +497,7 @@
         bias_out[0],
     )
     num_ticks = num_micro + sections - 1
-    current = fresh[:1]
+    current = extended(fresh[:1], (("row", 1),), 3)
     outputs = []
     for tick_index in range(num_ticks):
         hand_on = tick_index + 1 < num_ticks

time: 176 us -> 175 us (level)
  no operation moved by 1% of the time
where the time goes in v6:
time: 175 us
  Pallas kernels  162 us (93%)
  starting transfers between devices  6.48 us (4%)
  local copies, waits for them, and re-layouts  3.48 us (2%)
  other arithmetic  2.46 us (1%)
    pallas_call x7, Pallas kernels, pointwise(): pl.pallas_call(functools.partial(_pointwise_kernel, n, sections, hand_on,...  138 us
    pallas_call x1, Pallas kernels, gathered_weights(): pl.pallas_call(functools.partial(_gather_kernel, n, (pl.ds(0, 96), pl.ds(...  24.2 us
    ppermute x1, starting transfers between devices, extended(): lax.ppermute(tail, axis, [(i, (i + 1) % count) for i in range(ends)])  4.56 us
  transfers between devices with their start and end apart: 2, of which 0 were waited for; matrix products, arithmetic and copies ran while one was open for 1% of the time, Pallas kernels for 14%

profile of v6, /device:TPU:7, one launch (start us, length us, event | category | flops | bytes accessed | tf_op | source)
XLA Modules:
  0.0 174.7 jit_solution(5358810499806055128)
XLA Ops:
  0.0 0.9 slice_bitcast_fusion
  1.0 4.6 %collective-permute-start = (bf16[1,3,48,352]{3,2,1,0:T(8,128)(2,1)S(1)}, bf16[1,3,48,352]{3,2,1,0:T(8,128)(2,1)S(1)}, u32[]{:S(2)}, u32[]{:S(2)}) collective-permute-start(bf16[1,3,48,352]{3,2,1,0:T(8,128)(2,1)S(1)} %get-tuple-element.33), channel_id=1, source_target_pairs={{0,8},{8,16},{16,24},{24,32},{32,40},{40,48},{48,56},{56,64},{64,7... | collective-permute-start | bytes 304136 | tf_op jit(solution)/shard_map/ppermute | solution.py:25
  5.5 1.9 %collective-permute-start.1 = (bf16[1,3,48,352]{3,2,1,0:T(8,128)(2,1)S(1)}, bf16[1,3,48,352]{3,2,1,0:T(8,128)(2,1)S(1)}, u32[]{:S(2)}, u32[]{:S(2)}) collective-permute-start(bf16[1,3,48,352]{3,2,1,0:T(8,128)(2,1)S(1)} %get-tuple-element.34), channel_id=1, source_target_pairs={{8,0},{16,8},{24,16},{32,24},{40,32},{48,40},{56,48},{64,56},{72,6... | collective-permute-start | bytes 304136 | tf_op jit(solution)/shard_map/ppermute | solution.py:27
  7.5 1.6 bitcast_select_fusion.mine_ref
  9.1 0.0 copy-done.7
  9.1 0.6 reshape_squeeze.5.taps_ref
  9.8 24.2 %shard_map.109 = (bf16[8,176,352]{2,1,0:T(8,128)(2,1)}, bf16[8,176,352]{2,1,0:T(8,128)(2,1)}) custom-call(bf16[176,352]{1,0:T(8,128)(2,1)} %bitcast_select_fusion.mine_ref), custom_call_target="tpu_custom_call" | custom-call | tf_op jit(solution)/shard_map/pallas_call | solution.py:453
  34.0 0.0 collective-permute-done
  34.0 0.0 collective-permute-done.1
  34.0 0.8 pad_maximum_fusion
  34.8 27.7 %shard_map.110 = (bf16[192,352]{1,0:T(8,128)(2,1)}, bf16[480,352]{1,0:T(8,128)(2,1)}) custom-call(bf16[480,352]{1,0:T(8,128)(2,1)} %bitcast.42, bf16[4,192,352]{2,1,0:T(8,128)(2,1)} %bitcast.35, bf16[1408,352]{1,0:T(8,128)(2,1)} %bitcast.21, bf16[1408,352]{1,0:T(8,128)(2,1)} %bitcast.28, bf16[1,1408]{1,0:T(2,128)(2,1)} %bias_in_ref.13, ...), custom_call_target="tpu_custom_call" | custom-call | flops 380633088 | bytes 2523136 | tf_op jit(solution)/shard_map/pallas_call | solution.py:300
  62.6 21.4 %shard_map.111 = (bf16[192,352]{1,0:T(8,128)(2,1)}, bf16[480,352]{1,0:T(8,128)(2,1)}) custom-call(bf16[480,352]{1,0:T(8,128)(2,1)} %get-tuple-element.22.padded_ref, bf16[4,192,352]{2,1,0:T(8,128)(2,1)} %bitcast.36, bf16[1408,352]{1,0:T(8,128)(2,1)} %bitcast.22, bf16[1408,352]{1,0:T(8,128)(2,1)} %bitcast.29, bf16[1,1408]{1,0:T(2,128)(2,1)} %bias_in_ref.13, ...), custom_call_target="tpu_custom_call" | custom-call | flops 380633088 | bytes 2523136 | tf_op jit(solution)/shard_map/pallas_call | solution.py:300
  84.0 20.0 %shard_map.112 = (bf16[192,352]{1,0:T(8,128)(2,1)}, bf16[480,352]{1,0:T(8,128)(2,1)}) custom-call(bf16[480,352]{1,0:T(8,128)(2,1)} %get-tuple-element.24.padded_ref, bf16[4,192,352]{2,1,0:T(8,128)(2,1)} %bitcast.37, bf16[1408,352]{1,0:T(8,128)(2,1)} %bitcast.23, bf16[1408,352]{1,0:T(8,128)(2,1)} %bitcast.30, bf16[1,1408]{1,0:T(2,128)(2,1)} %bias_in_ref.13, ...), custom_call_target="tpu_custom_call" | custom-call | flops 380633088 | bytes 2523136 | tf_op jit(solution)/shard_map/pallas_call | solution.py:300
  104.0 19.5 %shard_map.113 = (bf16[192,352]{1,0:T(8,128)(2,1)}, bf16[480,352]{1,0:T(8,128)(2,1)}) custom-call(bf16[480,352]{1,0:T(8,128)(2,1)} %get-tuple-element.26.padded_ref, bf16[4,192,352]{2,1,0:T(8,128)(2,1)} %bitcast.38, bf16[1408,352]{1,0:T(8,128)(2,1)} %bitcast.24, bf16[1408,352]{1,0:T(8,128)(2,1)} %bitcast.31, bf16[1,1408]{1,0:T(2,128)(2,1)} %bias_in_ref.13, ...), custom_call_target="tpu_custom_call" | custom-call | flops 380633088 | bytes 2523136 | tf_op jit(solution)/shard_map/pallas_call | solution.py:300
  123.5 18.2 %shard_map.114 = (bf16[192,352]{1,0:T(8,128)(2,1)}, bf16[480,352]{1,0:T(8,128)(2,1)}) custom-call(bf16[480,352]{1,0:T(8,128)(2,1)} %get-tuple-element.28.padded_ref, bf16[4,192,352]{2,1,0:T(8,128)(2,1)} %bitcast.39, bf16[1408,352]{1,0:T(8,128)(2,1)} %bitcast.25, bf16[1408,352]{1,0:T(8,128)(2,1)} %bitcast.32, bf16[1,1408]{1,0:T(2,128)(2,1)} %bias_in_ref.13, ...), custom_call_target="tpu_custom_call" | custom-call | flops 380633088 | bytes 2523136 | tf_op jit(solution)/shard_map/pallas_call | solution.py:300
  141.7 18.9 %shard_map.115 = (bf16[192,352]{1,0:T(8,128)(2,1)}, bf16[480,352]{1,0:T(8,128)(2,1)}) custom-call(bf16[480,352]{1,0:T(8,128)(2,1)} %get-tuple-element.30.padded_ref, bf16[4,192,352]{2,1,0:T(8,128)(2,1)} %bitcast.40, bf16[1408,352]{1,0:T(8,128)(2,1)} %bitcast.26, bf16[1408,352]{1,0:T(8,128)(2,1)} %bitcast.33, bf16[1,1408]{1,0:T(2,128)(2,1)} %bias_in_ref.13, ...), custom_call_target="tpu_custom_call" | custom-call | flops 380633088 | bytes 2523136 | tf_op jit(solution)/shard_map/pallas_call | solution.py:300
  160.6 0.0 copy-start.1
  160.6 0.0 copy-start.2
  160.6 0.0 copy-start.3
  160.6 0.0 copy-start.4
  160.6 12.1 %shard_map.116 = bf16[192,352]{1,0:T(8,128)(2,1)} custom-call(bf16[480,352]{1,0:T(8,128)(2,1)} %get-tuple-element.32.padded_ref, bf16[4,192,352]{2,1,0:T(8,128)(2,1)} %bitcast.41, bf16[1408,352]{1,0:T(8,128)(2,1)} %bitcast.27, bf16[1408,352]{1,0:T(8,128)(2,1)} %bitcast.34, bf16[1,1408]{1,0:T(2,128)(2,1)} %bias_in_ref.13, bf16[1,1408]{1,0:T(2,128)(2,1)} %gamma_ref.13, ...), custom_call_target="tpu_custom_call" | custom-call | flops 380633088 | bytes 2523136 | tf_op jit(solution)/shard_map/pallas_call | solution.py:300
  172.7 0.0 copy-start.5
  172.7 0.0 copy-start.6
  172.7 0.0 copy-start
  172.7 0.0 copy-done.1
  172.8 0.0 copy-done.2
  172.8 0.0 copy-done.3
  172.9 0.0 copy-done.4
  172.9 0.7 copy-done.5
  173.7 0.0 copy-done.6
  173.7 0.0 copy-done
  173.8 0.9 dynamic-slice_bitcast_fusion
  (9 shorter events, 0.2 us)
Async XLA Ops:
  0.0 9.1 %copy-start.7 = (bf16[1,7,7,352]{3,2,1,0:T(8,128)(2,1)S(1)}, bf16[1,7,7,352]{3,2,1,0:T(8,128)(2,1)}, u32[]{:S(2)}) copy-start(bf16[1,7,7,352]{3,2,1,0:T(8,128)(2,1)} %param.12) | copy-start | bytes 103492
  1.0 33.0 %collective-permute-start = (bf16[1,3,48,352]{3,2,1,0:T(8,128)(2,1)S(1)}, bf16[1,3,48,352]{3,2,1,0:T(8,128)(2,1)S(1)}, u32[]{:S(2)}, u32[]{:S(2)}) collective-permute-start(bf16[1,3,48,352]{3,2,1,0:T(8,128)(2,1)S(1)} %get-tuple-element.33), channel_id=1, source_target_pairs={{0,8},{8,16},{16,24},{24,32},{32,40},{40,48},{48,56},{56,64},{64,7... | collective-permute-start | bytes 304136 | tf_op jit(solution)/shard_map/ppermute | solution.py:25
  5.5 28.5 %collective-permute-start.1 = (bf16[1,3,48,352]{3,2,1,0:T(8,128)(2,1)S(1)}, bf16[1,3,48,352]{3,2,1,0:T(8,128)(2,1)S(1)}, u32[]{:S(2)}, u32[]{:S(2)}) collective-permute-start(bf16[1,3,48,352]{3,2,1,0:T(8,128)(2,1)S(1)} %get-tuple-element.34), channel_id=1, source_target_pairs={{8,0},{16,8},{24,16},{32,24},{40,32},{48,40},{56,48},{64,56},{72,6... | collective-permute-start | bytes 304136 | tf_op jit(solution)/shard_map/ppermute | solution.py:27
  160.6 12.2 %copy-start.1 = (bf16[192,352]{1,0:T(8,128)(2,1)S(1)}, bf16[192,352]{1,0:T(8,128)(2,1)}, u32[]{:S(2)}) copy-start(bf16[192,352]{1,0:T(8,128)(2,1)} %get-tuple-element.21) | copy-start | bytes 405508
  160.6 12.2 %copy-start.2 = (bf16[192,352]{1,0:T(8,128)(2,1)S(1)}, bf16[192,352]{1,0:T(8,128)(2,1)}, u32[]{:S(2)}) copy-start(bf16[192,352]{1,0:T(8,128)(2,1)} %get-tuple-element.23) | copy-start | bytes 405508
  160.6 12.2 %copy-start.3 = (bf16[192,352]{1,0:T(8,128)(2,1)S(1)}, bf16[192,352]{1,0:T(8,128)(2,1)}, u32[]{:S(2)}) copy-start(bf16[192,352]{1,0:T(8,128)(2,1)} %get-tuple-element.25) | copy-start | bytes 405508
  160.6 12.3 %copy-start.4 = (bf16[192,352]{1,0:T(8,128)(2,1)S(1)}, bf16[192,352]{1,0:T(8,128)(2,1)}, u32[]{:S(2)}) copy-start(bf16[192,352]{1,0:T(8,128)(2,1)} %get-tuple-element.27) | copy-start | bytes 405508
  172.7 0.9 copy-start.5
  172.7 1.0 copy-start.6
  172.7 1.0 copy-start

commit v7 on v5

--- a/solution.py
+++ b/solution.py
@@ -385,16 +385,76 @@
     return produced, arriving
 
 
-def _gather_kernel(n, chunks, mine_ref, held_ref, other_ref, send_sem, recv_sem, pass_send, pass_recv):
+def _gather_kernel(
+    n,
+    chunks,
+    rows,
+    mine_ref,
+    images_ref,
+    held_ref,
+    other_ref,
+    fresh_ref,
+    send_sem,
+    recv_sem,
+    pass_send,
+    pass_recv,
+    halo_send,
+    halo_recv,
+    own_sem,
+):
     me = lax.axis_index("dp")
     row = lax.axis_index("row")
+    odd = lax.rem(row, 2) == 1
     partner = {"row": row + 1 - 2 * lax.rem(row, 2)}
+    outer = jnp.where(odd, row + 1, row - 1)
+    has_outer = jnp.logical_and(outer >= 0, outer < rows)
     right = {"dp": lax.rem(me + 1, n)}
     left = {"dp": lax.rem(me + n - 1, n)}
     barrier = pltpu.get_barrier_semaphore()
     for peer in (right, left, partner):
         pl.semaphore_signal(barrier, inc=1, device_id=peer, device_id_type=MESH)
-    pl.semaphore_wait(barrier, 3)
+
+    @pl.when(has_outer)
+    def _():
+        pl.semaphore_signal(barrier, inc=1, device_id={"row": outer}, device_id_type=MESH)
+
+    pl.semaphore_wait(barrier, 3 + has_outer.astype(jnp.int32))
+    cells = images_ref.shape[1]
+    edge = 3 * cells // 4
+    own = pltpu.make_async_copy(images_ref, fresh_ref.at[:, pl.ds(edge, cells)], own_sem)
+    own.start()
+    has_above = row > 0
+    has_below = row < rows - 1
+    halos = (
+        (0, pl.ds(0, edge), pl.ds(edge + cells, edge), -1, has_above),
+        (1, pl.ds(cells - edge, edge), pl.ds(0, edge), 1, has_below),
+    )
+
+    def halo_copy(slot, src, dst, peer_row):
+        return pltpu.make_async_remote_copy(
+            src_ref=images_ref.at[:, src],
+            dst_ref=fresh_ref.at[:, dst],
+            send_sem=halo_send.at[slot],
+            recv_sem=halo_recv.at[slot],
+            device_id={"row": peer_row},
+            device_id_type=MESH,
+        )
+
+    for slot, src, dst, shift, cond in halos:
+        pl.when(cond)(halo_copy(slot, src, dst, row + shift).start)
+
+    @pl.when(jnp.logical_not(has_above))
+    def _():
+        fresh_ref[:, pl.ds(0, edge), :] = jnp.zeros(
+            (fresh_ref.shape[0], edge, fresh_ref.shape[2]), fresh_ref.dtype
+        )
+
+    @pl.when(jnp.logical_not(has_below))
+    def _():
+        fresh_ref[:, pl.ds(edge + cells, edge), :] = jnp.zeros(
+            (fresh_ref.shape[0], edge, fresh_ref.shape[2]), fresh_ref.dtype
+        )
+
     sends = []
     parts = len(chunks)
 
@@ -441,31 +501,43 @@
     for slot in range(n):
         for c in range(parts):
             arrived(other_ref, pass_recv, slot, c)
+    for slot, src, dst, shift, cond in halos:
+        pl.when(halos[1 - slot][4])(halo_copy(slot, src, dst, row).wait_recv)
+    for slot, src, dst, shift, cond in halos:
+        pl.when(cond)(halo_copy(slot, src, dst, row + shift).wait_send)
+    own.wait()
     for copy in sends:
         copy.wait_send()
 
 
-def gathered_weights(proj_in, proj_out):
+def gathered_weights(proj_in, proj_out, images):
     n = lax.axis_size("dp")
     first_core = lax.rem(lax.axis_index("row"), 2) == 0
     mine = jnp.where(first_core, proj_in.T, proj_out)
     part, channels = mine.shape
     vmem = pl.BlockSpec(memory_space=pltpu.VMEM)
     gathered = jax.ShapeDtypeStruct((n, part, channels), mine.dtype)
-    held, other = pl.pallas_call(
-        functools.partial(_gather_kernel, n, (pl.ds(0, 96), pl.ds(96, part - 96))),
-        out_shape=[gathered, gathered],
-        in_specs=[vmem],
-        out_specs=[vmem, vmem],
+    micro, cells, _ = images.shape
+    fresh = jax.ShapeDtypeStruct((micro, cells * 5 // 2, channels), images.dtype)
+    held, other, fresh = pl.pallas_call(
+        functools.partial(
+            _gather_kernel, n, (pl.ds(0, 96), pl.ds(96, part - 96)), lax.axis_size("row")
+        ),
+        out_shape=[gathered, gathered, fresh],
+        in_specs=[vmem, vmem],
+        out_specs=[vmem, vmem, vmem],
         scratch_shapes=[
             pltpu.SemaphoreType.DMA((4 * n,)),
             pltpu.SemaphoreType.DMA((2 * n,)),
             pltpu.SemaphoreType.DMA((4 * n,)),
             pltpu.SemaphoreType.DMA((2 * n,)),
+            pltpu.SemaphoreType.DMA((2,)),
+            pltpu.SemaphoreType.DMA((2,)),
+            pltpu.SemaphoreType.DMA(()),
         ],
         compiler_params=pltpu.CompilerParams(collective_id=7, has_side_effects=True),
-    )(mine)
-    return held.reshape(n * part, channels), other.reshape(n * part, channels)
+    )(mine, images)
+    return held.reshape(n * part, channels), other.reshape(n * part, channels), fresh
 
 
 def on_device(
@@ -481,8 +553,11 @@
     proj_out,
     bias_out,
 ):
-    fresh = extended(inputs[:, 0], (("row", 1),), 3)
-    proj_in, proj_out = gathered_weights(proj_in[0], proj_out[0])
+    num_micro, _, num_rows, num_cols, channels = inputs.shape
+    proj_in, proj_out, fresh = gathered_weights(
+        proj_in[0], proj_out[0], inputs.reshape(num_micro, num_rows * num_cols, channels)
+    )
+    fresh = fresh.reshape(num_micro, -1, num_cols, channels)
     sections = lax.axis_size("section")
     section_index = lax.axis_index("section")
     num_micro = inputs.shape[0]

time: 176 us -> 172 us (0.977)
  starting transfers between devices: 6.48 us -> 0 us
  Pallas kernels: 162 us -> 164 us
    ppermute x2 -> x0, starting transfers between devices: 6.48 us -> none  [the longest x1 4.56 us: extended(): lax.ppermute(tail, axis, [(i, (i + 1) % count) for i in range(ends)])]
    pallas_call x1, Pallas kernels: 24.2 us -> 26.5 us  [gathered_weights(): pl.pallas_call(functools.partial(_gather_kernel, n, (pl.ds(0, 96), pl.ds(...]
    slice x2 -> x0, local copies, waits for them, and re-layouts: 2.15 us -> none  [the longest x1 1.32 us: extended(): lax.slice_in_dim(cells, cells.shape[dim] - width, cells.shape[dim], axis=...]
    reshape x0 -> x1, local copies, waits for them, and re-layouts: none -> 1.76 us  [conv_block(): padded.reshape(-1, channels)]
  transfers between devices with their start and end apart: 2 -> 0, of which waited for: 0 -> 0; matrix products, arithmetic and copies ran while one was open for 1% -> 0% of each run, Pallas kernels for 14% -> 0%
where the time goes in v7:
time: 172 us; the launch traced here: 171 us
  Pallas kernels  164 us (95%)
  local copies, waits for them, and re-layouts  4.99 us (3%)
    pallas_call x7, Pallas kernels, pointwise(): pl.pallas_call(functools.partial(_pointwise_kernel, n, sections, hand_on,...  138 us
    pallas_call x1, Pallas kernels, gathered_weights(): pl.pallas_call(functools.partial(_gather_kernel, n, (pl.ds(0, 96), pl.ds(...  26.5 us

profile of v7, /device:TPU:7, one launch (start us, length us, event | category | flops | bytes accessed | tf_op | source)
XLA Modules:
  0.0 171.1 jit_solution(18070319944581404818)
XLA Ops:
  0.0 1.4 reshape_squeeze.2.taps_ref
  1.4 1.6 bitcast_select_fusion.mine_ref
  3.1 26.5 %shard_map.109 = (bf16[8,176,352]{2,1,0:T(8,128)(2,1)}, bf16[8,176,352]{2,1,0:T(8,128)(2,1)}, bf16[4,480,352]{2,1,0:T(8,128)(2,1)}) custom-call(bf16[176,352]{1,0:T(8,128)(2,1)} %bitcast_select_fusion.mine_ref, bf16[4,192,352]{2,1,0:T(8,128)(2,1)} %bitcast.35), custom_call_target="tpu_custom_call" | custom-call | tf_op jit(solution)/shard_map/pallas_call | solution.py:522
  29.6 1.8 %slice_bitcast_fusion.padded_ref = bf16[480,352]{1,0:T(8,128)(2,1)} fusion(bf16[4,480,352]{2,1,0:T(8,128)(2,1)} %get-tuple-element.20.fresh_ref), kind=kLoop, calls=%fused_computation.1 | loop fusion | bytes 675840 | tf_op jit(solution)/shard_map/reshape | solution.py:367
  31.4 27.6 %shard_map.110 = (bf16[192,352]{1,0:T(8,128)(2,1)}, bf16[480,352]{1,0:T(8,128)(2,1)}) custom-call(bf16[480,352]{1,0:T(8,128)(2,1)} %slice_bitcast_fusion.padded_ref, bf16[4,480,352]{2,1,0:T(8,128)(2,1)} %get-tuple-element.20.fresh_ref, bf16[1408,352]{1,0:T(8,128)(2,1)} %bitcast.20, bf16[1408,352]{1,0:T(8,128)(2,1)} %bitcast.27, ...), custom_call_target="tpu_custom_call" | custom-call | flops 380633088 | bytes 2523136 | tf_op jit(solution)/shard_map/pallas_call | solution.py:302
  59.0 21.2 %shard_map.111 = (bf16[192,352]{1,0:T(8,128)(2,1)}, bf16[480,352]{1,0:T(8,128)(2,1)}) custom-call(bf16[480,352]{1,0:T(8,128)(2,1)} %get-tuple-element.24.padded_ref, bf16[4,480,352]{2,1,0:T(8,128)(2,1)} %get-tuple-element.20.fresh_ref, bf16[1408,352]{1,0:T(8,128)(2,1)} %bitcast.21, bf16[1408,352]{1,0:T(8,128)(2,1)} %bitcast.28, ...), custom_call_target="tpu_custom_call" | custom-call | flops 380633088 | bytes 2523136 | tf_op jit(solution)/shard_map/pallas_call | solution.py:302
  80.2 20.6 %shard_map.112 = (bf16[192,352]{1,0:T(8,128)(2,1)}, bf16[480,352]{1,0:T(8,128)(2,1)}) custom-call(bf16[480,352]{1,0:T(8,128)(2,1)} %get-tuple-element.26.padded_ref, bf16[4,480,352]{2,1,0:T(8,128)(2,1)} %get-tuple-element.20.fresh_ref, bf16[1408,352]{1,0:T(8,128)(2,1)} %bitcast.22, bf16[1408,352]{1,0:T(8,128)(2,1)} %bitcast.29, ...), custom_call_target="tpu_custom_call" | custom-call | flops 380633088 | bytes 2523136 | tf_op jit(solution)/shard_map/pallas_call | solution.py:302
  100.8 18.8 %shard_map.113 = (bf16[192,352]{1,0:T(8,128)(2,1)}, bf16[480,352]{1,0:T(8,128)(2,1)}) custom-call(bf16[480,352]{1,0:T(8,128)(2,1)} %get-tuple-element.28.padded_ref, bf16[4,480,352]{2,1,0:T(8,128)(2,1)} %get-tuple-element.20.fresh_ref, bf16[1408,352]{1,0:T(8,128)(2,1)} %bitcast.23, bf16[1408,352]{1,0:T(8,128)(2,1)} %bitcast.30, ...), custom_call_target="tpu_custom_call" | custom-call | flops 380633088 | bytes 2523136 | tf_op jit(solution)/shard_map/pallas_call | solution.py:302
  119.6 18.8 %shard_map.114 = (bf16[192,352]{1,0:T(8,128)(2,1)}, bf16[480,352]{1,0:T(8,128)(2,1)}) custom-call(bf16[480,352]{1,0:T(8,128)(2,1)} %get-tuple-element.30.padded_ref, bf16[4,480,352]{2,1,0:T(8,128)(2,1)} %get-tuple-element.20.fresh_ref, bf16[1408,352]{1,0:T(8,128)(2,1)} %bitcast.24, bf16[1408,352]{1,0:T(8,128)(2,1)} %bitcast.31, ...), custom_call_target="tpu_custom_call" | custom-call | flops 380633088 | bytes 2523136 | tf_op jit(solution)/shard_map/pallas_call | solution.py:302
  138.3 18.3 %shard_map.115 = (bf16[192,352]{1,0:T(8,128)(2,1)}, bf16[480,352]{1,0:T(8,128)(2,1)}) custom-call(bf16[480,352]{1,0:T(8,128)(2,1)} %get-tuple-element.32.padded_ref, bf16[4,480,352]{2,1,0:T(8,128)(2,1)} %get-tuple-element.20.fresh_ref, bf16[1408,352]{1,0:T(8,128)(2,1)} %bitcast.25, bf16[1408,352]{1,0:T(8,128)(2,1)} %bitcast.32, ...), custom_call_target="tpu_custom_call" | custom-call | flops 380633088 | bytes 2523136 | tf_op jit(solution)/shard_map/pallas_call | solution.py:302
  156.6 0.0 copy-start.1
  156.6 0.0 copy-start.2
  156.6 0.0 copy-start.3
  156.6 0.0 copy-start.4
  156.7 0.0 copy-start.5
  156.7 12.5 %shard_map.116 = bf16[192,352]{1,0:T(8,128)(2,1)} custom-call(bf16[480,352]{1,0:T(8,128)(2,1)} %get-tuple-element.34.padded_ref, bf16[4,480,352]{2,1,0:T(8,128)(2,1)} %get-tuple-element.20.fresh_ref, bf16[1408,352]{1,0:T(8,128)(2,1)} %bitcast.26, bf16[1408,352]{1,0:T(8,128)(2,1)} %bitcast.33, bf16[1,1408]{1,0:T(2,128)(2,1)} %bias_in_ref.13, ...), custom_call_target="tpu_custom_call" | custom-call | flops 380633088 | bytes 2523136 | tf_op jit(solution)/shard_map/pallas_call | solution.py:302
  169.2 0.0 copy-start.6
  169.2 0.0 copy-start
  169.2 0.0 copy-done.1
  169.2 0.0 copy-done.2
  169.3 0.0 copy-done.3
  169.3 0.0 copy-done.4
  169.4 0.0 copy-done.5
  169.4 0.7 copy-done.6
  170.1 0.0 copy-done
  170.2 0.9 dynamic-slice_bitcast_fusion
  (7 shorter events, 0.2 us)
Async XLA Ops:
  156.6 12.6 %copy-start.1 = (bf16[192,352]{1,0:T(8,128)(2,1)S(1)}, bf16[192,352]{1,0:T(8,128)(2,1)}, u32[]{:S(2)}) copy-start(bf16[192,352]{1,0:T(8,128)(2,1)} %get-tuple-element.23) | copy-start | bytes 405508
  156.6 12.6 %copy-start.2 = (bf16[192,352]{1,0:T(8,128)(2,1)S(1)}, bf16[192,352]{1,0:T(8,128)(2,1)}, u32[]{:S(2)}) copy-start(bf16[192,352]{1,0:T(8,128)(2,1)} %get-tuple-element.25) | copy-start | bytes 405508
  156.6 12.7 %copy-start.3 = (bf16[192,352]{1,0:T(8,128)(2,1)S(1)}, bf16[192,352]{1,0:T(8,128)(2,1)}, u32[]{:S(2)}) copy-start(bf16[192,352]{1,0:T(8,128)(2,1)} %get-tuple-element.27) | copy-start | bytes 405508
  156.6 12.7 %copy-start.4 = (bf16[192,352]{1,0:T(8,128)(2,1)S(1)}, bf16[192,352]{1,0:T(8,128)(2,1)}, u32[]{:S(2)}) copy-start(bf16[192,352]{1,0:T(8,128)(2,1)} %get-tuple-element.29) | copy-start | bytes 405508
  156.7 12.7 %copy-start.5 = (bf16[192,352]{1,0:T(8,128)(2,1)S(1)}, bf16[192,352]{1,0:T(8,128)(2,1)}, u32[]{:S(2)}) copy-start(bf16[192,352]{1,0:T(8,128)(2,1)} %get-tuple-element.31) | copy-start | bytes 405508
  169.2 0.9 copy-start.6
  169.2 1.0 copy-start

commit v8 on v7

--- a/solution.py
+++ b/solution.py
@@ -150,11 +150,8 @@
         copy.start()
         sends.append(copy)
     if hand_on:
-        @pl.when(section == 0)
-        def _():
-            fresh_copy = pltpu.make_async_copy(fresh_ref.at[fresh_index], next_ref, fresh_sem)
-            fresh_copy.start()
-            fresh_copy.wait()
+        fresh_copy = pltpu.make_async_copy(fresh_ref.at[fresh_index], next_ref, fresh_sem)
+        pl.when(section == 0)(fresh_copy.start)
 
         @pl.when(jnp.logical_and(has_prev, jnp.logical_not(has_above)))
         def _():
@@ -254,6 +251,7 @@
     def _():
         handed.wait_send()
 
+    pl.when(section == 0)(fresh_copy.wait)
     for copy in sends:
         copy.wait_send()
 

time: 172 us -> 172 us (level)
  no operation moved by 1% of the time
where the time goes in v8:
time: 172 us; the launch traced here: 171 us
  Pallas kernels  164 us (95%)
  local copies, waits for them, and re-layouts  4.99 us (3%)
    pallas_call x7, Pallas kernels, pointwise(): pl.pallas_call(functools.partial(_pointwise_kernel, n, sections, hand_on,...  138 us
    pallas_call x1, Pallas kernels, gathered_weights(): pl.pallas_call(functools.partial(_gather_kernel, n, (pl.ds(0, 96), pl.ds(...  26.5 us

profile of v8, /device:TPU:7, one launch (start us, length us, event | category | flops | bytes accessed | tf_op | source)
XLA Modules:
  0.0 171.3 jit_solution(11568916428058644865)
XLA Ops:
  0.0 1.4 reshape_squeeze.2.taps_ref
  1.4 1.6 bitcast_select_fusion.mine_ref
  3.1 26.5 %shard_map.109 = (bf16[8,176,352]{2,1,0:T(8,128)(2,1)}, bf16[8,176,352]{2,1,0:T(8,128)(2,1)}, bf16[4,480,352]{2,1,0:T(8,128)(2,1)}) custom-call(bf16[176,352]{1,0:T(8,128)(2,1)} %bitcast_select_fusion.mine_ref, bf16[4,192,352]{2,1,0:T(8,128)(2,1)} %bitcast.35), custom_call_target="tpu_custom_call" | custom-call | tf_op jit(solution)/shard_map/pallas_call | solution.py:520
  29.6 1.8 %slice_bitcast_fusion.padded_ref = bf16[480,352]{1,0:T(8,128)(2,1)} fusion(bf16[4,480,352]{2,1,0:T(8,128)(2,1)} %get-tuple-element.20.fresh_ref), kind=kLoop, calls=%fused_computation.1 | loop fusion | bytes 675840 | tf_op jit(solution)/shard_map/reshape | solution.py:365
  31.4 27.6 %shard_map.110 = (bf16[192,352]{1,0:T(8,128)(2,1)}, bf16[480,352]{1,0:T(8,128)(2,1)}) custom-call(bf16[480,352]{1,0:T(8,128)(2,1)} %slice_bitcast_fusion.padded_ref, bf16[4,480,352]{2,1,0:T(8,128)(2,1)} %get-tuple-element.20.fresh_ref, bf16[1408,352]{1,0:T(8,128)(2,1)} %bitcast.20, bf16[1408,352]{1,0:T(8,128)(2,1)} %bitcast.27, ...), custom_call_target="tpu_custom_call" | custom-call | flops 380633088 | bytes 2523136 | tf_op jit(solution)/shard_map/pallas_call | solution.py:300
  59.0 21.2 %shard_map.111 = (bf16[192,352]{1,0:T(8,128)(2,1)}, bf16[480,352]{1,0:T(8,128)(2,1)}) custom-call(bf16[480,352]{1,0:T(8,128)(2,1)} %get-tuple-element.24.padded_ref, bf16[4,480,352]{2,1,0:T(8,128)(2,1)} %get-tuple-element.20.fresh_ref, bf16[1408,352]{1,0:T(8,128)(2,1)} %bitcast.21, bf16[1408,352]{1,0:T(8,128)(2,1)} %bitcast.28, ...), custom_call_target="tpu_custom_call" | custom-call | flops 380633088 | bytes 2523136 | tf_op jit(solution)/shard_map/pallas_call | solution.py:300
  80.2 20.6 %shard_map.112 = (bf16[192,352]{1,0:T(8,128)(2,1)}, bf16[480,352]{1,0:T(8,128)(2,1)}) custom-call(bf16[480,352]{1,0:T(8,128)(2,1)} %get-tuple-element.26.padded_ref, bf16[4,480,352]{2,1,0:T(8,128)(2,1)} %get-tuple-element.20.fresh_ref, bf16[1408,352]{1,0:T(8,128)(2,1)} %bitcast.22, bf16[1408,352]{1,0:T(8,128)(2,1)} %bitcast.29, ...), custom_call_target="tpu_custom_call" | custom-call | flops 380633088 | bytes 2523136 | tf_op jit(solution)/shard_map/pallas_call | solution.py:300
  100.8 18.8 %shard_map.113 = (bf16[192,352]{1,0:T(8,128)(2,1)}, bf16[480,352]{1,0:T(8,128)(2,1)}) custom-call(bf16[480,352]{1,0:T(8,128)(2,1)} %get-tuple-element.28.padded_ref, bf16[4,480,352]{2,1,0:T(8,128)(2,1)} %get-tuple-element.20.fresh_ref, bf16[1408,352]{1,0:T(8,128)(2,1)} %bitcast.23, bf16[1408,352]{1,0:T(8,128)(2,1)} %bitcast.30, ...), custom_call_target="tpu_custom_call" | custom-call | flops 380633088 | bytes 2523136 | tf_op jit(solution)/shard_map/pallas_call | solution.py:300
  119.6 19.0 %shard_map.114 = (bf16[192,352]{1,0:T(8,128)(2,1)}, bf16[480,352]{1,0:T(8,128)(2,1)}) custom-call(bf16[480,352]{1,0:T(8,128)(2,1)} %get-tuple-element.30.padded_ref, bf16[4,480,352]{2,1,0:T(8,128)(2,1)} %get-tuple-element.20.fresh_ref, bf16[1408,352]{1,0:T(8,128)(2,1)} %bitcast.24, bf16[1408,352]{1,0:T(8,128)(2,1)} %bitcast.31, ...), custom_call_target="tpu_custom_call" | custom-call | flops 380633088 | bytes 2523136 | tf_op jit(solution)/shard_map/pallas_call | solution.py:300
  138.6 18.2 %shard_map.115 = (bf16[192,352]{1,0:T(8,128)(2,1)}, bf16[480,352]{1,0:T(8,128)(2,1)}) custom-call(bf16[480,352]{1,0:T(8,128)(2,1)} %get-tuple-element.32.padded_ref, bf16[4,480,352]{2,1,0:T(8,128)(2,1)} %get-tuple-element.20.fresh_ref, bf16[1408,352]{1,0:T(8,128)(2,1)} %bitcast.25, bf16[1408,352]{1,0:T(8,128)(2,1)} %bitcast.32, ...), custom_call_target="tpu_custom_call" | custom-call | flops 380633088 | bytes 2523136 | tf_op jit(solution)/shard_map/pallas_call | solution.py:300
  156.8 0.0 copy-start.1
  156.8 0.0 copy-start.2
  156.8 0.0 copy-start.3
  156.8 0.0 copy-start.4
  156.8 0.0 copy-start.5
  156.8 12.6 %shard_map.116 = bf16[192,352]{1,0:T(8,128)(2,1)} custom-call(bf16[480,352]{1,0:T(8,128)(2,1)} %get-tuple-element.34.padded_ref, bf16[4,480,352]{2,1,0:T(8,128)(2,1)} %get-tuple-element.20.fresh_ref, bf16[1408,352]{1,0:T(8,128)(2,1)} %bitcast.26, bf16[1408,352]{1,0:T(8,128)(2,1)} %bitcast.33, bf16[1,1408]{1,0:T(2,128)(2,1)} %bias_in_ref.13, ...), custom_call_target="tpu_custom_call" | custom-call | flops 380633088 | bytes 2523136 | tf_op jit(solution)/shard_map/pallas_call | solution.py:300
  169.4 0.0 copy-start.6
  169.4 0.0 copy-start
  169.4 0.0 copy-done.1
  169.5 0.0 copy-done.2
  169.5 0.0 copy-done.3
  169.5 0.0 copy-done.4
  169.6 0.0 copy-done.5
  169.6 0.7 copy-done.6
  170.3 0.0 copy-done
  170.4 0.9 dynamic-slice_bitcast_fusion
  (7 shorter events, 0.2 us)
Async XLA Ops:
  156.8 12.7 %copy-start.1 = (bf16[192,352]{1,0:T(8,128)(2,1)S(1)}, bf16[192,352]{1,0:T(8,128)(2,1)}, u32[]{:S(2)}) copy-start(bf16[192,352]{1,0:T(8,128)(2,1)} %get-tuple-element.23) | copy-start | bytes 405508
  156.8 12.7 %copy-start.2 = (bf16[192,352]{1,0:T(8,128)(2,1)S(1)}, bf16[192,352]{1,0:T(8,128)(2,1)}, u32[]{:S(2)}) copy-start(bf16[192,352]{1,0:T(8,128)(2,1)} %get-tuple-element.25) | copy-start | bytes 405508
  156.8 12.7 %copy-start.3 = (bf16[192,352]{1,0:T(8,128)(2,1)S(1)}, bf16[192,352]{1,0:T(8,128)(2,1)}, u32[]{:S(2)}) copy-start(bf16[192,352]{1,0:T(8,128)(2,1)} %get-tuple-element.27) | copy-start | bytes 405508
  156.8 12.7 %copy-start.4 = (bf16[192,352]{1,0:T(8,128)(2,1)S(1)}, bf16[192,352]{1,0:T(8,128)(2,1)}, u32[]{:S(2)}) copy-start(bf16[192,352]{1,0:T(8,128)(2,1)} %get-tuple-element.29) | copy-start | bytes 405508
  156.8 12.8 %copy-start.5 = (bf16[192,352]{1,0:T(8,128)(2,1)S(1)}, bf16[192,352]{1,0:T(8,128)(2,1)}, u32[]{:S(2)}) copy-start(bf16[192,352]{1,0:T(8,128)(2,1)} %get-tuple-element.31) | copy-start | bytes 405508
  169.4 0.9 copy-start.6
  169.4 1.0 copy-start

commit v9 on v8

--- a/solution.py
+++ b/solution.py
@@ -79,7 +79,7 @@
 
         waits = waits + has_next.astype(jnp.int32)
     padded_rows, margin_cols, channels = wide_ref.shape
-    cols = padded_ref.shape[0] // padded_rows
+    cols = out_ref.shape[0] // (padded_rows - 6)
     out_rows = padded_rows - 6
     zeros = jnp.zeros((8, channels), jnp.float32)
     for r in range(padded_rows):
@@ -101,7 +101,7 @@
                 for h in range(out_rows):
                     i = r - h
                     if 0 <= i < 7:
-                        tap = taps_ref[pl.ds(i * 7 + j, 1), lanes].astype(jnp.float32)
+                        tap = taps_ref[i, pl.ds(j, 1), lanes].astype(jnp.float32)
                         acc[h] = acc[h] + slab * tap
         for h in range(out_rows):
             conv_ref[h, :, lanes] = acc[h]
@@ -276,7 +276,7 @@
     n = lax.axis_size("row")
     sections = lax.axis_size("section")
     channels = padded.shape[1]
-    padded_rows = padded.shape[0] // cols
+    padded_rows = fresh.shape[1] // cols
     cells = (padded_rows - 6) * cols
     hidden_units = held.shape[0]
     vmem = pl.BlockSpec(memory_space=pltpu.VMEM)
@@ -320,7 +320,7 @@
         grn_gamma.reshape(1, -1),
         grn_beta.reshape(1, -1),
         bias_out.reshape(1, -1),
-        depth_kernel.reshape(-1, channels),
+        depth_kernel,
         depth_bias.reshape(1, -1),
         norm_gain.reshape(1, -1),
         norm_bias.reshape(1, -1),
@@ -378,8 +378,8 @@
         num_cols,
         hand_on,
     )
-    produced = results[0].reshape(num_items, padded_rows - 6, num_cols, channels)
-    arriving = results[1].reshape(padded.shape) if hand_on else None
+    produced = results[0].reshape(1, -1, num_cols, channels)
+    arriving = results[1].reshape(1, -1, num_cols, channels) if hand_on else None
     return produced, arriving
 
 
@@ -572,7 +572,7 @@
         bias_out[0],
     )
     num_ticks = num_micro + sections - 1
-    current = fresh[:1]
+    current = fresh
     outputs = []
     for tick_index in range(num_ticks):
         hand_on = tick_index + 1 < num_ticks

time: 172 us -> 169 us (0.983)
  local copies, waits for them, and re-layouts: 4.99 us -> 1.88 us
    reshape x1 -> x0, local copies, waits for them, and re-layouts: 1.76 us -> none  [conv_block(): padded.reshape(-1, channels)]
where the time goes in v9:
time: 169 us; the launch traced here: 168 us
  Pallas kernels  165 us (98%)
  local copies, waits for them, and re-layouts  1.88 us (1%)
    pallas_call x7, Pallas kernels, pointwise(): pl.pallas_call(functools.partial(_pointwise_kernel, n, sections, hand_on,...  138 us
    pallas_call x1, Pallas kernels, gathered_weights(): pl.pallas_call(functools.partial(_gather_kernel, n, (pl.ds(0, 96), pl.ds(...  26.5 us

profile of v9, /device:TPU:7, one launch (start us, length us, event | category | flops | bytes accessed | tf_op | source)
XLA Modules:
  0.0 168.3 jit_solution(3281774467999554831)
XLA Ops:
  0.0 1.6 bitcast_select_fusion.mine_ref
  1.6 26.5 %shard_map.109 = (bf16[8,176,352]{2,1,0:T(8,128)(2,1)}, bf16[8,176,352]{2,1,0:T(8,128)(2,1)}, bf16[4,480,352]{2,1,0:T(8,128)(2,1)}) custom-call(bf16[176,352]{1,0:T(8,128)(2,1)} %bitcast_select_fusion.mine_ref, bf16[4,192,352]{2,1,0:T(8,128)(2,1)} %bitcast.43), custom_call_target="tpu_custom_call" | custom-call | tf_op jit(solution)/shard_map/pallas_call | solution.py:520
  28.2 27.9 %shard_map.110 = (bf16[192,352]{1,0:T(8,128)(2,1)}, bf16[480,352]{1,0:T(8,128)(2,1)}) custom-call(bf16[1920,352]{1,0:T(8,128)(2,1)} %bitcast.20, bf16[4,480,352]{2,1,0:T(8,128)(2,1)} %get-tuple-element.20.fresh_ref, bf16[1408,352]{1,0:T(8,128)(2,1)} %bitcast.21, bf16[1408,352]{1,0:T(8,128)(2,1)} %bitcast.28, bf16[1,1408]{1,0:T(2,128)(2,1)} %bias_in_ref.13, ...), custom_call_target="tpu_custom_call" | custom-call | flops 380633088 | bytes 2523136 | tf_op jit(solution)/shard_map/pallas_call | solution.py:300
  56.1 21.2 %shard_map.111 = (bf16[192,352]{1,0:T(8,128)(2,1)}, bf16[480,352]{1,0:T(8,128)(2,1)}) custom-call(bf16[480,352]{1,0:T(8,128)(2,1)} %get-tuple-element.24.padded_ref, bf16[4,480,352]{2,1,0:T(8,128)(2,1)} %get-tuple-element.20.fresh_ref, bf16[1408,352]{1,0:T(8,128)(2,1)} %bitcast.22, bf16[1408,352]{1,0:T(8,128)(2,1)} %bitcast.29, ...), custom_call_target="tpu_custom_call" | custom-call | flops 380633088 | bytes 2523136 | tf_op jit(solution)/shard_map/pallas_call | solution.py:300
  77.3 20.6 %shard_map.112 = (bf16[192,352]{1,0:T(8,128)(2,1)}, bf16[480,352]{1,0:T(8,128)(2,1)}) custom-call(bf16[480,352]{1,0:T(8,128)(2,1)} %get-tuple-element.26.padded_ref, bf16[4,480,352]{2,1,0:T(8,128)(2,1)} %get-tuple-element.20.fresh_ref, bf16[1408,352]{1,0:T(8,128)(2,1)} %bitcast.23, bf16[1408,352]{1,0:T(8,128)(2,1)} %bitcast.30, ...), custom_call_target="tpu_custom_call" | custom-call | flops 380633088 | bytes 2523136 | tf_op jit(solution)/shard_map/pallas_call | solution.py:300
  97.9 18.8 %shard_map.113 = (bf16[192,352]{1,0:T(8,128)(2,1)}, bf16[480,352]{1,0:T(8,128)(2,1)}) custom-call(bf16[480,352]{1,0:T(8,128)(2,1)} %get-tuple-element.28.padded_ref, bf16[4,480,352]{2,1,0:T(8,128)(2,1)} %get-tuple-element.20.fresh_ref, bf16[1408,352]{1,0:T(8,128)(2,1)} %bitcast.24, bf16[1408,352]{1,0:T(8,128)(2,1)} %bitcast.31, ...), custom_call_target="tpu_custom_call" | custom-call | flops 380633088 | bytes 2523136 | tf_op jit(solution)/shard_map/pallas_call | solution.py:300
  116.7 18.9 %shard_map.114 = (bf16[192,352]{1,0:T(8,128)(2,1)}, bf16[480,352]{1,0:T(8,128)(2,1)}) custom-call(bf16[480,352]{1,0:T(8,128)(2,1)} %get-tuple-element.30.padded_ref, bf16[4,480,352]{2,1,0:T(8,128)(2,1)} %get-tuple-element.20.fresh_ref, bf16[1408,352]{1,0:T(8,128)(2,1)} %bitcast.25, bf16[1408,352]{1,0:T(8,128)(2,1)} %bitcast.32, ...), custom_call_target="tpu_custom_call" | custom-call | flops 380633088 | bytes 2523136 | tf_op jit(solution)/shard_map/pallas_call | solution.py:300
  135.7 18.1 %shard_map.115 = (bf16[192,352]{1,0:T(8,128)(2,1)}, bf16[480,352]{1,0:T(8,128)(2,1)}) custom-call(bf16[480,352]{1,0:T(8,128)(2,1)} %get-tuple-element.32.padded_ref, bf16[4,480,352]{2,1,0:T(8,128)(2,1)} %get-tuple-element.20.fresh_ref, bf16[1408,352]{1,0:T(8,128)(2,1)} %bitcast.26, bf16[1408,352]{1,0:T(8,128)(2,1)} %bitcast.33, ...), custom_call_target="tpu_custom_call" | custom-call | flops 380633088 | bytes 2523136 | tf_op jit(solution)/shard_map/pallas_call | solution.py:300
  153.8 0.0 copy-start.1
  153.8 0.0 copy-start.2
  153.8 0.0 copy-start.3
  153.8 0.0 copy-start.4
  153.9 12.5 %shard_map.116 = bf16[192,352]{1,0:T(8,128)(2,1)} custom-call(bf16[480,352]{1,0:T(8,128)(2,1)} %get-tuple-element.34.padded_ref, bf16[4,480,352]{2,1,0:T(8,128)(2,1)} %get-tuple-element.20.fresh_ref, bf16[1408,352]{1,0:T(8,128)(2,1)} %bitcast.27, bf16[1408,352]{1,0:T(8,128)(2,1)} %bitcast.34, bf16[1,1408]{1,0:T(2,128)(2,1)} %bias_in_ref.13, ...), custom_call_target="tpu_custom_call" | custom-call | flops 380633088 | bytes 2523136 | tf_op jit(solution)/shard_map/pallas_call | solution.py:300
  166.4 0.0 copy-start.5
  166.4 0.0 copy-start.6
  166.4 0.0 copy-start
  166.4 0.0 copy-done.1
  166.4 0.0 copy-done.2
  166.5 0.0 copy-done.3
  166.5 0.0 copy-done.4
  166.6 0.7 copy-done.5
  167.3 0.0 copy-done.6
  167.4 0.0 copy-done
  167.4 0.9 dynamic-slice_bitcast_fusion
  (7 shorter events, 0.2 us)
Async XLA Ops:
  153.8 12.6 %copy-start.1 = (bf16[192,352]{1,0:T(8,128)(2,1)S(1)}, bf16[192,352]{1,0:T(8,128)(2,1)}, u32[]{:S(2)}) copy-start(bf16[192,352]{1,0:T(8,128)(2,1)} %get-tuple-element.23) | copy-start | bytes 405508
  153.8 12.6 %copy-start.2 = (bf16[192,352]{1,0:T(8,128)(2,1)S(1)}, bf16[192,352]{1,0:T(8,128)(2,1)}, u32[]{:S(2)}) copy-start(bf16[192,352]{1,0:T(8,128)(2,1)} %get-tuple-element.25) | copy-start | bytes 405508
  153.8 12.6 %copy-start.3 = (bf16[192,352]{1,0:T(8,128)(2,1)S(1)}, bf16[192,352]{1,0:T(8,128)(2,1)}, u32[]{:S(2)}) copy-start(bf16[192,352]{1,0:T(8,128)(2,1)} %get-tuple-element.27) | copy-start | bytes 405508
  153.8 12.7 %copy-start.4 = (bf16[192,352]{1,0:T(8,128)(2,1)S(1)}, bf16[192,352]{1,0:T(8,128)(2,1)}, u32[]{:S(2)}) copy-start(bf16[192,352]{1,0:T(8,128)(2,1)} %get-tuple-element.29) | copy-start | bytes 405508
  166.4 0.9 copy-start.5
  166.4 1.0 copy-start.6
  166.4 1.0 copy-start

commit v10 on v9

--- a/solution.py
+++ b/solution.py
@@ -387,7 +387,8 @@
     n,
     chunks,
     rows,
-    mine_ref,
+    proj_in_ref,
+    proj_out_ref,
     images_ref,
     held_ref,
     other_ref,
@@ -399,6 +400,7 @@
     halo_send,
     halo_recv,
     own_sem,
+    mine_ref,
 ):
     me = lax.axis_index("dp")
     row = lax.axis_index("row")
@@ -411,6 +413,15 @@
     barrier = pltpu.get_barrier_semaphore()
     for peer in (right, left, partner):
         pl.semaphore_signal(barrier, inc=1, device_id=peer, device_id_type=MESH)
+    first_core = jnp.logical_not(odd)
+
+    @pl.when(first_core)
+    def _():
+        mine_ref[...] = proj_in_ref[...].astype(jnp.float32).T.astype(mine_ref.dtype)
+
+    @pl.when(odd)
+    def _():
+        mine_ref[...] = proj_out_ref[...]
 
     @pl.when(has_outer)
     def _():
@@ -510,11 +521,9 @@
 
 def gathered_weights(proj_in, proj_out, images):
     n = lax.axis_size("dp")
-    first_core = lax.rem(lax.axis_index("row"), 2) == 0
-    mine = jnp.where(first_core, proj_in.T, proj_out)
-    part, channels = mine.shape
+    part, channels = proj_out.shape
     vmem = pl.BlockSpec(memory_space=pltpu.VMEM)
-    gathered = jax.ShapeDtypeStruct((n, part, channels), mine.dtype)
+    gathered = jax.ShapeDtypeStruct((n, part, channels), proj_out.dtype)
     micro, cells, _ = images.shape
     fresh = jax.ShapeDtypeStruct((micro, cells * 5 // 2, channels), images.dtype)
     held, other, fresh = pl.pallas_call(
@@ -522,7 +531,7 @@
             _gather_kernel, n, (pl.ds(0, 96), pl.ds(96, part - 96)), lax.axis_size("row")
         ),
         out_shape=[gathered, gathered, fresh],
-        in_specs=[vmem, vmem],
+        in_specs=[vmem, vmem, vmem],
         out_specs=[vmem, vmem, vmem],
         scratch_shapes=[
             pltpu.SemaphoreType.DMA((4 * n,)),
@@ -532,9 +541,10 @@
             pltpu.SemaphoreType.DMA((2,)),
             pltpu.SemaphoreType.DMA((2,)),
             pltpu.SemaphoreType.DMA(()),
+            pltpu.VMEM((part, channels), proj_out.dtype),
         ],
         compiler_params=pltpu.CompilerParams(collective_id=7, has_side_effects=True),
-    )(mine, images)
+    )(proj_in, proj_out, images)
     return held.reshape(n * part, channels), other.reshape(n * part, channels), fresh
 
 

time: 169 us -> 169 us (level)
  local copies, waits for them, and re-layouts: 1.88 us -> 3.58 us
    unnamed x20 -> x21, local copies, waits for them, and re-layouts: 0.97 us -> 2.68 us
where the time goes in v10:
time: 169 us; the launch traced here: 168 us
  Pallas kernels  164 us (97%)
  local copies, waits for them, and re-layouts  3.58 us (2%)
    pallas_call x7, Pallas kernels, pointwise(): pl.pallas_call(functools.partial(_pointwise_kernel, n, sections, hand_on,...  138 us
    pallas_call x1, Pallas kernels, gathered_weights(): pl.pallas_call(functools.partial(_gather_kernel, n, (pl.ds(0, 96), pl.ds(...  26.5 us

profile of v10, /device:TPU:7, one launch (start us, length us, event | category | flops | bytes accessed | tf_op | source)
XLA Modules:
  0.0 168.3 jit_solution(3723835032352643841)
XLA Ops:
  0.0 1.7 %copy.12 = bf16[1,352,176]{2,1,0:T(8,128)(2,1)} copy(bf16[1,352,176]{1,2,0:T(8,128)(2,1)} %param.16) | data formatting | bytes 247808 | tf_op args[5]
  1.7 26.5 %shard_map.109 = (bf16[8,176,352]{2,1,0:T(8,128)(2,1)}, bf16[8,176,352]{2,1,0:T(8,128)(2,1)}, bf16[4,480,352]{2,1,0:T(8,128)(2,1)}) custom-call(bf16[352,176]{1,0:T(8,128)(2,1)} %bitcast.38, bf16[176,352]{1,0:T(8,128)(2,1)} %bitcast.47, bf16[4,192,352]{2,1,0:T(8,128)(2,1)} %bitcast.40), custom_call_target="tpu_custom_call" | custom-call | tf_op jit(solution)/shard_map/pallas_call | solution.py:529
  28.2 28.2 %shard_map.110 = (bf16[192,352]{1,0:T(8,128)(2,1)}, bf16[480,352]{1,0:T(8,128)(2,1)}) custom-call(bf16[1920,352]{1,0:T(8,128)(2,1)} %bitcast.16, bf16[4,480,352]{2,1,0:T(8,128)(2,1)} %get-tuple-element.20.fresh_ref, bf16[1408,352]{1,0:T(8,128)(2,1)} %bitcast.17, bf16[1408,352]{1,0:T(8,128)(2,1)} %bitcast.24, bf16[1,1408]{1,0:T(2,128)(2,1)} %bias_in_ref.13, ...), custom_call_target="tpu_custom_call" | custom-call | flops 380633088 | bytes 2523136 | tf_op jit(solution)/shard_map/pallas_call | solution.py:300
  56.4 21.2 %shard_map.111 = (bf16[192,352]{1,0:T(8,128)(2,1)}, bf16[480,352]{1,0:T(8,128)(2,1)}) custom-call(bf16[480,352]{1,0:T(8,128)(2,1)} %get-tuple-element.24.padded_ref, bf16[4,480,352]{2,1,0:T(8,128)(2,1)} %get-tuple-element.20.fresh_ref, bf16[1408,352]{1,0:T(8,128)(2,1)} %bitcast.18, bf16[1408,352]{1,0:T(8,128)(2,1)} %bitcast.25, ...), custom_call_target="tpu_custom_call" | custom-call | flops 380633088 | bytes 2523136 | tf_op jit(solution)/shard_map/pallas_call | solution.py:300
  77.5 20.4 %shard_map.112 = (bf16[192,352]{1,0:T(8,128)(2,1)}, bf16[480,352]{1,0:T(8,128)(2,1)}) custom-call(bf16[480,352]{1,0:T(8,128)(2,1)} %get-tuple-element.26.padded_ref, bf16[4,480,352]{2,1,0:T(8,128)(2,1)} %get-tuple-element.20.fresh_ref, bf16[1408,352]{1,0:T(8,128)(2,1)} %bitcast.19, bf16[1408,352]{1,0:T(8,128)(2,1)} %bitcast.26, ...), custom_call_target="tpu_custom_call" | custom-call | flops 380633088 | bytes 2523136 | tf_op jit(solution)/shard_map/pallas_call | solution.py:300
  97.9 19.0 %shard_map.113 = (bf16[192,352]{1,0:T(8,128)(2,1)}, bf16[480,352]{1,0:T(8,128)(2,1)}) custom-call(bf16[480,352]{1,0:T(8,128)(2,1)} %get-tuple-element.28.padded_ref, bf16[4,480,352]{2,1,0:T(8,128)(2,1)} %get-tuple-element.20.fresh_ref, bf16[1408,352]{1,0:T(8,128)(2,1)} %bitcast.20, bf16[1408,352]{1,0:T(8,128)(2,1)} %bitcast.27, ...), custom_call_target="tpu_custom_call" | custom-call | flops 380633088 | bytes 2523136 | tf_op jit(solution)/shard_map/pallas_call | solution.py:300
  116.9 18.7 %shard_map.114 = (bf16[192,352]{1,0:T(8,128)(2,1)}, bf16[480,352]{1,0:T(8,128)(2,1)}) custom-call(bf16[480,352]{1,0:T(8,128)(2,1)} %get-tuple-element.30.padded_ref, bf16[4,480,352]{2,1,0:T(8,128)(2,1)} %get-tuple-element.20.fresh_ref, bf16[1408,352]{1,0:T(8,128)(2,1)} %bitcast.21, bf16[1408,352]{1,0:T(8,128)(2,1)} %bitcast.28, ...), custom_call_target="tpu_custom_call" | custom-call | flops 380633088 | bytes 2523136 | tf_op jit(solution)/shard_map/pallas_call | solution.py:300
  135.7 18.5 %shard_map.115 = (bf16[192,352]{1,0:T(8,128)(2,1)}, bf16[480,352]{1,0:T(8,128)(2,1)}) custom-call(bf16[480,352]{1,0:T(8,128)(2,1)} %get-tuple-element.32.padded_ref, bf16[4,480,352]{2,1,0:T(8,128)(2,1)} %get-tuple-element.20.fresh_ref, bf16[1408,352]{1,0:T(8,128)(2,1)} %bitcast.22, bf16[1408,352]{1,0:T(8,128)(2,1)} %bitcast.29, ...), custom_call_target="tpu_custom_call" | custom-call | flops 380633088 | bytes 2523136 | tf_op jit(solution)/shard_map/pallas_call | solution.py:300
  154.2 0.0 copy-start.1
  154.2 0.0 copy-start.2
  154.2 0.0 copy-start.3
  154.2 0.0 copy-start.4
  154.2 12.1 %shard_map.116 = bf16[192,352]{1,0:T(8,128)(2,1)} custom-call(bf16[480,352]{1,0:T(8,128)(2,1)} %get-tuple-element.34.padded_ref, bf16[4,480,352]{2,1,0:T(8,128)(2,1)} %get-tuple-element.20.fresh_ref, bf16[1408,352]{1,0:T(8,128)(2,1)} %bitcast.23, bf16[1408,352]{1,0:T(8,128)(2,1)} %bitcast.30, bf16[1,1408]{1,0:T(2,128)(2,1)} %bias_in_ref.13, ...), custom_call_target="tpu_custom_call" | custom-call | flops 380633088 | bytes 2523136 | tf_op jit(solution)/shard_map/pallas_call | solution.py:300
  166.3 0.0 copy-start.5
  166.3 0.0 copy-start.6
  166.3 0.0 copy-start
  166.3 0.0 copy-done.1
  166.4 0.0 copy-done.2
  166.4 0.0 copy-done.3
  166.5 0.0 copy-done.4
  166.5 0.7 copy-done.5
  167.2 0.0 copy-done.6
  167.3 0.0 copy-done
  167.4 0.9 dynamic-slice_bitcast_fusion
  (7 shorter events, 0.2 us)
Async XLA Ops:
  154.2 12.1 %copy-start.1 = (bf16[192,352]{1,0:T(8,128)(2,1)S(1)}, bf16[192,352]{1,0:T(8,128)(2,1)}, u32[]{:S(2)}) copy-start(bf16[192,352]{1,0:T(8,128)(2,1)} %get-tuple-element.23) | copy-start | bytes 405508
  154.2 12.2 %copy-start.2 = (bf16[192,352]{1,0:T(8,128)(2,1)S(1)}, bf16[192,352]{1,0:T(8,128)(2,1)}, u32[]{:S(2)}) copy-start(bf16[192,352]{1,0:T(8,128)(2,1)} %get-tuple-element.25) | copy-start | bytes 405508
  154.2 12.2 %copy-start.3 = (bf16[192,352]{1,0:T(8,128)(2,1)S(1)}, bf16[192,352]{1,0:T(8,128)(2,1)}, u32[]{:S(2)}) copy-start(bf16[192,352]{1,0:T(8,128)(2,1)} %get-tuple-element.27) | copy-start | bytes 405508
  154.2 12.2 %copy-start.4 = (bf16[192,352]{1,0:T(8,128)(2,1)S(1)}, bf16[192,352]{1,0:T(8,128)(2,1)}, u32[]{:S(2)}) copy-start(bf16[192,352]{1,0:T(8,128)(2,1)} %get-tuple-element.29) | copy-start | bytes 405508
  166.3 0.9 copy-start.5
  166.3 1.0 copy-start.6
  166.3 1.0 copy-start

commit v11 on v10

--- a/solution.py
+++ b/solution.py
@@ -528,16 +528,16 @@
     fresh = jax.ShapeDtypeStruct((micro, cells * 5 // 2, channels), images.dtype)
     held, other, fresh = pl.pallas_call(
         functools.partial(
-            _gather_kernel, n, (pl.ds(0, 96), pl.ds(96, part - 96)), lax.axis_size("row")
+            _gather_kernel, n, (pl.ds(0, 64), pl.ds(64, 64), pl.ds(128, part - 128)), lax.axis_size("row")
         ),
         out_shape=[gathered, gathered, fresh],
         in_specs=[vmem, vmem, vmem],
         out_specs=[vmem, vmem, vmem],
         scratch_shapes=[
-            pltpu.SemaphoreType.DMA((4 * n,)),
-            pltpu.SemaphoreType.DMA((2 * n,)),
-            pltpu.SemaphoreType.DMA((4 * n,)),
-            pltpu.SemaphoreType.DMA((2 * n,)),
+            pltpu.SemaphoreType.DMA((6 * n,)),
+            pltpu.SemaphoreType.DMA((3 * n,)),
+            pltpu.SemaphoreType.DMA((6 * n,)),
+            pltpu.SemaphoreType.DMA((3 * n,)),
             pltpu.SemaphoreType.DMA((2,)),
             pltpu.SemaphoreType.DMA((2,)),
             pltpu.SemaphoreType.DMA(()),

time: 169 us -> 168 us (level)
  no operation moved by 1% of the time
where the time goes in v11:
time: 168 us; the launch traced here: 167 us
  Pallas kernels  164 us (98%)
  local copies, waits for them, and re-layouts  3.58 us (2%)
    pallas_call x7, Pallas kernels, pointwise(): pl.pallas_call(functools.partial(_pointwise_kernel, n, sections, hand_on,...  138 us
    pallas_call x1, Pallas kernels, gathered_weights(): pl.pallas_call(functools.partial(_gather_kernel, n, (pl.ds(0, 64), pl.ds(...  26.1 us

profile of v11, /device:TPU:7, one launch (start us, length us, event | category | flops | bytes accessed | tf_op | source)
XLA Modules:
  0.0 167.5 jit_solution(8199746801224913046)
XLA Ops:
  0.0 1.7 %copy.12 = bf16[1,352,176]{2,1,0:T(8,128)(2,1)} copy(bf16[1,352,176]{1,2,0:T(8,128)(2,1)} %param.16) | data formatting | bytes 247808 | tf_op args[5]
  1.7 26.1 %shard_map.109 = (bf16[8,176,352]{2,1,0:T(8,128)(2,1)}, bf16[8,176,352]{2,1,0:T(8,128)(2,1)}, bf16[4,480,352]{2,1,0:T(8,128)(2,1)}) custom-call(bf16[352,176]{1,0:T(8,128)(2,1)} %bitcast.38, bf16[176,352]{1,0:T(8,128)(2,1)} %bitcast.47, bf16[4,192,352]{2,1,0:T(8,128)(2,1)} %bitcast.40), custom_call_target="tpu_custom_call" | custom-call | tf_op jit(solution)/shard_map/pallas_call | solution.py:529
  27.8 27.9 %shard_map.110 = (bf16[192,352]{1,0:T(8,128)(2,1)}, bf16[480,352]{1,0:T(8,128)(2,1)}) custom-call(bf16[1920,352]{1,0:T(8,128)(2,1)} %bitcast.16, bf16[4,480,352]{2,1,0:T(8,128)(2,1)} %get-tuple-element.20.fresh_ref, bf16[1408,352]{1,0:T(8,128)(2,1)} %bitcast.17, bf16[1408,352]{1,0:T(8,128)(2,1)} %bitcast.24, bf16[1,1408]{1,0:T(2,128)(2,1)} %bias_in_ref.13, ...), custom_call_target="tpu_custom_call" | custom-call | flops 380633088 | bytes 2523136 | tf_op jit(solution)/shard_map/pallas_call | solution.py:300
  55.7 20.9 %shard_map.111 = (bf16[192,352]{1,0:T(8,128)(2,1)}, bf16[480,352]{1,0:T(8,128)(2,1)}) custom-call(bf16[480,352]{1,0:T(8,128)(2,1)} %get-tuple-element.24.padded_ref, bf16[4,480,352]{2,1,0:T(8,128)(2,1)} %get-tuple-element.20.fresh_ref, bf16[1408,352]{1,0:T(8,128)(2,1)} %bitcast.18, bf16[1408,352]{1,0:T(8,128)(2,1)} %bitcast.25, ...), custom_call_target="tpu_custom_call" | custom-call | flops 380633088 | bytes 2523136 | tf_op jit(solution)/shard_map/pallas_call | solution.py:300
  76.6 21.2 %shard_map.112 = (bf16[192,352]{1,0:T(8,128)(2,1)}, bf16[480,352]{1,0:T(8,128)(2,1)}) custom-call(bf16[480,352]{1,0:T(8,128)(2,1)} %get-tuple-element.26.padded_ref, bf16[4,480,352]{2,1,0:T(8,128)(2,1)} %get-tuple-element.20.fresh_ref, bf16[1408,352]{1,0:T(8,128)(2,1)} %bitcast.19, bf16[1408,352]{1,0:T(8,128)(2,1)} %bitcast.26, ...), custom_call_target="tpu_custom_call" | custom-call | flops 380633088 | bytes 2523136 | tf_op jit(solution)/shard_map/pallas_call | solution.py:300
  97.8 18.3 %shard_map.113 = (bf16[192,352]{1,0:T(8,128)(2,1)}, bf16[480,352]{1,0:T(8,128)(2,1)}) custom-call(bf16[480,352]{1,0:T(8,128)(2,1)} %get-tuple-element.28.padded_ref, bf16[4,480,352]{2,1,0:T(8,128)(2,1)} %get-tuple-element.20.fresh_ref, bf16[1408,352]{1,0:T(8,128)(2,1)} %bitcast.20, bf16[1408,352]{1,0:T(8,128)(2,1)} %bitcast.27, ...), custom_call_target="tpu_custom_call" | custom-call | flops 380633088 | bytes 2523136 | tf_op jit(solution)/shard_map/pallas_call | solution.py:300
  116.1 18.8 %shard_map.114 = (bf16[192,352]{1,0:T(8,128)(2,1)}, bf16[480,352]{1,0:T(8,128)(2,1)}) custom-call(bf16[480,352]{1,0:T(8,128)(2,1)} %get-tuple-element.30.padded_ref, bf16[4,480,352]{2,1,0:T(8,128)(2,1)} %get-tuple-element.20.fresh_ref, bf16[1408,352]{1,0:T(8,128)(2,1)} %bitcast.21, bf16[1408,352]{1,0:T(8,128)(2,1)} %bitcast.28, ...), custom_call_target="tpu_custom_call" | custom-call | flops 380633088 | bytes 2523136 | tf_op jit(solution)/shard_map/pallas_call | solution.py:300
  134.9 18.6 %shard_map.115 = (bf16[192,352]{1,0:T(8,128)(2,1)}, bf16[480,352]{1,0:T(8,128)(2,1)}) custom-call(bf16[480,352]{1,0:T(8,128)(2,1)} %get-tuple-element.32.padded_ref, bf16[4,480,352]{2,1,0:T(8,128)(2,1)} %get-tuple-element.20.fresh_ref, bf16[1408,352]{1,0:T(8,128)(2,1)} %bitcast.22, bf16[1408,352]{1,0:T(8,128)(2,1)} %bitcast.29, ...), custom_call_target="tpu_custom_call" | custom-call | flops 380633088 | bytes 2523136 | tf_op jit(solution)/shard_map/pallas_call | solution.py:300
  153.5 0.0 copy-start.1
  153.5 0.0 copy-start.2
  153.5 0.0 copy-start.3
  153.5 0.0 copy-start.4
  153.5 12.0 %shard_map.116 = bf16[192,352]{1,0:T(8,128)(2,1)} custom-call(bf16[480,352]{1,0:T(8,128)(2,1)} %get-tuple-element.34.padded_ref, bf16[4,480,352]{2,1,0:T(8,128)(2,1)} %get-tuple-element.20.fresh_ref, bf16[1408,352]{1,0:T(8,128)(2,1)} %bitcast.23, bf16[1408,352]{1,0:T(8,128)(2,1)} %bitcast.30, bf16[1,1408]{1,0:T(2,128)(2,1)} %bias_in_ref.13, ...), custom_call_target="tpu_custom_call" | custom-call | flops 380633088 | bytes 2523136 | tf_op jit(solution)/shard_map/pallas_call | solution.py:300
  165.5 0.0 copy-start.5
  165.5 0.0 copy-start.6
  165.5 0.0 copy-start
  165.6 0.0 copy-done.1
  165.6 0.0 copy-done.2
  165.6 0.0 copy-done.3
  165.7 0.0 copy-done.4
  165.7 0.7 copy-done.5
  166.5 0.0 copy-done.6
  166.5 0.0 copy-done
  166.6 0.9 dynamic-slice_bitcast_fusion
  (7 shorter events, 0.2 us)
Async XLA Ops:
  153.5 12.1 %copy-start.1 = (bf16[192,352]{1,0:T(8,128)(2,1)S(1)}, bf16[192,352]{1,0:T(8,128)(2,1)}, u32[]{:S(2)}) copy-start(bf16[192,352]{1,0:T(8,128)(2,1)} %get-tuple-element.23) | copy-start | bytes 405508
  153.5 12.1 %copy-start.2 = (bf16[192,352]{1,0:T(8,128)(2,1)S(1)}, bf16[192,352]{1,0:T(8,128)(2,1)}, u32[]{:S(2)}) copy-start(bf16[192,352]{1,0:T(8,128)(2,1)} %get-tuple-element.25) | copy-start | bytes 405508
  153.5 12.2 %copy-start.3 = (bf16[192,352]{1,0:T(8,128)(2,1)S(1)}, bf16[192,352]{1,0:T(8,128)(2,1)}, u32[]{:S(2)}) copy-start(bf16[192,352]{1,0:T(8,128)(2,1)} %get-tuple-element.27) | copy-start | bytes 405508
  153.5 12.2 %copy-start.4 = (bf16[192,352]{1,0:T(8,128)(2,1)S(1)}, bf16[192,352]{1,0:T(8,128)(2,1)}, u32[]{:S(2)}) copy-start(bf16[192,352]{1,0:T(8,128)(2,1)} %get-tuple-element.29) | copy-start | bytes 405508
  165.5 0.9 copy-start.5
  165.5 1.0 copy-start.6
  165.5 1.0 copy-start

commit v12 on v10

--- a/solution.py
+++ b/solution.py
@@ -528,16 +528,16 @@
     fresh = jax.ShapeDtypeStruct((micro, cells * 5 // 2, channels), images.dtype)
     held, other, fresh = pl.pallas_call(
         functools.partial(
-            _gather_kernel, n, (pl.ds(0, 96), pl.ds(96, part - 96)), lax.axis_size("row")
+            _gather_kernel, n, (pl.ds(0, 48), pl.ds(48, 48), pl.ds(96, 48), pl.ds(144, part - 144)), lax.axis_size("row")
         ),
         out_shape=[gathered, gathered, fresh],
         in_specs=[vmem, vmem, vmem],
         out_specs=[vmem, vmem, vmem],
         scratch_shapes=[
+            pltpu.SemaphoreType.DMA((8 * n,)),
             pltpu.SemaphoreType.DMA((4 * n,)),
-            pltpu.SemaphoreType.DMA((2 * n,)),
+            pltpu.SemaphoreType.DMA((8 * n,)),
             pltpu.SemaphoreType.DMA((4 * n,)),
-            pltpu.SemaphoreType.DMA((2 * n,)),
             pltpu.SemaphoreType.DMA((2,)),
             pltpu.SemaphoreType.DMA((2,)),
             pltpu.SemaphoreType.DMA(()),

time: 169 us -> 169 us (level)
  no operation moved by 1% of the time
where the time goes in v12:
time: 169 us; the launch traced here: 168 us
  Pallas kernels  164 us (97%)
  local copies, waits for them, and re-layouts  3.58 us (2%)
    pallas_call x7, Pallas kernels, pointwise(): pl.pallas_call(functools.partial(_pointwise_kernel, n, sections, hand_on,...  138 us
    pallas_call x1, Pallas kernels, gathered_weights(): pl.pallas_call(functools.partial(_gather_kernel, n, (pl.ds(0, 48), pl.ds(...  26.3 us

profile of v12, /device:TPU:7, one launch (start us, length us, event | category | flops | bytes accessed | tf_op | source)
XLA Modules:
  0.0 168.0 jit_solution(16725115096185631556)
XLA Ops:
  0.0 1.7 %copy.12 = bf16[1,352,176]{2,1,0:T(8,128)(2,1)} copy(bf16[1,352,176]{1,2,0:T(8,128)(2,1)} %param.16) | data formatting | bytes 247808 | tf_op args[5]
  1.7 26.3 %shard_map.109 = (bf16[8,176,352]{2,1,0:T(8,128)(2,1)}, bf16[8,176,352]{2,1,0:T(8,128)(2,1)}, bf16[4,480,352]{2,1,0:T(8,128)(2,1)}) custom-call(bf16[352,176]{1,0:T(8,128)(2,1)} %bitcast.38, bf16[176,352]{1,0:T(8,128)(2,1)} %bitcast.47, bf16[4,192,352]{2,1,0:T(8,128)(2,1)} %bitcast.40), custom_call_target="tpu_custom_call" | custom-call | tf_op jit(solution)/shard_map/pallas_call | solution.py:529
  28.0 28.1 %shard_map.110 = (bf16[192,352]{1,0:T(8,128)(2,1)}, bf16[480,352]{1,0:T(8,128)(2,1)}) custom-call(bf16[1920,352]{1,0:T(8,128)(2,1)} %bitcast.16, bf16[4,480,352]{2,1,0:T(8,128)(2,1)} %get-tuple-element.20.fresh_ref, bf16[1408,352]{1,0:T(8,128)(2,1)} %bitcast.17, bf16[1408,352]{1,0:T(8,128)(2,1)} %bitcast.24, bf16[1,1408]{1,0:T(2,128)(2,1)} %bias_in_ref.13, ...), custom_call_target="tpu_custom_call" | custom-call | flops 380633088 | bytes 2523136 | tf_op jit(solution)/shard_map/pallas_call | solution.py:300
  56.1 20.9 %shard_map.111 = (bf16[192,352]{1,0:T(8,128)(2,1)}, bf16[480,352]{1,0:T(8,128)(2,1)}) custom-call(bf16[480,352]{1,0:T(8,128)(2,1)} %get-tuple-element.24.padded_ref, bf16[4,480,352]{2,1,0:T(8,128)(2,1)} %get-tuple-element.20.fresh_ref, bf16[1408,352]{1,0:T(8,128)(2,1)} %bitcast.18, bf16[1408,352]{1,0:T(8,128)(2,1)} %bitcast.25, ...), custom_call_target="tpu_custom_call" | custom-call | flops 380633088 | bytes 2523136 | tf_op jit(solution)/shard_map/pallas_call | solution.py:300
  77.0 21.0 %shard_map.112 = (bf16[192,352]{1,0:T(8,128)(2,1)}, bf16[480,352]{1,0:T(8,128)(2,1)}) custom-call(bf16[480,352]{1,0:T(8,128)(2,1)} %get-tuple-element.26.padded_ref, bf16[4,480,352]{2,1,0:T(8,128)(2,1)} %get-tuple-element.20.fresh_ref, bf16[1408,352]{1,0:T(8,128)(2,1)} %bitcast.19, bf16[1408,352]{1,0:T(8,128)(2,1)} %bitcast.26, ...), custom_call_target="tpu_custom_call" | custom-call | flops 380633088 | bytes 2523136 | tf_op jit(solution)/shard_map/pallas_call | solution.py:300
  98.0 18.3 %shard_map.113 = (bf16[192,352]{1,0:T(8,128)(2,1)}, bf16[480,352]{1,0:T(8,128)(2,1)}) custom-call(bf16[480,352]{1,0:T(8,128)(2,1)} %get-tuple-element.28.padded_ref, bf16[4,480,352]{2,1,0:T(8,128)(2,1)} %get-tuple-element.20.fresh_ref, bf16[1408,352]{1,0:T(8,128)(2,1)} %bitcast.20, bf16[1408,352]{1,0:T(8,128)(2,1)} %bitcast.27, ...), custom_call_target="tpu_custom_call" | custom-call | flops 380633088 | bytes 2523136 | tf_op jit(solution)/shard_map/pallas_call | solution.py:300
  116.3 18.9 %shard_map.114 = (bf16[192,352]{1,0:T(8,128)(2,1)}, bf16[480,352]{1,0:T(8,128)(2,1)}) custom-call(bf16[480,352]{1,0:T(8,128)(2,1)} %get-tuple-element.30.padded_ref, bf16[4,480,352]{2,1,0:T(8,128)(2,1)} %get-tuple-element.20.fresh_ref, bf16[1408,352]{1,0:T(8,128)(2,1)} %bitcast.21, bf16[1408,352]{1,0:T(8,128)(2,1)} %bitcast.28, ...), custom_call_target="tpu_custom_call" | custom-call | flops 380633088 | bytes 2523136 | tf_op jit(solution)/shard_map/pallas_call | solution.py:300
  135.2 18.2 %shard_map.115 = (bf16[192,352]{1,0:T(8,128)(2,1)}, bf16[480,352]{1,0:T(8,128)(2,1)}) custom-call(bf16[480,352]{1,0:T(8,128)(2,1)} %get-tuple-element.32.padded_ref, bf16[4,480,352]{2,1,0:T(8,128)(2,1)} %get-tuple-element.20.fresh_ref, bf16[1408,352]{1,0:T(8,128)(2,1)} %bitcast.22, bf16[1408,352]{1,0:T(8,128)(2,1)} %bitcast.29, ...), custom_call_target="tpu_custom_call" | custom-call | flops 380633088 | bytes 2523136 | tf_op jit(solution)/shard_map/pallas_call | solution.py:300
  153.4 0.0 copy-start.1
  153.5 0.0 copy-start.2
  153.5 0.0 copy-start.3
  153.5 0.0 copy-start.4
  153.5 12.5 %shard_map.116 = bf16[192,352]{1,0:T(8,128)(2,1)} custom-call(bf16[480,352]{1,0:T(8,128)(2,1)} %get-tuple-element.34.padded_ref, bf16[4,480,352]{2,1,0:T(8,128)(2,1)} %get-tuple-element.20.fresh_ref, bf16[1408,352]{1,0:T(8,128)(2,1)} %bitcast.23, bf16[1408,352]{1,0:T(8,128)(2,1)} %bitcast.30, bf16[1,1408]{1,0:T(2,128)(2,1)} %bias_in_ref.13, ...), custom_call_target="tpu_custom_call" | custom-call | flops 380633088 | bytes 2523136 | tf_op jit(solution)/shard_map/pallas_call | solution.py:300
  166.0 0.0 copy-start.5
  166.0 0.0 copy-start.6
  166.1 0.0 copy-start
  166.1 0.0 copy-done.1
  166.1 0.0 copy-done.2
  166.1 0.0 copy-done.3
  166.2 0.0 copy-done.4
  166.2 0.7 copy-done.5
  167.0 0.0 copy-done.6
  167.0 0.0 copy-done
  167.1 0.9 dynamic-slice_bitcast_fusion
  (7 shorter events, 0.2 us)
Async XLA Ops:
  153.4 12.6 %copy-start.1 = (bf16[192,352]{1,0:T(8,128)(2,1)S(1)}, bf16[192,352]{1,0:T(8,128)(2,1)}, u32[]{:S(2)}) copy-start(bf16[192,352]{1,0:T(8,128)(2,1)} %get-tuple-element.23) | copy-start | bytes 405508
  153.5 12.7 %copy-start.2 = (bf16[192,352]{1,0:T(8,128)(2,1)S(1)}, bf16[192,352]{1,0:T(8,128)(2,1)}, u32[]{:S(2)}) copy-start(bf16[192,352]{1,0:T(8,128)(2,1)} %get-tuple-element.25) | copy-start | bytes 405508
  153.5 12.7 %copy-start.3 = (bf16[192,352]{1,0:T(8,128)(2,1)S(1)}, bf16[192,352]{1,0:T(8,128)(2,1)}, u32[]{:S(2)}) copy-start(bf16[192,352]{1,0:T(8,128)(2,1)} %get-tuple-element.27) | copy-start | bytes 405508
  153.5 12.7 %copy-start.4 = (bf16[192,352]{1,0:T(8,128)(2,1)S(1)}, bf16[192,352]{1,0:T(8,128)(2,1)}, u32[]{:S(2)}) copy-start(bf16[192,352]{1,0:T(8,128)(2,1)} %get-tuple-element.29) | copy-start | bytes 405508
  166.0 0.9 copy-start.5
  166.0 1.0 copy-start.6
  166.1 1.0 copy-start
